TPU v7x, 32 devices: a whole 2x2x4 slice. The times are simulated.
32 devices in a mesh: fsdp: 16 (over z, x, core), dp: 2 (over y).
Axes of the slice: x: 2, y: 2, z: 4, core: 2. Of those that a mesh axis runs over, the one named last changes fastest.
Arguments:
- inputs: bfloat16 [6144, 4096], P(('fsdp', 'dp')), may hold values from -6 to 6
- grad_out: bfloat16 [6144, 14336], P(('fsdp', 'dp')), may hold values from -0.009765625 to 0.009765625
- projection: bfloat16 [4096, 128], P('fsdp'), may hold values from -0.375 to 0.375
- moment: float32 [14336, 128], P('fsdp'), may hold values from -1.5 to 1.5
- second: float32 [14336, 128], P('fsdp'), may hold values from 0.0001 to 0.001
Outputs:
- update: bfloat16 [4096, 14336], P('fsdp')
- new_moment: float32 [14336, 128], P('fsdp')
- new_second: float32 [14336, 128], P('fsdp')
All inputs are finite; a program needn't handle non-finite values.
Results may differ from a plain program's by a relative error of at most 0.0051.
Values may be sent and summed in bfloat16 or wider, within the bound.
No kernel may reach another device: no remote copies, remote signals or barrier semaphores. Data moves between devices by JAX's collectives and lax.ppermute only.
A program may use at most 64 MiB of HBM per device.

v0:
```python
import jax
import jax.numpy as jnp
from jax import lax
from jax.sharding import PartitionSpec as P

STEP = 10


def adam_step(low_rank, moment, second):
    new_moment = 0.9 * moment + 0.1 * low_rank
    new_second = 0.999 * second + 0.001 * (low_rank * low_rank)
    first_fix = 1.0 - 0.9**STEP
    second_fix = 1.0 - 0.999**STEP
    normalized = (new_moment / first_fix / (jnp.sqrt(new_second / second_fix) + 1e-08)).astype(
        jnp.bfloat16
    )
    return (new_moment, new_second, normalized)


def local(inputs, grad_out, projection, moment, second):
    projected = jnp.dot(
        inputs,
        lax.all_gather(projection, "fsdp", axis=0, tiled=True),
        preferred_element_type=jnp.float32,
    ).astype(jnp.bfloat16)
    contract = (((0,), (0,)), ((), ()))
    whole = lax.dot_general(grad_out, projected, contract, preferred_element_type=jnp.float32)
    whole = lax.psum(whole, "dp")
    low_rank = lax.psum_scatter(whole, "fsdp", scatter_dimension=0, tiled=True)
    new_moment, new_second, normalized = adam_step(low_rank, moment, second)
    expand = (((1,), (1,)), ((), ()))
    update = lax.dot_general(
        projection,
        lax.all_gather(normalized, "fsdp", axis=0, tiled=True),
        expand,
        preferred_element_type=jnp.float32,
    ).astype(jnp.bfloat16)
    return (update, new_moment, new_second)


def solution(mesh):
    in_specs = (
        P(("fsdp", "dp"), None),
        P(("fsdp", "dp"), None),
        P("fsdp", None),
        P("fsdp", None),
        P("fsdp", None),
    )
    out_specs = (P("fsdp", None), P("fsdp", None), P("fsdp", None))
    return jax.shard_map(local, mesh=mesh, in_specs=in_specs, out_specs=out_specs, check_vma=False)
```

profile of v0, /device:TPU:0, one launch (start us, length us, event | category | flops | bytes accessed | tf_op | source)
XLA Modules:
  0.0 252.6 jit_solution(8466995799311963233)
XLA Ops:
  7.2 0.0 copy-start
  7.2 0.0 all-gather.3.cloned.1.call-start
  7.2 0.7 all-gather.3.cloned.1.call-update
  7.9 0.0 reduce-scatter.2.cloned.1.call-start
  8.0 42.8 %all-gather.3.cloned.1.call-done = bf16[4096,128]{1,0:T(8,128)(2,1)} async-done(((bf16[256,128]{1,0:T(8,128)(2,1)}), bf16[4096,128]{1,0:T(8,128)(2,1)}) %all-gather.3.cloned.1.call-update) | async-done | bytes 1048592 | tf_op jit(solution)/shard_map/all_gather | solution.py:23
  50.7 0.0 copy-done
  50.7 7.6 %convolution_bitcast_fusion = f32[14336,128]{0,1:T(8,128)} fusion(bf16[192,14336]{1,0:T(8,128)(2,1)} %param.6, bf16[192,4096]{1,0:T(8,128)(2,1)S(1)} %copy-done, bf16[4096,128]{1,0:T(8,128)(2,1)} %all-gather.3.cloned.1.call-done), kind=kOutput, calls=%fused_computation.2 | convolution fusion | flops 905994240 | bytes 15466496 | tf_op jit(solution)/shard_map/dot_general | solution.py:27
  58.4 0.0 copy-start.1
  58.4 0.0 copy-start.2
  58.4 0.0 copy-start.3
  58.4 0.0 reduce-scatter.2.cloned.1.call-update
  58.4 0.0 all-reduce.2.cloned.1.call-start
  58.5 90.7 %reduce-scatter.2.cloned.1.call-done = f32[896,128]{0,1:T(8,128)} async-done(((f32[14336,128]{0,1:T(8,128)}), f32[896,128]{0,1:T(8,128)}) %reduce-scatter.2.cloned.1.call-update) | async-done | bytes 458768 | tf_op jit(solution)/shard_map/reduce_scatter | solution.py:29
  149.2 0.0 all-reduce.2.cloned.1.call-update
  149.2 0.0 all-gather.5.cloned.1.call-start
  149.3 0.0 copy-done.1
  149.3 0.2 copy.8
  149.5 0.0 copy-done.2
  149.5 0.2 copy.9
  149.7 28.8 %all-reduce.2.cloned.1.call-done = f32[896,128]{0,1:T(8,128)} async-done(((f32[896,128]{0,1:T(8,128)}), f32[896,128]{0,1:T(8,128)}) %all-reduce.2.cloned.1.call-update) | async-done | bytes 458768 | tf_op jit(solution)/shard_map/psum | solution.py:28
  178.5 2.0 divide_convert_fusion
  180.5 0.0 all-gather.5.cloned.1.call-update
  180.5 1.0 copy.11
  181.5 1.0 copy.12
  182.4 46.4 %all-gather.5.cloned.1.call-done = bf16[14336,128]{0,1:T(8,128)(2,1)} async-done(((bf16[896,128]{0,1:T(8,128)(2,1)}), bf16[14336,128]{0,1:T(8,128)(2,1)}) %all-gather.5.cloned.1.call-update) | async-done | bytes 3670032 | tf_op jit(solution)/shard_map/all_gather | solution.py:34
  228.9 0.0 copy-done.3
  228.9 7.1 %fusion = bf16[256,14336]{0,1:T(8,128)(2,1)} fusion(bf16[14336,128]{0,1:T(8,128)(2,1)} %all-gather.5.cloned.1.call-done, bf16[256,128]{1,0:T(8,128)(2,1)S(1)} %copy-done.3), kind=kOutput, calls=%fused_computation.1 | convolution fusion | flops 943194112 | bytes 11075584 | tf_op jit(solution)/shard_map/dot_general | solution.py:32
  236.0 10.1 %copy.10 = bf16[256,14336]{1,0:T(8,128)(2,1)} copy(bf16[256,14336]{0,1:T(8,128)(2,1)} %fusion) | data formatting | bytes 14680064
Async XLA Ops:
  7.2 43.6 %copy-start = (bf16[192,4096]{1,0:T(8,128)(2,1)S(1)}, bf16[192,4096]{1,0:T(8,128)(2,1)}, u32[]{:S(2)}) copy-start(bf16[192,4096]{1,0:T(8,128)(2,1)} %param.5) | copy-start | bytes 4718596
  7.2 43.6 %all-gather.3.cloned.1.call-start = ((), (), s32[]{:S(2)}) async-start(), calls=%async_computation.1 | async-start | bytes 1114112 | tf_op jit(solution)/shard_map/all_gather | solution.py:23
  7.9 141.3 %reduce-scatter.2.cloned.1.call-start = ((), (), s32[]{:S(2)}) async-start(), calls=%async_computation.3 | async-start | bytes 7798784 | tf_op jit(solution)/shard_map/reduce_scatter | solution.py:29
  58.4 90.9 %copy-start.1 = (f32[896,128]{1,0:T(8,128)S(1)}, f32[896,128]{1,0:T(8,128)}, u32[]{:S(2)}) copy-start(f32[896,128]{1,0:T(8,128)} %param.8) | copy-start | bytes 1376260
  58.4 91.1 %copy-start.2 = (f32[896,128]{1,0:T(8,128)S(1)}, f32[896,128]{1,0:T(8,128)}, u32[]{:S(2)}) copy-start(f32[896,128]{1,0:T(8,128)} %param.9) | copy-start | bytes 1376260
  58.4 170.5 %copy-start.3 = (bf16[256,128]{1,0:T(8,128)(2,1)S(1)}, bf16[256,128]{1,0:T(8,128)(2,1)}, u32[]{:S(2)}) copy-start(bf16[256,128]{1,0:T(8,128)(2,1)} %param.7) | copy-start | bytes 196612
  58.4 120.1 %all-reduce.2.cloned.1.call-start = ((), (), s32[]{:S(2)}) async-start(), calls=%async_computation.4 | async-start | bytes 917504 | tf_op jit(solution)/shard_map/psum | solution.py:28
  149.2 79.6 %all-gather.5.cloned.1.call-start = ((), (), s32[]{:S(2)}) async-start(), calls=%async_computation.2 | async-start | bytes 3899392 | tf_op jit(solution)/shard_map/all_gather | solution.py:34
Sparse Core Ops, SparseCore 0:
  10.1 40.5 all-gather.2
  58.5 90.6 reduce-scatter.1
  151.5 26.9 all-reduce.1
  181.1 47.7 all-gather.4
where the time goes:
time: 253 us
  waiting for transfers between devices  209 us (83%)
  matrix products  14.7 us (6%)
  between operations  13.8 us (5%)
  local copies, waits for them, and re-layouts  12.5 us (5%)
    reduce_scatter x1, waiting for transfers between devices, local(): low_rank = lax.psum_scatter(whole, 'fsdp', scatter_dimension=0, tiled=True)  90.7 us
    all_gather x1, waiting for transfers between devices, local(): lax.all_gather(normalized, 'fsdp', axis=0, tiled=True)  46.4 us
    all_gather x1, waiting for transfers between devices, local(): lax.all_gather(projection, 'fsdp', axis=0, tiled=True)  42.8 us
    psum x1, waiting for transfers between devices, local(): whole = lax.psum(whole, 'dp')  28.8 us
    unnamed x13, local copies, waits for them, and re-layouts  12.5 us
    dot_general x1, matrix products, local(): lax.dot_general(grad_out, projected, contract, preferred_element_type=jnp...  7.64 us
    dot_general x1, matrix products, local(): lax.dot_general(projection, lax.all_gather(normalized, 'fsdp', axis=0, ti...  7.09 us
  transfers between devices with their start and end apart: 4, of which 4 were waited for; matrix products, arithmetic and copies ran while one was open for 1% of the time, Pallas kernels for 0%

commit v1 on v0

v1 whole, which is shorter than its diff:
```python
import functools

import jax
import jax.numpy as jnp
from jax import lax
from jax.experimental import pallas as pl
from jax.experimental.pallas import tpu as pltpu
from jax.sharding import PartitionSpec as P

STEP = 10
AXES = ("fsdp", "dp")


def bits_of(size):
    return size.bit_length() - 1


def orders(n, m):
    f = [("f", k) for k in range(1, bits_of(n))]
    d = [("d", k) for k in range(bits_of(m))]
    even = f[:1] + d[:1] + f[1:] + d[1:]
    odd = d[:1] + f[1:2] + f[:1] + f[2:] + d[1:]
    return even, odd


def gather_plan(n):
    plan = []
    for block in sorted(range(1, n // 2), key=lambda b: (b.bit_count(), -b)):
        low = block & -block
        via = low if block.bit_count() < 3 else (block ^ low) & -(block ^ low)
        plan.append((block, block ^ via, bits_of(via) + 1))
    return plan


def chunks_of(width):
    tiles = width // 128
    if width % 128 or tiles < 2:
        return ((0, width),)
    cut = tiles // 2 * 128
    return ((0, cut), (cut, width))


def pairs(n, m, both):
    out = []
    for i in range(n):
        for y in range(m):
            kind, k = both[i & 1]
            j, w = (i ^ (1 << k), y) if kind == "f" else (i, y ^ (1 << k))
            out.append((i * m + y, j * m + w))
    return out


def slot_of(order, block, part):
    t = 0
    for kind, k in order:
        t = 2 * t + ((block >> (k - 1)) & 1 if kind == "f" else (part >> k) & 1)
    return t


def state_kernel(moment_ref, second_ref, *refs):
    fulls, (new_m_ref, new_s_ref) = refs[:-2], refs[-2:]
    full = jnp.concatenate([full[...] for full in fulls], axis=1).T
    new_m_ref[...] = 0.9 * moment_ref[...] + 0.1 * full
    new_s_ref[...] = 0.999 * second_ref[...] + 0.001 * (full * full)


def project_kernel(n, m, width, a_hbm, own_hbm, g_hbm, b_ref, *refs):
    blocks, h_ref, outs, (a_ref, own_ref, g_ref, sems) = refs[: n - 1], refs[n - 1], refs[n:-4], refs[-4:]
    i, mine = lax.axis_index("fsdp"), lax.axis_index("dp")
    core, own = i & 1, i >> 1
    depth, rank = own_ref.shape
    half, size, _ = outs[0].shape
    rows = b_ref.shape[0]
    span = g_ref.shape[2]

    def columns_of(block):
        start = (2 * (block ^ own) + core) * width if span == width else (block ^ own) * span
        return pl.ds(pl.multiple_of(start, 128), span)

    first = [
        pltpu.make_async_copy(own_hbm, own_ref, sems.at[n // 2]),
        pltpu.make_async_copy(a_hbm, a_ref, sems.at[n // 2 + 1]),
    ]
    loads = [
        pltpu.make_async_copy(g_hbm.at[:, columns_of(block)], g_ref.at[block], sems.at[block])
        for block in range(n // 2)
    ]
    for load in first + loads:
        load.start()

    left = []
    for x_ref, load in zip((b_ref, a_ref), first):
        total = jnp.zeros((rows, rank), jnp.float32)
        if x_ref is a_ref:
            load.wait()
        for k in (*range(1, n), 0):
            if k == 0 and x_ref is b_ref:
                load.wait()
            w_ref = blocks[k - 1] if k else own_ref
            start = pl.multiple_of((2 * (own ^ (k >> 1)) + (core ^ (k & 1))) * depth, depth)
            total += jnp.dot(x_ref[:, pl.ds(start, depth)], w_ref[...], preferred_element_type=jnp.float32)
        total = total.T
        for k in range(bits_of(m)):
            swapped = [total[(p ^ (1 << k)) * size :][:size] for p in range(m)]
            total = jnp.where(((mine >> k) & 1) == 0, total, jnp.concatenate(swapped, axis=0))
        left.append(total.astype(jnp.bfloat16))

    def columns(c):
        for block in range(n // 2):
            acc = jnp.dot(left[0], h_ref[:, columns_of(block)], preferred_element_type=jnp.float32)
            loads[block].wait()
            acc += jnp.dot(left[1], g_ref[block], preferred_element_type=jnp.float32)
            if span != width:
                acc = acc[:, c * width : (c + 1) * width]
            for part in range(m):
                slot = slot_of(orders(n, m)[c], block, part)
                for (first, last), keep_ref, send_ref in zip(chunks_of(width), outs[::2], outs[1::2]):
                    piece = acc[part * size : (part + 1) * size, first:last]
                    if slot < half:
                        keep_ref[slot] = piece
                    else:
                        send_ref[slot - half] = piece.astype(jnp.bfloat16)

    for c in range(2):
        pl.when(core == c)(functools.partial(columns, c))


def expand_kernel(n, m, width, p_ref, *refs):
    parts, (o_ref, stage_ref, sems) = refs[:-3], refs[-3:]
    i = lax.axis_index("fsdp")
    core, own = i & 1, i >> 1
    half = parts[0].shape[0]
    paired = width % 128 != 0

    def rows(c):
        copies = []
        for block in range(n // 2):
            pair = []
            for owner in range(2):
                outs = []
                for k in range(len(chunks_of(width))):
                    mine = parts[4 * k : 4 * k + 2] if owner == c else parts[4 * k + 2 : 4 * k + 4]
                    slots = [slot_of(orders(n, m)[owner], block, part) for part in range(m)]
                    right = jnp.concatenate([mine[t // half][t % half] for t in slots], axis=0)
                    out = jnp.dot(p_ref[...], right, preferred_element_type=jnp.float32)
                    outs.append(out.astype(o_ref.dtype))
                pair.append(outs[0] if len(outs) == 1 else jnp.concatenate(outs, axis=1))
            whole = [jnp.concatenate(pair, axis=1)] if paired else pair
            for owner, out in enumerate(whole):
                k = block * len(whole) + owner
                start = (block ^ own) * 2 * width + owner * width
                stage_ref[k] = out
                copy = pltpu.make_async_copy(
                    stage_ref.at[k], o_ref.at[:, pl.ds(pl.multiple_of(start, 128), out.shape[1])], sems.at[k]
                )
                copy.start()
                copies.append(copy)
        for copy in copies:
            copy.wait()

    for c in range(2):
        pl.when(core == c)(functools.partial(rows, c))


def relative_ranks(x, y, m):
    size = x.shape[1] // m
    for k in range(bits_of(m)):
        swapped = jnp.concatenate([x[:, (p ^ (1 << k)) * size :][:, :size] for p in range(m)], axis=1)
        x = jnp.where(((y >> k) & 1) == 0, x, swapped)
    return x


def placed(space, *arrays):
    return [pltpu.with_memory_space_constraint(x, space) for x in arrays]


VMEM = pl.BlockSpec(memory_space=pltpu.VMEM)
HBM = pl.BlockSpec(memory_space=pltpu.HBM)


def local(n, m, inputs, grad_out, projection, moment, second):
    y = lax.axis_index("dp")
    width, rank = moment.shape
    size = rank // m
    partner = [(k, k ^ 1) for k in range(n)]

    inputs_too = lax.ppermute(inputs, "fsdp", partner)
    grad_too = lax.ppermute(grad_out, "fsdp", partner)

    held = {0: projection}
    held_too = {0: lax.ppermute(projection, "fsdp", partner)}
    for block, source, k in gather_plan(n):
        held[block] = lax.ppermute(held[source], "fsdp", [(w, w ^ (1 << k)) for w in range(n)])
        held_too[block] = lax.ppermute(held[block], "fsdp", partner)
    blocks = [x for block in range(n // 2) for x in (held[block], held_too[block])]

    half = n // 2 * m // 2
    shapes = [
        pltpu.VMEM((half, size, stop - start), dtype)
        for start, stop in chunks_of(width)
        for dtype in (jnp.float32, jnp.bfloat16)
    ]
    sums = pl.pallas_call(
        functools.partial(project_kernel, n, m, width),
        in_specs=[HBM] * 3 + [VMEM] * (n + 1),
        out_specs=[VMEM] * len(shapes),
        out_shape=shapes,
        scratch_shapes=[
            pltpu.VMEM(inputs.shape, inputs.dtype),
            pltpu.VMEM(projection.shape, projection.dtype),
            pltpu.VMEM((n // 2, inputs.shape[0], width if width % 128 == 0 else 2 * width), grad_out.dtype),
            pltpu.SemaphoreType.DMA((n // 2 + 2,)),
        ],
        compiler_params=pltpu.CompilerParams(vmem_limit_bytes=16 << 20),
        name="project",
    )(
        *placed(pltpu.HBM, inputs, projection, grad_out),
        *placed(pltpu.VMEM, inputs_too, *blocks[1:], grad_too),
    )

    moment_t = lax.dynamic_slice_in_dim(moment.T, y * size, size)
    second_t = lax.dynamic_slice_in_dim(second.T, y * size, size)
    first_fix = 1.0 - 0.9**STEP
    second_fix = 1.0 - 0.999**STEP
    steps = list(zip(*orders(n, m)))
    parts, fulls = [], []
    for chunk, (start, stop) in enumerate(chunks_of(width)):
        keep, send = sums[2 * chunk : 2 * chunk + 2]
        for s, both in enumerate(steps):
            got = lax.ppermute(send, AXES, pairs(n, m, both)).astype(jnp.float32)
            if s + 1 < len(steps):
                cut = keep.shape[0] // 2
                send = (keep[cut:] + got[cut:]).astype(jnp.bfloat16)
                keep = keep[:cut] + got[:cut]
            else:
                low_rank = (keep + got)[0]

        new_m = 0.9 * moment_t[:, start:stop] + 0.1 * low_rank
        new_s = 0.999 * second_t[:, start:stop] + 0.001 * (low_rank * low_rank)
        normalized = (new_m / first_fix / (jnp.sqrt(new_s / second_fix) + 1e-08)).astype(jnp.bfloat16)

        full = low_rank
        for k in range(bits_of(m)):
            got = lax.ppermute(full, "dp", [(w, w ^ (1 << k)) for w in range(m)])
            first = ((y >> k) & 1) == 0
            full = jnp.concatenate([jnp.where(first, full, got), jnp.where(first, got, full)], axis=0)

        held = normalized[None]
        for both in steps[:0:-1]:
            got = lax.ppermute(held, AXES, pairs(n, m, both))
            held = jnp.concatenate([held, got], axis=0)
        fulls.append(full)
        if stop == width:
            new_moment, new_second = pl.pallas_call(
                state_kernel,
                out_shape=[jax.ShapeDtypeStruct(moment.shape, jnp.float32)] * 2,
                compiler_params=pltpu.CompilerParams(vmem_limit_bytes=16 << 20),
                name="state",
            )(moment, second, *fulls)
        rest = lax.ppermute(held, AXES, pairs(n, m, steps[0]))
        if stop == width:
            rest, new_moment, new_second = lax.optimization_barrier((rest, new_moment, new_second))
        parts += [held, rest, lax.ppermute(held, "fsdp", partner), lax.ppermute(rest, "fsdp", partner)]

    copies = n if width % 128 == 0 else n // 2
    update = pl.pallas_call(
        functools.partial(expand_kernel, n, m, width),
        in_specs=[VMEM] * (1 + len(parts)),
        out_specs=HBM,
        out_shape=jax.ShapeDtypeStruct((projection.shape[0], n * width), jnp.bfloat16),
        scratch_shapes=[
            pltpu.VMEM((copies, projection.shape[0], n * width // copies), jnp.bfloat16),
            pltpu.SemaphoreType.DMA((copies,)),
        ],
        compiler_params=pltpu.CompilerParams(vmem_limit_bytes=16 << 20),
        name="expand",
    )(*placed(pltpu.VMEM, relative_ranks(projection, y, m), *parts))
    return (update, new_moment, new_second)


def solution(mesh):
    in_specs = (
        P(AXES, None),
        P(AXES, None),
        P("fsdp", None),
        P("fsdp", None),
        P("fsdp", None),
    )
    out_specs = (P("fsdp", None), P("fsdp", None), P("fsdp", None))

    def body(*args):
        return local(mesh.shape["fsdp"], mesh.shape["dp"], *args)

    return jax.shard_map(body, mesh=mesh, in_specs=in_specs, out_specs=out_specs, check_vma=False)
```

time: 253 us -> 105 us (0.42)
  waiting for transfers between devices: 209 us -> 48.4 us
  starting transfers between devices: 0.16 us -> 43.4 us
  matrix products: 14.7 us -> 0 us
  between operations: 13.8 us -> 0.85 us
  local copies, waits for them, and re-layouts: 12.5 us -> 0.77 us
  Pallas kernels: 0 us -> 9.66 us
    reduce_scatter x1 -> x0, waiting for transfers between devices: 90.7 us -> none  [local(): low_rank = lax.psum_scatter(whole, 'fsdp', scatter_dimension=0, tiled=True)]
    all_gather x2 -> x0, waiting for transfers between devices: 89.2 us -> none  [the longest x1 46.4 us: local(): lax.all_gather(normalized, 'fsdp', axis=0, tiled=True)]
    ppermute x0 -> x39, waiting for transfers between devices: none -> 48.4 us  [the longest x8 17.2 us: local(): got = lax.ppermute(send, AXES, pairs(n, m, both)).astype(jnp.float32)]
    ppermute x0 -> x39, starting transfers between devices: none -> 43.4 us  [the longest x7 15.3 us: local(): lax.ppermute(held[source], 'fsdp', [(w, w ^ 1 << k) for w in range(n)])]
    psum x1 -> x0, waiting for transfers between devices: 28.8 us -> none  [local(): whole = lax.psum(whole, 'dp')]
    dot_general x2 -> x0, matrix products: 14.7 us -> none  [the longest x1 7.64 us: local(): lax.dot_general(grad_out, projected, contract, preferred_element_type=jnp...]
    unnamed x13 -> x8, local copies, waits for them, and re-layouts: 12.5 us -> 0.38 us
    pallas_call x0 -> x3, Pallas kernels: none -> 9.66 us  [the longest x1 5.15 us: local(): pl.pallas_call(functools.partial(project_kernel, n, m, width), in_specs=[...]
  transfers between devices with their start and end apart: 4 -> 39, of which waited for: 4 -> 23; matrix products, arithmetic and copies ran while one was open for 1% -> 2% of each run, Pallas kernels for 0% -> 1%
where the time goes in v1:
time: 105 us; the launch traced here: 104 us
  waiting for transfers between devices  48.4 us (46%)
  starting transfers between devices  43.4 us (41%)
  Pallas kernels  9.66 us (9%)
  other arithmetic  1.35 us (1%)
    ppermute x8, waiting for transfers between devices, local(): got = lax.ppermute(send, AXES, pairs(n, m, both)).astype(jnp.float32)  17.2 us
    ppermute x7, starting transfers between devices, local(): lax.ppermute(held[source], 'fsdp', [(w, w ^ 1 << k) for w in range(n)])  15.3 us
    ppermute x8, starting transfers between devices, local(): got = lax.ppermute(send, AXES, pairs(n, m, both)).astype(jnp.float32)  12.3 us
    ppermute x6, waiting for transfers between devices, local(): got = lax.ppermute(held, AXES, pairs(n, m, both))  12 us
    ppermute x6, starting transfers between devices, local(): got = lax.ppermute(held, AXES, pairs(n, m, both))  11.3 us
    ppermute x7, waiting for transfers between devices, local(): lax.ppermute(held[source], 'fsdp', [(w, w ^ 1 << k) for w in range(n)])  5.98 us
    pallas_call x1, Pallas kernels, local(): pl.pallas_call(functools.partial(project_kernel, n, m, width), in_specs=[...  5.15 us
    ppermute x2, waiting for transfers between devices, local(): rest = lax.ppermute(held, AXES, pairs(n, m, steps[0]))  4.8 us
  transfers between devices with their start and end apart: 39, of which 23 were waited for; matrix products, arithmetic and copies ran while one was open for 2% of the time, Pallas kernels for 1%

profile of v1, /device:TPU:0, one launch (start us, length us, event | category | flops | bytes accessed | tf_op | source)
XLA Modules:
  0.0 104.5 jit_solution(10138229076902161959)
XLA Ops:
  0.6 0.6 collective-permute-start.16
  1.3 2.9 %collective-permute-start.2 = (bf16[256,128]{1,0:T(8,128)(2,1)}, bf16[256,128]{1,0:T(8,128)(2,1)S(1)}, u32[]{:S(2)}, u32[]{:S(2)}) collective-permute-start(bf16[256,128]{1,0:T(8,128)(2,1)} %own_hbm.1), channel_id=1, source_target_pairs={{0,4},{2,6},{4,0},{6,2},{8,12},{10,14},{12,8},{14,10},{16,20},{18,... | collective-permute-start | bytes 196616 | tf_op jit(solution)/shard_map/ppermute | solution.py:193
  4.2 1.6 %collective-permute-start.4 = (bf16[256,128]{1,0:T(8,128)(2,1)}, bf16[256,128]{1,0:T(8,128)(2,1)S(1)}, u32[]{:S(2)}, u32[]{:S(2)}) collective-permute-start(bf16[256,128]{1,0:T(8,128)(2,1)} %own_hbm.1), channel_id=1, source_target_pairs={{0,8},{2,10},{4,12},{6,14},{8,0},{10,2},{12,4},{14,6},{16,24},{18,... | collective-permute-start | bytes 196616 | tf_op jit(solution)/shard_map/ppermute | solution.py:193
  5.8 1.0 collective-permute-done.2.refs_1_
  6.7 3.0 %collective-permute-start.8 = (bf16[256,128]{1,0:T(8,128)(2,1)}, bf16[256,128]{1,0:T(8,128)(2,1)S(1)}, u32[]{:S(2)}, u32[]{:S(2)}) collective-permute-start(bf16[256,128]{1,0:T(8,128)(2,1)} %own_hbm.1), channel_id=1, source_target_pairs={{0,16},{2,18},{4,20},{6,22},{8,24},{10,26},{12,28},{14,30},{16,0},... | collective-permute-start | bytes 196616 | tf_op jit(solution)/shard_map/ppermute | solution.py:193
  9.7 2.7 %collective-permute-done.1.refs_0_ = bf16[256,128]{1,0:T(8,128)(2,1)S(1)} collective-permute-done((bf16[256,128]{1,0:T(8,128)(2,1)}, bf16[256,128]{1,0:T(8,128)(2,1)S(1)}, u32[]{:S(2)}, u32[]{:S(2)}) %collective-permute-start.1) | collective-permute-done | bytes 65568 | tf_op jit(solution)/shard_map/ppermute | solution.py:191
  12.4 0.4 collective-permute-start.3
  12.8 2.6 %collective-permute-start.6 = (bf16[256,128]{1,0:T(8,128)(2,1)S(1)}, bf16[256,128]{1,0:T(8,128)(2,1)S(1)}, u32[]{:S(2)}, u32[]{:S(2)}) collective-permute-start(bf16[256,128]{1,0:T(8,128)(2,1)S(1)} %collective-permute-done.4.refs_3_), channel_id=1, source_target_pairs={{0,4},{2,6},{4,0},{6,2},{8,12},{10,14},{12,8},{14,10},{16,20},{18,... | collective-permute-start | bytes 196616 | tf_op jit(solution)/shard_map/ppermute | solution.py:193
  15.5 1.6 %collective-permute-start.12 = (bf16[256,128]{1,0:T(8,128)(2,1)S(1)}, bf16[256,128]{1,0:T(8,128)(2,1)S(1)}, u32[]{:S(2)}, u32[]{:S(2)}) collective-permute-start(bf16[256,128]{1,0:T(8,128)(2,1)S(1)} %collective-permute-done.8.refs_7_), channel_id=1, source_target_pairs={{0,8},{2,10},{4,12},{6,14},{8,0},{10,2},{12,4},{14,6},{16,24},{18,... | collective-permute-start | bytes 196616 | tf_op jit(solution)/shard_map/ppermute | solution.py:193
  17.1 0.9 collective-permute-done.6.refs_5_
  18.0 1.7 %collective-permute-start.10 = (bf16[256,128]{1,0:T(8,128)(2,1)S(1)}, bf16[256,128]{1,0:T(8,128)(2,1)S(1)}, u32[]{:S(2)}, u32[]{:S(2)}) collective-permute-start(bf16[256,128]{1,0:T(8,128)(2,1)S(1)} %collective-permute-done.8.refs_7_), channel_id=1, source_target_pairs={{0,4},{2,6},{4,0},{6,2},{8,12},{10,14},{12,8},{14,10},{16,20},{18,... | collective-permute-start | bytes 196616 | tf_op jit(solution)/shard_map/ppermute | solution.py:193
  19.9 0.4 collective-permute-start.7
  20.3 2.0 %collective-permute-done.10.refs_9_ = bf16[256,128]{1,0:T(8,128)(2,1)S(1)} collective-permute-done((bf16[256,128]{1,0:T(8,128)(2,1)S(1)}, bf16[256,128]{1,0:T(8,128)(2,1)S(1)}, u32[]{:S(2)}, u32[]{:S(2)}) %collective-permute-start.10) | collective-permute-done | bytes 65568 | tf_op jit(solution)/shard_map/ppermute | solution.py:193
  22.3 1.8 %collective-permute-start.14 = (bf16[256,128]{1,0:T(8,128)(2,1)S(1)}, bf16[256,128]{1,0:T(8,128)(2,1)S(1)}, u32[]{:S(2)}, u32[]{:S(2)}) collective-permute-start(bf16[256,128]{1,0:T(8,128)(2,1)S(1)} %collective-permute-done.10.refs_9_), channel_id=1, source_target_pairs={{0,8},{2,10},{4,12},{6,14},{8,0},{10,2},{12,4},{14,6},{16,24},{18,... | collective-permute-start | bytes 196616 | tf_op jit(solution)/shard_map/ppermute | solution.py:193
  24.1 0.5 collective-permute-start.13
  24.6 1.9 %collective-permute-done.14.refs_13_ = bf16[256,128]{1,0:T(8,128)(2,1)S(1)} collective-permute-done((bf16[256,128]{1,0:T(8,128)(2,1)S(1)}, bf16[256,128]{1,0:T(8,128)(2,1)S(1)}, u32[]{:S(2)}, u32[]{:S(2)}) %collective-permute-start.14) | collective-permute-done | bytes 65568 | tf_op jit(solution)/shard_map/ppermute | solution.py:193
  26.6 1.2 %collective-permute-done.15.refs_14_ = bf16[256,128]{1,0:T(8,128)(2,1)S(1)} collective-permute-done((bf16[256,128]{1,0:T(8,128)(2,1)S(1)}, bf16[256,128]{1,0:T(8,128)(2,1)S(1)}, u32[]{:S(2)}, u32[]{:S(2)}) %collective-permute-start.15) | collective-permute-done | bytes 65568 | tf_op jit(solution)/shard_map/ppermute | solution.py:194
  27.8 5.2 %project.1 = (f32[8,64,384]{2,1,0:T(8,128)S(1)}, bf16[8,64,384]{2,1,0:T(8,128)(2,1)S(1)}, f32[8,64,512]{2,1,0:T(8,128)S(1)}, bf16[8,64,512]{2,1,0:T(8,128)(2,1)S(1)}) custom-call(bf16[192,4096]{1,0:T(8,128)(2,1)} %a_hbm.1, bf16[256,128]{1,0:T(8,128)(2,1)} %own_hbm.1, bf16[192,14336]{1,0:T(8,128)(2,1)} %g_hbm.1, ...), custom_call_target="tpu_custom_call" | custom-call | tf_op jit(solution)/shard_map/project/pallas_call | solution.py:203
  33.0 1.8 %collective-permute-start.17 = (bf16[8,64,384]{2,1,0:T(8,128)(2,1)S(1)}, bf16[8,64,384]{2,1,0:T(8,128)(2,1)S(1)}, u32[]{:S(2)}, u32[]{:S(2)}) collective-permute-start(bf16[8,64,384]{2,1,0:T(8,128)(2,1)S(1)} %get-tuple-element.13), channel_id=1, source_target_pairs={{0,4},{1,5},{2,3},{3,2},{4,0},{5,1},{6,7},{7,6},{8,12},{9,13},{10,... | collective-permute-start | bytes 1179656 | tf_op jit(solution)/shard_map/ppermute | solution.py:230
  35.1 5.8 %collective-permute-done.17 = bf16[8,64,384]{2,1,0:T(8,128)(2,1)S(1)} collective-permute-done((bf16[8,64,384]{2,1,0:T(8,128)(2,1)S(1)}, bf16[8,64,384]{2,1,0:T(8,128)(2,1)S(1)}, u32[]{:S(2)}, u32[]{:S(2)}) %collective-permute-start.17) | collective-permute-done | bytes 393248 | tf_op jit(solution)/shard_map/ppermute | solution.py:230
  41.0 1.8 %collective-permute-start.18 = (bf16[4,64,384]{2,1,0:T(8,128)(2,1)S(1)}, bf16[4,64,384]{2,1,0:T(8,128)(2,1)S(1)}, u32[]{:S(2)}, u32[]{:S(2)}) collective-permute-start(bf16[4,64,384]{2,1,0:T(8,128)(2,1)S(1)} %get-tuple-element.28), channel_id=1, source_target_pairs={{0,1},{1,0},{2,10},{3,11},{4,5},{5,4},{6,14},{7,15},{8,9},{9,8},{1... | collective-permute-start | bytes 589832 | tf_op jit(solution)/shard_map/ppermute | solution.py:230
  42.8 3.6 %collective-permute-done.27 = bf16[8,64,512]{2,1,0:T(8,128)(2,1)S(1)} collective-permute-done((bf16[8,64,512]{2,1,0:T(8,128)(2,1)S(1)}, bf16[8,64,512]{2,1,0:T(8,128)(2,1)S(1)}, u32[]{:S(2)}, u32[]{:S(2)}) %collective-permute-start.27) | collective-permute-done | bytes 524320 | tf_op jit(solution)/shard_map/ppermute | solution.py:230
  46.8 1.8 %collective-permute-start.28 = (bf16[4,64,512]{2,1,0:T(8,128)(2,1)S(1)}, bf16[4,64,512]{2,1,0:T(8,128)(2,1)S(1)}, u32[]{:S(2)}, u32[]{:S(2)}) collective-permute-start(bf16[4,64,512]{2,1,0:T(8,128)(2,1)S(1)} %get-tuple-element.26), channel_id=1, source_target_pairs={{0,1},{1,0},{2,10},{3,11},{4,5},{5,4},{6,14},{7,15},{8,9},{9,8},{1... | collective-permute-start | bytes 786440 | tf_op jit(solution)/shard_map/ppermute | solution.py:230
  48.7 1.6 %collective-permute-start.19 = (bf16[2,64,384]{2,1,0:T(8,128)(2,1)S(1)}, bf16[2,64,384]{2,1,0:T(8,128)(2,1)S(1)}, u32[]{:S(2)}, u32[]{:S(2)}) collective-permute-start(bf16[2,64,384]{2,1,0:T(8,128)(2,1)S(1)} %get-tuple-element.32), channel_id=1, source_target_pairs={{0,8},{1,9},{2,6},{3,7},{4,12},{5,13},{6,2},{7,3},{8,0},{9,1},{10,... | collective-permute-start | bytes 294920 | tf_op jit(solution)/shard_map/ppermute | solution.py:230
  50.4 2.9 %collective-permute-done.28 = bf16[4,64,512]{2,1,0:T(8,128)(2,1)S(1)} collective-permute-done((bf16[4,64,512]{2,1,0:T(8,128)(2,1)S(1)}, bf16[4,64,512]{2,1,0:T(8,128)(2,1)S(1)}, u32[]{:S(2)}, u32[]{:S(2)}) %collective-permute-start.28) | collective-permute-done | bytes 262176 | tf_op jit(solution)/shard_map/ppermute | solution.py:230
  53.4 1.9 %collective-permute-start.29 = (bf16[2,64,512]{2,1,0:T(8,128)(2,1)S(1)}, bf16[2,64,512]{2,1,0:T(8,128)(2,1)S(1)}, u32[]{:S(2)}, u32[]{:S(2)}) collective-permute-start(bf16[2,64,512]{2,1,0:T(8,128)(2,1)S(1)} %get-tuple-element.30), channel_id=1, source_target_pairs={{0,8},{1,9},{2,6},{3,7},{4,12},{5,13},{6,2},{7,3},{8,0},{9,1},{10,... | collective-permute-start | bytes 393224 | tf_op jit(solution)/shard_map/ppermute | solution.py:230
  56.0 2.4 %collective-permute-done.29 = bf16[2,64,512]{2,1,0:T(8,128)(2,1)S(1)} collective-permute-done((bf16[2,64,512]{2,1,0:T(8,128)(2,1)S(1)}, bf16[2,64,512]{2,1,0:T(8,128)(2,1)S(1)}, u32[]{:S(2)}, u32[]{:S(2)}) %collective-permute-start.29) | collective-permute-done | bytes 131104 | tf_op jit(solution)/shard_map/ppermute | solution.py:230
  58.5 2.9 %collective-permute-start.30 = (bf16[1,64,512]{2,1,0:T(8,128)(2,1)S(1)}, bf16[1,64,512]{2,1,0:T(8,128)(2,1)S(1)}, u32[]{:S(2)}, u32[]{:S(2)}) collective-permute-start(bf16[1,64,512]{2,1,0:T(8,128)(2,1)S(1)} %fusion.9), channel_id=1, source_target_pairs={{0,16},{1,17},{2,18},{3,19},{4,20},{5,21},{6,22},{7,23},{8,24},{9,... | collective-permute-start | bytes 196616 | tf_op jit(solution)/shard_map/ppermute | solution.py:230
  61.6 2.3 %collective-permute-done.30 = bf16[1,64,512]{2,1,0:T(8,128)(2,1)S(1)} collective-permute-done((bf16[1,64,512]{2,1,0:T(8,128)(2,1)S(1)}, bf16[1,64,512]{2,1,0:T(8,128)(2,1)S(1)}, u32[]{:S(2)}, u32[]{:S(2)}) %collective-permute-start.30) | collective-permute-done | bytes 65568 | tf_op jit(solution)/shard_map/ppermute | solution.py:230
  64.0 2.7 %collective-permute-start.31 = (bf16[1,64,512]{2,1,0:T(8,128)(2,1)S(1)}, bf16[1,64,512]{2,1,0:T(8,128)(2,1)S(1)}, u32[]{:S(2)}, u32[]{:S(2)}) collective-permute-start(bf16[1,64,512]{2,1,0:T(8,128)(2,1)S(1)} %get-tuple-element.21), channel_id=1, source_target_pairs={{0,16},{1,17},{2,18},{3,19},{4,20},{5,21},{6,22},{7,23},{8,24},{9,... | collective-permute-start | bytes 196616 | tf_op jit(solution)/shard_map/ppermute | solution.py:250
  67.2 2.1 %collective-permute-done.31 = bf16[1,64,512]{2,1,0:T(8,128)(2,1)S(1)} collective-permute-done((bf16[1,64,512]{2,1,0:T(8,128)(2,1)S(1)}, bf16[1,64,512]{2,1,0:T(8,128)(2,1)S(1)}, u32[]{:S(2)}, u32[]{:S(2)}) %collective-permute-start.31) | collective-permute-done | bytes 65568 | tf_op jit(solution)/shard_map/ppermute | solution.py:250
  69.3 4.4 %collective-permute-start.32 = (bf16[2,64,512]{2,1,0:T(8,128)(2,1)S(1)}, bf16[2,64,512]{2,1,0:T(8,128)(2,1)S(1)}, u32[]{:S(2)}, u32[]{:S(2)}) collective-permute-start(bf16[2,64,512]{2,1,0:T(8,128)(2,1)S(1)} %pad_maximum_fusion.6), channel_id=1, source_target_pairs={{0,8},{1,9},{2,6},{3,7},{4,12},{5,13},{6,2},{7,3},{8,0},{9,1},{10,... | collective-permute-start | bytes 393224 | tf_op jit(solution)/shard_map/ppermute | solution.py:250
  74.0 2.0 %collective-permute-start.22 = (bf16[2,64,384]{2,1,0:T(8,128)(2,1)S(1)}, bf16[2,64,384]{2,1,0:T(8,128)(2,1)S(1)}, u32[]{:S(2)}, u32[]{:S(2)}) collective-permute-start(bf16[2,64,384]{2,1,0:T(8,128)(2,1)S(1)} %pad_maximum_fusion.7), channel_id=1, source_target_pairs={{0,8},{1,9},{2,6},{3,7},{4,12},{5,13},{6,2},{7,3},{8,0},{9,1},{10,... | collective-permute-start | bytes 294920 | tf_op jit(solution)/shard_map/ppermute | solution.py:250
  76.0 1.2 %collective-permute-done.32 = bf16[2,64,512]{2,1,0:T(8,128)(2,1)S(1)} collective-permute-done((bf16[2,64,512]{2,1,0:T(8,128)(2,1)S(1)}, bf16[2,64,512]{2,1,0:T(8,128)(2,1)S(1)}, u32[]{:S(2)}, u32[]{:S(2)}) %collective-permute-start.32) | collective-permute-done | bytes 131104 | tf_op jit(solution)/shard_map/ppermute | solution.py:250
  77.3 1.0 collective-permute-done.35
  78.4 1.4 %collective-permute-done.22 = bf16[2,64,384]{2,1,0:T(8,128)(2,1)S(1)} collective-permute-done((bf16[2,64,384]{2,1,0:T(8,128)(2,1)S(1)}, bf16[2,64,384]{2,1,0:T(8,128)(2,1)S(1)}, u32[]{:S(2)}, u32[]{:S(2)}) %collective-permute-start.22) | collective-permute-done | bytes 98336 | tf_op jit(solution)/shard_map/ppermute | solution.py:250
  79.8 1.9 %collective-permute-start.23 = (bf16[4,64,384]{2,1,0:T(8,128)(2,1)S(1)}, bf16[4,64,384]{2,1,0:T(8,128)(2,1)S(1)}, u32[]{:S(2)}, u32[]{:S(2)}) collective-permute-start(bf16[4,64,384]{2,1,0:T(8,128)(2,1)S(1)} %pad_maximum_fusion.4), channel_id=1, source_target_pairs={{0,1},{1,0},{2,10},{3,11},{4,5},{5,4},{6,14},{7,15},{8,9},{9,8},{1... | collective-permute-start | bytes 589832 | tf_op jit(solution)/shard_map/ppermute | solution.py:250
  81.8 4.0 %collective-permute-done.33 = bf16[4,64,512]{2,1,0:T(8,128)(2,1)S(1)} collective-permute-done((bf16[4,64,512]{2,1,0:T(8,128)(2,1)S(1)}, bf16[4,64,512]{2,1,0:T(8,128)(2,1)S(1)}, u32[]{:S(2)}, u32[]{:S(2)}) %collective-permute-start.33) | collective-permute-done | bytes 262176 | tf_op jit(solution)/shard_map/ppermute | solution.py:250
  85.9 0.7 collective-permute-start.34
  86.7 3.4 %collective-permute-done.23 = bf16[4,64,384]{2,1,0:T(8,128)(2,1)S(1)} collective-permute-done((bf16[4,64,384]{2,1,0:T(8,128)(2,1)S(1)}, bf16[4,64,384]{2,1,0:T(8,128)(2,1)S(1)}, u32[]{:S(2)}, u32[]{:S(2)}) %collective-permute-start.23) | collective-permute-done | bytes 196640 | tf_op jit(solution)/shard_map/ppermute | solution.py:250
  90.1 0.7 collective-permute-start.24
  90.9 2.0 %collective-permute-done.36 = f32[64,512]{1,0:T(8,128)S(1)} collective-permute-done((f32[64,512]{1,0:T(8,128)S(1)}, f32[64,512]{1,0:T(8,128)S(1)}, u32[]{:S(2)}, u32[]{:S(2)}) %collective-permute-start.36) | collective-permute-done | bytes 131104 | tf_op jit(solution)/shard_map/ppermute | solution.py:244
  92.9 1.1 %state.1 = (f32[896,128]{1,0:T(8,128)}, f32[896,128]{1,0:T(8,128)}) custom-call(f32[896,128]{1,0:T(8,128)S(1)} %copy-done.1, f32[896,128]{1,0:T(8,128)S(1)} %copy-done, f32[128,384]{1,0:T(8,128)S(1)} %pad_maximum_fusion.5.refs_0_, f32[128,512]{1,0:T(8,128)S(1)} %pad_maximum_fusion.3.refs_1_), custom_call_target="tpu_custom_call" | custom-call | tf_op jit(solution)/shard_map/state/pallas_call | solution.py:254
  94.0 1.1 %collective-permute-done.34.refs_5_ = bf16[8,64,512]{2,1,0:T(8,128)(2,1)S(1)} collective-permute-done((bf16[8,64,512]{2,1,0:T(8,128)(2,1)S(1)}, bf16[8,64,512]{2,1,0:T(8,128)(2,1)S(1)}, u32[]{:S(2)}, u32[]{:S(2)}) %collective-permute-start.34) | collective-permute-done | bytes 524320 | tf_op jit(solution)/shard_map/ppermute | solution.py:260
  95.2 0.5 collective-permute-start.25
  95.7 3.7 %collective-permute-done.24.refs_1_ = bf16[8,64,384]{2,1,0:T(8,128)(2,1)S(1)} collective-permute-done((bf16[8,64,384]{2,1,0:T(8,128)(2,1)S(1)}, bf16[8,64,384]{2,1,0:T(8,128)(2,1)S(1)}, u32[]{:S(2)}, u32[]{:S(2)}) %collective-permute-start.24) | collective-permute-done | bytes 393248 | tf_op jit(solution)/shard_map/ppermute | solution.py:260
  99.6 1.5 %collective-permute-done.26.refs_3_ = bf16[8,64,384]{2,1,0:T(8,128)(2,1)S(1)} collective-permute-done((bf16[8,64,384]{2,1,0:T(8,128)(2,1)S(1)}, bf16[8,64,384]{2,1,0:T(8,128)(2,1)S(1)}, u32[]{:S(2)}, u32[]{:S(2)}) %collective-permute-start.26) | collective-permute-done | bytes 393248 | tf_op jit(solution)/shard_map/ppermute | solution.py:263
  101.1 3.4 %expand.1 = bf16[256,14336]{1,0:T(8,128)(2,1)} custom-call(bf16[256,128]{1,0:T(8,128)(2,1)S(1)} %maximum_select_fusion.p_ref, bf16[8,64,384]{2,1,0:T(8,128)(2,1)S(1)} %pad_maximum_fusion.1.refs_0_, bf16[8,64,384]{2,1,0:T(8,128)(2,1)S(1)} %collective-permute-done.24.refs_1_, bf16[8,64,384]{2,1,0:T(8,128)(2,1)S(1)} %collective-permute-done.25.refs_2_, ...), custom_call_target="tpu_custom_call" | custom-call | tf_op jit(solution)/shard_map/expand/pallas_call | solution.py:266
  (68 shorter events, 3.9 us)
Async XLA Ops:
  0.6 27.2 %collective-permute-start.16 = (bf16[192,14336]{1,0:T(8,128)(2,1)}, bf16[192,14336]{1,0:T(8,128)(2,1)S(1)}, u32[]{:S(2)}, u32[]{:S(2)}) collective-permute-start(bf16[192,14336]{1,0:T(8,128)(2,1)} %g_hbm.1), channel_id=1, source_target_pairs={{0,2},{2,0},{4,6},{6,4},{8,10},{10,8},{12,14},{14,12},{16,18},{18,... | collective-permute-start | bytes 16515080 | tf_op jit(solution)/shard_map/ppermute | solution.py:188
  1.2 26.6 %collective-permute-start = (bf16[192,4096]{1,0:T(8,128)(2,1)}, bf16[192,4096]{1,0:T(8,128)(2,1)S(1)}, u32[]{:S(2)}, u32[]{:S(2)}) collective-permute-start(bf16[192,4096]{1,0:T(8,128)(2,1)} %a_hbm.1), channel_id=1, source_target_pairs={{0,2},{2,0},{4,6},{6,4},{8,10},{10,8},{12,14},{14,12},{16,18},{18,... | collective-permute-start | bytes 4718600 | tf_op jit(solution)/shard_map/ppermute | solution.py:187
  1.3 5.4 %collective-permute-start.2 = (bf16[256,128]{1,0:T(8,128)(2,1)}, bf16[256,128]{1,0:T(8,128)(2,1)S(1)}, u32[]{:S(2)}, u32[]{:S(2)}) collective-permute-start(bf16[256,128]{1,0:T(8,128)(2,1)} %own_hbm.1), channel_id=1, source_target_pairs={{0,4},{2,6},{4,0},{6,2},{8,12},{10,14},{12,8},{14,10},{16,20},{18,... | collective-permute-start | bytes 196616 | tf_op jit(solution)/shard_map/ppermute | solution.py:193
  4.2 8.2 %collective-permute-start.1 = (bf16[256,128]{1,0:T(8,128)(2,1)}, bf16[256,128]{1,0:T(8,128)(2,1)S(1)}, u32[]{:S(2)}, u32[]{:S(2)}) collective-permute-start(bf16[256,128]{1,0:T(8,128)(2,1)} %own_hbm.1), channel_id=1, source_target_pairs={{0,2},{2,0},{4,6},{6,4},{8,10},{10,8},{12,14},{14,12},{16,18},{18,... | collective-permute-start | bytes 196616 | tf_op jit(solution)/shard_map/ppermute | solution.py:191
  4.2 8.6 %collective-permute-start.4 = (bf16[256,128]{1,0:T(8,128)(2,1)}, bf16[256,128]{1,0:T(8,128)(2,1)S(1)}, u32[]{:S(2)}, u32[]{:S(2)}) collective-permute-start(bf16[256,128]{1,0:T(8,128)(2,1)} %own_hbm.1), channel_id=1, source_target_pairs={{0,8},{2,10},{4,12},{6,14},{8,0},{10,2},{12,4},{14,6},{16,24},{18,... | collective-permute-start | bytes 196616 | tf_op jit(solution)/shard_map/ppermute | solution.py:193
  6.7 8.7 %collective-permute-start.8 = (bf16[256,128]{1,0:T(8,128)(2,1)}, bf16[256,128]{1,0:T(8,128)(2,1)S(1)}, u32[]{:S(2)}, u32[]{:S(2)}) collective-permute-start(bf16[256,128]{1,0:T(8,128)(2,1)} %own_hbm.1), channel_id=1, source_target_pairs={{0,16},{2,18},{4,20},{6,22},{8,24},{10,26},{12,28},{14,30},{16,0},... | collective-permute-start | bytes 196616 | tf_op jit(solution)/shard_map/ppermute | solution.py:193
  12.4 3.1 %collective-permute-start.3 = (bf16[256,128]{1,0:T(8,128)(2,1)S(1)}, bf16[256,128]{1,0:T(8,128)(2,1)S(1)}, u32[]{:S(2)}, u32[]{:S(2)}) collective-permute-start(bf16[256,128]{1,0:T(8,128)(2,1)S(1)} %collective-permute-done.2.refs_1_), channel_id=1, source_target_pairs={{0,2},{2,0},{4,6},{6,4},{8,10},{10,8},{12,14},{14,12},{16,18},{18,... | collective-permute-start | bytes 196616 | tf_op jit(solution)/shard_map/ppermute | solution.py:194
  12.8 5.2 %collective-permute-start.6 = (bf16[256,128]{1,0:T(8,128)(2,1)S(1)}, bf16[256,128]{1,0:T(8,128)(2,1)S(1)}, u32[]{:S(2)}, u32[]{:S(2)}) collective-permute-start(bf16[256,128]{1,0:T(8,128)(2,1)S(1)} %collective-permute-done.4.refs_3_), channel_id=1, source_target_pairs={{0,4},{2,6},{4,0},{6,2},{8,12},{10,14},{12,8},{14,10},{16,20},{18,... | collective-permute-start | bytes 196616 | tf_op jit(solution)/shard_map/ppermute | solution.py:193
  15.4 4.4 %collective-permute-start.5 = (bf16[256,128]{1,0:T(8,128)(2,1)S(1)}, bf16[256,128]{1,0:T(8,128)(2,1)S(1)}, u32[]{:S(2)}, u32[]{:S(2)}) collective-permute-start(bf16[256,128]{1,0:T(8,128)(2,1)S(1)} %collective-permute-done.4.refs_3_), channel_id=1, source_target_pairs={{0,2},{2,0},{4,6},{6,4},{8,10},{10,8},{12,14},{14,12},{16,18},{18,... | collective-permute-start | bytes 196616 | tf_op jit(solution)/shard_map/ppermute | solution.py:194
  15.5 4.4 %collective-permute-start.12 = (bf16[256,128]{1,0:T(8,128)(2,1)S(1)}, bf16[256,128]{1,0:T(8,128)(2,1)S(1)}, u32[]{:S(2)}, u32[]{:S(2)}) collective-permute-start(bf16[256,128]{1,0:T(8,128)(2,1)S(1)} %collective-permute-done.8.refs_7_), channel_id=1, source_target_pairs={{0,8},{2,10},{4,12},{6,14},{8,0},{10,2},{12,4},{14,6},{16,24},{18,... | collective-permute-start | bytes 196616 | tf_op jit(solution)/shard_map/ppermute | solution.py:193
  18.0 4.3 %collective-permute-start.10 = (bf16[256,128]{1,0:T(8,128)(2,1)S(1)}, bf16[256,128]{1,0:T(8,128)(2,1)S(1)}, u32[]{:S(2)}, u32[]{:S(2)}) collective-permute-start(bf16[256,128]{1,0:T(8,128)(2,1)S(1)} %collective-permute-done.8.refs_7_), channel_id=1, source_target_pairs={{0,4},{2,6},{4,0},{6,2},{8,12},{10,14},{12,8},{14,10},{16,20},{18,... | collective-permute-start | bytes 196616 | tf_op jit(solution)/shard_map/ppermute | solution.py:193
  19.8 4.4 %collective-permute-start.9 = (bf16[256,128]{1,0:T(8,128)(2,1)S(1)}, bf16[256,128]{1,0:T(8,128)(2,1)S(1)}, u32[]{:S(2)}, u32[]{:S(2)}) collective-permute-start(bf16[256,128]{1,0:T(8,128)(2,1)S(1)} %collective-permute-done.8.refs_7_), channel_id=1, source_target_pairs={{0,2},{2,0},{4,6},{6,4},{8,10},{10,8},{12,14},{14,12},{16,18},{18,... | collective-permute-start | bytes 196616 | tf_op jit(solution)/shard_map/ppermute | solution.py:194
  19.9 4.2 %collective-permute-start.7 = (bf16[256,128]{1,0:T(8,128)(2,1)S(1)}, bf16[256,128]{1,0:T(8,128)(2,1)S(1)}, u32[]{:S(2)}, u32[]{:S(2)}) collective-permute-start(bf16[256,128]{1,0:T(8,128)(2,1)S(1)} %collective-permute-done.6.refs_5_), channel_id=1, source_target_pairs={{0,2},{2,0},{4,6},{6,4},{8,10},{10,8},{12,14},{14,12},{16,18},{18,... | collective-permute-start | bytes 196616 | tf_op jit(solution)/shard_map/ppermute | solution.py:194
  22.3 4.3 %collective-permute-start.14 = (bf16[256,128]{1,0:T(8,128)(2,1)S(1)}, bf16[256,128]{1,0:T(8,128)(2,1)S(1)}, u32[]{:S(2)}, u32[]{:S(2)}) collective-permute-start(bf16[256,128]{1,0:T(8,128)(2,1)S(1)} %collective-permute-done.10.refs_9_), channel_id=1, source_target_pairs={{0,8},{2,10},{4,12},{6,14},{8,0},{10,2},{12,4},{14,6},{16,24},{18,... | collective-permute-start | bytes 196616 | tf_op jit(solution)/shard_map/ppermute | solution.py:193
  24.1 2.4 %collective-permute-start.11 = (bf16[256,128]{1,0:T(8,128)(2,1)S(1)}, bf16[256,128]{1,0:T(8,128)(2,1)S(1)}, u32[]{:S(2)}, u32[]{:S(2)}) collective-permute-start(bf16[256,128]{1,0:T(8,128)(2,1)S(1)} %collective-permute-done.10.refs_9_), channel_id=1, source_target_pairs={{0,2},{2,0},{4,6},{6,4},{8,10},{10,8},{12,14},{14,12},{16,18},{18,... | collective-permute-start | bytes 196616 | tf_op jit(solution)/shard_map/ppermute | solution.py:194
  24.1 2.4 %collective-permute-start.13 = (bf16[256,128]{1,0:T(8,128)(2,1)S(1)}, bf16[256,128]{1,0:T(8,128)(2,1)S(1)}, u32[]{:S(2)}, u32[]{:S(2)}) collective-permute-start(bf16[256,128]{1,0:T(8,128)(2,1)S(1)} %collective-permute-done.12.refs_11_), channel_id=1, source_target_pairs={{0,2},{2,0},{4,6},{6,4},{8,10},{10,8},{12,14},{14,12},{16,18},{18,... | collective-permute-start | bytes 196616 | tf_op jit(solution)/shard_map/ppermute | solution.py:194
  26.6 1.3 %collective-permute-start.15 = (bf16[256,128]{1,0:T(8,128)(2,1)S(1)}, bf16[256,128]{1,0:T(8,128)(2,1)S(1)}, u32[]{:S(2)}, u32[]{:S(2)}) collective-permute-start(bf16[256,128]{1,0:T(8,128)(2,1)S(1)} %collective-permute-done.14.refs_13_), channel_id=1, source_target_pairs={{0,2},{2,0},{4,6},{6,4},{8,10},{10,8},{12,14},{14,12},{16,18},{18,... | collective-permute-start | bytes 196616 | tf_op jit(solution)/shard_map/ppermute | solution.py:194
  33.0 7.8 %collective-permute-start.17 = (bf16[8,64,384]{2,1,0:T(8,128)(2,1)S(1)}, bf16[8,64,384]{2,1,0:T(8,128)(2,1)S(1)}, u32[]{:S(2)}, u32[]{:S(2)}) collective-permute-start(bf16[8,64,384]{2,1,0:T(8,128)(2,1)S(1)} %get-tuple-element.13), channel_id=1, source_target_pairs={{0,4},{1,5},{2,3},{3,2},{4,0},{5,1},{6,7},{7,6},{8,12},{9,13},{10,... | collective-permute-start | bytes 1179656 | tf_op jit(solution)/shard_map/ppermute | solution.py:230
  34.8 11.7 %collective-permute-start.27 = (bf16[8,64,512]{2,1,0:T(8,128)(2,1)S(1)}, bf16[8,64,512]{2,1,0:T(8,128)(2,1)S(1)}, u32[]{:S(2)}, u32[]{:S(2)}) collective-permute-start(bf16[8,64,512]{2,1,0:T(8,128)(2,1)S(1)} %get-tuple-element.15), channel_id=1, source_target_pairs={{0,4},{1,5},{2,3},{3,2},{4,0},{5,1},{6,7},{7,6},{8,12},{9,13},{10,... | collective-permute-start | bytes 1572872 | tf_op jit(solution)/shard_map/ppermute | solution.py:230
  40.9 14.4 %copy-start = (f32[896,128]{1,0:T(8,128)S(1)}, f32[896,128]{1,0:T(8,128)}, u32[]{:S(2)}) copy-start(f32[896,128]{1,0:T(8,128)} %second_ref.1) | copy-start | bytes 1376260
  40.9 14.4 %copy-start.1 = (f32[896,128]{1,0:T(8,128)S(1)}, f32[896,128]{1,0:T(8,128)}, u32[]{:S(2)}) copy-start(f32[896,128]{1,0:T(8,128)} %moment_ref.1) | copy-start | bytes 1376260
  41.0 7.6 %collective-permute-start.18 = (bf16[4,64,384]{2,1,0:T(8,128)(2,1)S(1)}, bf16[4,64,384]{2,1,0:T(8,128)(2,1)S(1)}, u32[]{:S(2)}, u32[]{:S(2)}) collective-permute-start(bf16[4,64,384]{2,1,0:T(8,128)(2,1)S(1)} %get-tuple-element.28), channel_id=1, source_target_pairs={{0,1},{1,0},{2,10},{3,11},{4,5},{5,4},{6,14},{7,15},{8,9},{9,8},{1... | collective-permute-start | bytes 589832 | tf_op jit(solution)/shard_map/ppermute | solution.py:230
  46.8 6.4 %collective-permute-start.28 = (bf16[4,64,512]{2,1,0:T(8,128)(2,1)S(1)}, bf16[4,64,512]{2,1,0:T(8,128)(2,1)S(1)}, u32[]{:S(2)}, u32[]{:S(2)}) collective-permute-start(bf16[4,64,512]{2,1,0:T(8,128)(2,1)S(1)} %get-tuple-element.26), channel_id=1, source_target_pairs={{0,1},{1,0},{2,10},{3,11},{4,5},{5,4},{6,14},{7,15},{8,9},{9,8},{1... | collective-permute-start | bytes 786440 | tf_op jit(solution)/shard_map/ppermute | solution.py:230
  48.7 7.2 %collective-permute-start.19 = (bf16[2,64,384]{2,1,0:T(8,128)(2,1)S(1)}, bf16[2,64,384]{2,1,0:T(8,128)(2,1)S(1)}, u32[]{:S(2)}, u32[]{:S(2)}) collective-permute-start(bf16[2,64,384]{2,1,0:T(8,128)(2,1)S(1)} %get-tuple-element.32), channel_id=1, source_target_pairs={{0,8},{1,9},{2,6},{3,7},{4,12},{5,13},{6,2},{7,3},{8,0},{9,1},{10,... | collective-permute-start | bytes 294920 | tf_op jit(solution)/shard_map/ppermute | solution.py:230
  53.4 5.0 %collective-permute-start.29 = (bf16[2,64,512]{2,1,0:T(8,128)(2,1)S(1)}, bf16[2,64,512]{2,1,0:T(8,128)(2,1)S(1)}, u32[]{:S(2)}, u32[]{:S(2)}) collective-permute-start(bf16[2,64,512]{2,1,0:T(8,128)(2,1)S(1)} %get-tuple-element.30), channel_id=1, source_target_pairs={{0,8},{1,9},{2,6},{3,7},{4,12},{5,13},{6,2},{7,3},{8,0},{9,1},{10,... | collective-permute-start | bytes 393224 | tf_op jit(solution)/shard_map/ppermute | solution.py:230
  55.6 43.8 %copy-start.2 = (bf16[256,128]{1,0:T(8,128)(2,1)S(1)}, bf16[256,128]{1,0:T(8,128)(2,1)}, u32[]{:S(2)}) copy-start(bf16[256,128]{1,0:T(8,128)(2,1)} %own_hbm.1) | copy-start | bytes 196612
  58.5 5.4 %collective-permute-start.30 = (bf16[1,64,512]{2,1,0:T(8,128)(2,1)S(1)}, bf16[1,64,512]{2,1,0:T(8,128)(2,1)S(1)}, u32[]{:S(2)}, u32[]{:S(2)}) collective-permute-start(bf16[1,64,512]{2,1,0:T(8,128)(2,1)S(1)} %fusion.9), channel_id=1, source_target_pairs={{0,16},{1,17},{2,18},{3,19},{4,20},{5,21},{6,22},{7,23},{8,24},{9,... | collective-permute-start | bytes 196616 | tf_op jit(solution)/shard_map/ppermute | solution.py:230
  61.4 5.5 %collective-permute-start.20 = (bf16[1,64,384]{2,1,0:T(8,128)(2,1)S(1)}, bf16[1,64,384]{2,1,0:T(8,128)(2,1)S(1)}, u32[]{:S(2)}, u32[]{:S(2)}) collective-permute-start(bf16[1,64,384]{2,1,0:T(8,128)(2,1)S(1)} %fusion.20), channel_id=1, source_target_pairs={{0,16},{1,17},{2,18},{3,19},{4,20},{5,21},{6,22},{7,23},{8,24},{9,... | collective-permute-start | bytes 147464 | tf_op jit(solution)/shard_map/ppermute | solution.py:230
  64.0 5.3 %collective-permute-start.31 = (bf16[1,64,512]{2,1,0:T(8,128)(2,1)S(1)}, bf16[1,64,512]{2,1,0:T(8,128)(2,1)S(1)}, u32[]{:S(2)}, u32[]{:S(2)}) collective-permute-start(bf16[1,64,512]{2,1,0:T(8,128)(2,1)S(1)} %get-tuple-element.21), channel_id=1, source_target_pairs={{0,16},{1,17},{2,18},{3,19},{4,20},{5,21},{6,22},{7,23},{8,24},{9,... | collective-permute-start | bytes 196616 | tf_op jit(solution)/shard_map/ppermute | solution.py:250
  67.0 7.0 %collective-permute-start.21 = (bf16[1,64,384]{2,1,0:T(8,128)(2,1)S(1)}, bf16[1,64,384]{2,1,0:T(8,128)(2,1)S(1)}, u32[]{:S(2)}, u32[]{:S(2)}) collective-permute-start(bf16[1,64,384]{2,1,0:T(8,128)(2,1)S(1)} %get-tuple-element.23), channel_id=1, source_target_pairs={{0,16},{1,17},{2,18},{3,19},{4,20},{5,21},{6,22},{7,23},{8,24},{9,... | collective-permute-start | bytes 147464 | tf_op jit(solution)/shard_map/ppermute | solution.py:250
  69.3 7.9 %collective-permute-start.32 = (bf16[2,64,512]{2,1,0:T(8,128)(2,1)S(1)}, bf16[2,64,512]{2,1,0:T(8,128)(2,1)S(1)}, u32[]{:S(2)}, u32[]{:S(2)}) collective-permute-start(bf16[2,64,512]{2,1,0:T(8,128)(2,1)S(1)} %pad_maximum_fusion.6), channel_id=1, source_target_pairs={{0,8},{1,9},{2,6},{3,7},{4,12},{5,13},{6,2},{7,3},{8,0},{9,1},{10,... | collective-permute-start | bytes 393224 | tf_op jit(solution)/shard_map/ppermute | solution.py:250
  73.7 4.6 %collective-permute-start.35 = (f32[64,384]{1,0:T(8,128)S(1)}, f32[64,384]{1,0:T(8,128)S(1)}, u32[]{:S(2)}, u32[]{:S(2)}) collective-permute-start(f32[64,384]{1,0:T(8,128)S(1)} %get-tuple-element.24), channel_id=1, source_target_pairs={{0,1},{1,0},{2,3},{3,2},{4,5},{5,4},{6,7},{7,6},{8,9},{9,8},{10,11... | collective-permute-start | bytes 294920 | tf_op jit(solution)/shard_map/ppermute | solution.py:244
  74.0 5.7 %collective-permute-start.22 = (bf16[2,64,384]{2,1,0:T(8,128)(2,1)S(1)}, bf16[2,64,384]{2,1,0:T(8,128)(2,1)S(1)}, u32[]{:S(2)}, u32[]{:S(2)}) collective-permute-start(bf16[2,64,384]{2,1,0:T(8,128)(2,1)S(1)} %pad_maximum_fusion.7), channel_id=1, source_target_pairs={{0,8},{1,9},{2,6},{3,7},{4,12},{5,13},{6,2},{7,3},{8,0},{9,1},{10,... | collective-permute-start | bytes 294920 | tf_op jit(solution)/shard_map/ppermute | solution.py:250
  77.2 8.6 %collective-permute-start.33 = (bf16[4,64,512]{2,1,0:T(8,128)(2,1)S(1)}, bf16[4,64,512]{2,1,0:T(8,128)(2,1)S(1)}, u32[]{:S(2)}, u32[]{:S(2)}) collective-permute-start(bf16[4,64,512]{2,1,0:T(8,128)(2,1)S(1)} %pad_maximum_fusion.2), channel_id=1, source_target_pairs={{0,1},{1,0},{2,10},{3,11},{4,5},{5,4},{6,14},{7,15},{8,9},{9,8},{1... | collective-permute-start | bytes 786440 | tf_op jit(solution)/shard_map/ppermute | solution.py:250
  79.8 10.3 %collective-permute-start.23 = (bf16[4,64,384]{2,1,0:T(8,128)(2,1)S(1)}, bf16[4,64,384]{2,1,0:T(8,128)(2,1)S(1)}, u32[]{:S(2)}, u32[]{:S(2)}) collective-permute-start(bf16[4,64,384]{2,1,0:T(8,128)(2,1)S(1)} %pad_maximum_fusion.4), channel_id=1, source_target_pairs={{0,1},{1,0},{2,10},{3,11},{4,5},{5,4},{6,14},{7,15},{8,9},{9,8},{1... | collective-permute-start | bytes 589832 | tf_op jit(solution)/shard_map/ppermute | solution.py:250
  81.6 11.3 %collective-permute-start.36 = (f32[64,512]{1,0:T(8,128)S(1)}, f32[64,512]{1,0:T(8,128)S(1)}, u32[]{:S(2)}, u32[]{:S(2)}) collective-permute-start(f32[64,512]{1,0:T(8,128)S(1)} %get-tuple-element.22), channel_id=1, source_target_pairs={{0,1},{1,0},{2,3},{3,2},{4,5},{5,4},{6,7},{7,6},{8,9},{9,8},{10,11... | collective-permute-start | bytes 393224 | tf_op jit(solution)/shard_map/ppermute | solution.py:244
  85.9 9.2 %collective-permute-start.34 = (bf16[8,64,512]{2,1,0:T(8,128)(2,1)S(1)}, bf16[8,64,512]{2,1,0:T(8,128)(2,1)S(1)}, u32[]{:S(2)}, u32[]{:S(2)}) collective-permute-start(bf16[8,64,512]{2,1,0:T(8,128)(2,1)S(1)} %pad_maximum_fusion.refs_4_), channel_id=1, source_target_pairs={{0,4},{1,5},{2,3},{3,2},{4,0},{5,1},{6,7},{7,6},{8,12},{9,13},{10,... | collective-permute-start | bytes 1572872 | tf_op jit(solution)/shard_map/ppermute | solution.py:260
  90.1 9.2 %collective-permute-start.24 = (bf16[8,64,384]{2,1,0:T(8,128)(2,1)S(1)}, bf16[8,64,384]{2,1,0:T(8,128)(2,1)S(1)}, u32[]{:S(2)}, u32[]{:S(2)}) collective-permute-start(bf16[8,64,384]{2,1,0:T(8,128)(2,1)S(1)} %pad_maximum_fusion.1.refs_0_), channel_id=1, source_target_pairs={{0,4},{1,5},{2,3},{3,2},{4,0},{5,1},{6,7},{7,6},{8,12},{9,13},{10,... | collective-permute-start | bytes 1179656 | tf_op jit(solution)/shard_map/ppermute | solution.py:260
  94.0 7.0 %collective-permute-start.37 = (bf16[8,64,512]{2,1,0:T(8,128)(2,1)S(1)}, bf16[8,64,512]{2,1,0:T(8,128)(2,1)S(1)}, u32[]{:S(2)}, u32[]{:S(2)}) collective-permute-start(bf16[8,64,512]{2,1,0:T(8,128)(2,1)S(1)} %pad_maximum_fusion.refs_4_), channel_id=1, source_target_pairs={{0,2},{2,0},{4,6},{6,4},{8,10},{10,8},{12,14},{14,12},{16,18},{18,... | collective-permute-start | bytes 1572872 | tf_op jit(solution)/shard_map/ppermute | solution.py:263
  95.1 5.9 %collective-permute-start.38 = (bf16[8,64,512]{2,1,0:T(8,128)(2,1)S(1)}, bf16[8,64,512]{2,1,0:T(8,128)(2,1)S(1)}, u32[]{:S(2)}, u32[]{:S(2)}) collective-permute-start(bf16[8,64,512]{2,1,0:T(8,128)(2,1)S(1)} %collective-permute-done.34.refs_5_), channel_id=1, source_target_pairs={{0,2},{2,0},{4,6},{6,4},{8,10},{10,8},{12,14},{14,12},{16,18},{18,... | collective-permute-start | bytes 1572872 | tf_op jit(solution)/shard_map/ppermute | solution.py:263
  95.2 4.4 %collective-permute-start.25 = (bf16[8,64,384]{2,1,0:T(8,128)(2,1)S(1)}, bf16[8,64,384]{2,1,0:T(8,128)(2,1)S(1)}, u32[]{:S(2)}, u32[]{:S(2)}) collective-permute-start(bf16[8,64,384]{2,1,0:T(8,128)(2,1)S(1)} %pad_maximum_fusion.1.refs_0_), channel_id=1, source_target_pairs={{0,2},{2,0},{4,6},{6,4},{8,10},{10,8},{12,14},{14,12},{16,18},{18,... | collective-permute-start | bytes 1179656 | tf_op jit(solution)/shard_map/ppermute | solution.py:263
  99.4 1.7 %collective-permute-start.26 = (bf16[8,64,384]{2,1,0:T(8,128)(2,1)S(1)}, bf16[8,64,384]{2,1,0:T(8,128)(2,1)S(1)}, u32[]{:S(2)}, u32[]{:S(2)}) collective-permute-start(bf16[8,64,384]{2,1,0:T(8,128)(2,1)S(1)} %collective-permute-done.24.refs_1_), channel_id=1, source_target_pairs={{0,2},{2,0},{4,6},{6,4},{8,10},{10,8},{12,14},{14,12},{16,18},{18,... | collective-permute-start | bytes 1179656 | tf_op jit(solution)/shard_map/ppermute | solution.py:263

commit v2 on v1

v2 whole, which is shorter than its diff:
```python
import functools

import jax
import jax.numpy as jnp
from jax import lax
from jax.experimental import pallas as pl
from jax.experimental.pallas import tpu as pltpu
from jax.sharding import PartitionSpec as P

STEP = 10
ORDERS = (("zyxw", "zxyw"), ("xzyw", "yxzw"))
EXPAND = (1, 0)
AXES = ("fsdp", "dp")


def bits_of(size):
    return size.bit_length() - 1


def orders(n, m, chunk):
    f = [("f", k) for k in range(1, bits_of(n))]
    d = [("d", k) for k in range(bits_of(m))]
    bits = dict(x=f[:1], y=d[:1], z=f[1:2], w=f[2:])
    return tuple([bit for axis in order for bit in bits[axis]] + d[1:] for order in ORDERS[chunk])


def gather_plan(n):
    plan = []
    for block in sorted(range(1, n // 2), key=lambda b: (b.bit_count(), -b)):
        low = block & -block
        via = low if block.bit_count() < 3 else (block ^ low) & -(block ^ low)
        plan.append((block, block ^ via, bits_of(via) + 1))
    return plan


def chunks_of(width):
    tiles = width // 128
    if width % 128 or tiles < 2:
        return ((0, width),)
    cut = (tiles - 1) // 2 * 128
    return ((0, cut), (cut, width))


def pairs(n, m, both):
    out = []
    for i in range(n):
        for y in range(m):
            kind, k = both[i & 1]
            j, w = (i ^ (1 << k), y) if kind == "f" else (i, y ^ (1 << k))
            out.append((i * m + y, j * m + w))
    return out


def slot_of(order, block, part):
    t = 0
    for kind, k in order:
        t = 2 * t + ((block >> (k - 1)) & 1 if kind == "f" else (part >> k) & 1)
    return t


def state_kernel(moment_ref, second_ref, *refs):
    fulls, (new_m_ref, new_s_ref) = refs[:-2], refs[-2:]
    full = jnp.concatenate([full[...] for full in fulls], axis=1).T
    new_m_ref[...] = 0.9 * moment_ref[...] + 0.1 * full
    new_s_ref[...] = 0.999 * second_ref[...] + 0.001 * (full * full)


def start_columns(n, width, chunk, g_hbm, g_ref, sems):
    i = lax.axis_index("fsdp")
    loads = []
    for block in range(n // 2):
        at = columns_of(width, chunk, block ^ (i >> 1), i & 1)
        loads.append(pltpu.make_async_copy(g_hbm.at[:, at], g_ref.at[block], sems.at[block]))
        loads[-1].start()
    return loads


def columns_of(width, chunk, block, core):
    if width % 128:
        return pl.ds(pl.multiple_of(block * 2 * width, 128), 2 * width)
    first, last = chunks_of(width)[chunk]
    return pl.ds(pl.multiple_of((2 * block + core) * width + first, 128), last - first)


def multiply(n, m, width, chunk, left_ref, loads, g_ref, h_ref, keep_ref, send_ref):
    i = lax.axis_index("fsdp")
    core, own = i & 1, i >> 1
    half, size, _ = keep_ref.shape

    def columns(c):
        for block in range(n // 2):
            at = columns_of(width, chunk, block ^ own, c)
            acc = jnp.dot(left_ref[1], h_ref[:, at], preferred_element_type=jnp.float32)
            loads[block].wait()
            acc += jnp.dot(left_ref[0], g_ref[block], preferred_element_type=jnp.float32)
            if width % 128:
                acc = acc[:, c * width : (c + 1) * width]
            for part in range(m):
                slot = slot_of(orders(n, m, chunk)[c], block, part)
                piece = acc[part * size : (part + 1) * size]
                if slot < half:
                    keep_ref[slot] = piece
                else:
                    send_ref[slot - half] = piece.astype(jnp.bfloat16)

    for c in range(2):
        pl.when(core == c)(functools.partial(columns, c))


def first_kernel(n, m, width, a_hbm, own_hbm, g_hbm, b_ref, *refs):
    blocks, h_ref, (keep_ref, send_ref, left_ref, a_ref, own_ref, g_ref, sems) = refs[: n - 1], refs[n - 1], refs[n:]
    i, mine = lax.axis_index("fsdp"), lax.axis_index("dp")
    core, own = i & 1, i >> 1
    depth, rank = own_ref.shape
    rows = b_ref.shape[0]
    size = rank // m
    copies = [
        pltpu.make_async_copy(own_hbm, own_ref, sems.at[n // 2]),
        pltpu.make_async_copy(a_hbm, a_ref, sems.at[n // 2 + 1]),
    ]
    for copy in copies:
        copy.start()
    loads = start_columns(n, width, 0, g_hbm, g_ref, sems)
    for place, x_ref in ((1, b_ref), (0, a_ref)):
        total = jnp.zeros((rows, rank), jnp.float32)
        if x_ref is a_ref:
            copies[1].wait()
        for k in (*range(1, n), 0):
            if k == 0 and x_ref is b_ref:
                copies[0].wait()
            w_ref = blocks[k - 1] if k else own_ref
            start = pl.multiple_of((2 * (own ^ (k >> 1)) + (core ^ (k & 1))) * depth, depth)
            total += jnp.dot(x_ref[:, pl.ds(start, depth)], w_ref[...], preferred_element_type=jnp.float32)
        total = total.T
        for k in range(bits_of(m)):
            swapped = [total[(p ^ (1 << k)) * size :][:size] for p in range(m)]
            total = jnp.where(((mine >> k) & 1) == 0, total, jnp.concatenate(swapped, axis=0))
        left_ref[place] = total.astype(jnp.bfloat16)
    multiply(n, m, width, 0, left_ref, loads, g_ref, h_ref, keep_ref, send_ref)


def next_kernel(n, m, width, chunk, g_hbm, h_ref, left_ref, keep_ref, send_ref, g_ref, sems):
    loads = start_columns(n, width, chunk, g_hbm, g_ref, sems)
    multiply(n, m, width, chunk, left_ref, loads, g_ref, h_ref, keep_ref, send_ref)


def expand_kernel(n, m, width, chunk, p_ref, *refs):
    parts, (o_ref, stage_ref, sems) = refs[:4], refs[-3:]
    i = lax.axis_index("fsdp")
    core, own = i & 1, i >> 1
    half = parts[0].shape[0]

    def rows(c):
        copies = []
        for block in range(n // 2):
            pair = []
            for owner in range(2):
                mine = parts[:2] if owner == c else parts[2:]
                slots = [slot_of(orders(n, m, chunk)[owner], block, part) for part in range(m)]
                right = jnp.concatenate([mine[t // half][t % half] for t in slots], axis=0)
                out = jnp.dot(p_ref[...], right, preferred_element_type=jnp.float32)
                pair.append(out.astype(o_ref.dtype))
            whole = [jnp.concatenate(pair, axis=1)] if width % 128 else pair
            for owner, out in enumerate(whole):
                k = block * len(whole) + owner
                stage_ref[k] = out
                at = columns_of(width, chunk, block ^ own, owner)
                copies.append(pltpu.make_async_copy(stage_ref.at[k], o_ref.at[:, at], sems.at[k]))
                copies[-1].start()
        for copy in copies:
            copy.wait()

    for c in range(2):
        pl.when(core == c)(functools.partial(rows, c))


def relative_ranks(x, y, m):
    size = x.shape[1] // m
    for k in range(bits_of(m)):
        swapped = jnp.concatenate([x[:, (p ^ (1 << k)) * size :][:, :size] for p in range(m)], axis=1)
        x = jnp.where(((y >> k) & 1) == 0, x, swapped)
    return x


def placed(space, *arrays):
    return [pltpu.with_memory_space_constraint(x, space) for x in arrays]


VMEM = pl.BlockSpec(memory_space=pltpu.VMEM)
HBM = pl.BlockSpec(memory_space=pltpu.HBM)


def local(n, m, inputs, grad_out, projection, moment, second):
    y = lax.axis_index("dp")
    width, rank = moment.shape
    rows = inputs.shape[0]
    size = rank // m
    partner = [(k, k ^ 1) for k in range(n)]

    inputs_too = lax.ppermute(inputs, "fsdp", partner)
    grad_too = lax.ppermute(grad_out, "fsdp", partner)

    held = {0: projection}
    held_too = {0: lax.ppermute(projection, "fsdp", partner)}
    for block, source, k in gather_plan(n):
        held[block] = lax.ppermute(held[source], "fsdp", [(w, w ^ (1 << k)) for w in range(n)])
        held_too[block] = lax.ppermute(held[block], "fsdp", partner)
    blocks = [x for block in range(n // 2) for x in (held[block], held_too[block])]

    half = n // 2 * m // 2
    sums, left = [], None
    for chunk, (start, stop) in enumerate(chunks_of(width)):
        span = stop - start if width % 128 == 0 else 2 * width
        shapes = [
            pltpu.VMEM((half, size, stop - start), jnp.float32),
            pltpu.VMEM((half, size, stop - start), jnp.bfloat16),
        ]
        held_columns = pltpu.VMEM((n // 2, rows, span), grad_out.dtype)
        params = pltpu.CompilerParams(vmem_limit_bytes=16 << 20)
        if left is None:
            *pair, left = pl.pallas_call(
                functools.partial(first_kernel, n, m, width),
                in_specs=[HBM] * 3 + [VMEM] * (n + 1),
                out_specs=[VMEM] * 3,
                out_shape=shapes + [pltpu.VMEM((2, rank, rows), jnp.bfloat16)],
                scratch_shapes=[
                    pltpu.VMEM(inputs.shape, inputs.dtype),
                    pltpu.VMEM(projection.shape, projection.dtype),
                    held_columns,
                    pltpu.SemaphoreType.DMA((n // 2 + 2,)),
                ],
                compiler_params=params,
                name="project",
            )(
                *placed(pltpu.HBM, inputs, projection, grad_out),
                *placed(pltpu.VMEM, inputs_too, *blocks[1:], grad_too),
            )
        else:
            pair = pl.pallas_call(
                functools.partial(next_kernel, n, m, width, chunk),
                in_specs=[HBM] + [VMEM] * 2,
                out_specs=[VMEM] * 2,
                out_shape=shapes,
                scratch_shapes=[held_columns, pltpu.SemaphoreType.DMA((n // 2,))],
                compiler_params=params,
                name="multiply",
            )(*placed(pltpu.HBM, grad_out), *placed(pltpu.VMEM, grad_too, left))
        sums += pair

    moment_t = lax.dynamic_slice_in_dim(moment.T, y * size, size)
    second_t = lax.dynamic_slice_in_dim(second.T, y * size, size)
    first_fix = 1.0 - 0.9**STEP
    second_fix = 1.0 - 0.999**STEP
    parts, fulls = [], []
    for chunk, (start, stop) in enumerate(chunks_of(width)):
        steps = list(zip(*orders(n, m, chunk)))
        keep, send = sums[2 * chunk : 2 * chunk + 2]
        for s, both in enumerate(steps):
            got = lax.ppermute(send, AXES, pairs(n, m, both)).astype(jnp.float32)
            if s + 1 < len(steps):
                cut = keep.shape[0] // 2
                send = (keep[cut:] + got[cut:]).astype(jnp.bfloat16)
                keep = keep[:cut] + got[:cut]
            else:
                low_rank = (keep + got)[0]

        new_m = 0.9 * moment_t[:, start:stop] + 0.1 * low_rank
        new_s = 0.999 * second_t[:, start:stop] + 0.001 * (low_rank * low_rank)
        normalized = (new_m / first_fix / (jnp.sqrt(new_s / second_fix) + 1e-08)).astype(jnp.bfloat16)

        full = low_rank
        for k in range(bits_of(m)):
            got = lax.ppermute(full, "dp", [(w, w ^ (1 << k)) for w in range(m)])
            first = ((y >> k) & 1) == 0
            full = jnp.concatenate([jnp.where(first, full, got), jnp.where(first, got, full)], axis=0)

        held = normalized[None]
        for both in steps[:0:-1]:
            got = lax.ppermute(held, AXES, pairs(n, m, both))
            held = jnp.concatenate([held, got], axis=0)
        fulls.append(full)
        if stop == width:
            new_moment, new_second = pl.pallas_call(
                state_kernel,
                out_shape=[jax.ShapeDtypeStruct(moment.shape, jnp.float32)] * 2,
                compiler_params=pltpu.CompilerParams(vmem_limit_bytes=16 << 20),
                name="state",
            )(moment, second, *fulls)
        rest = lax.ppermute(held, AXES, pairs(n, m, steps[0]))
        if stop == width:
            rest, new_moment, new_second = lax.optimization_barrier((rest, new_moment, new_second))
        parts.append([held, rest, lax.ppermute(held, "fsdp", partner), lax.ppermute(rest, "fsdp", partner)])

    copies = n if width % 128 == 0 else n // 2
    relative = relative_ranks(projection, y, m)
    update = []
    for chunk in EXPAND[-len(parts) :]:
        start, stop = chunks_of(width)[chunk]
        update = [
            pl.pallas_call(
                functools.partial(expand_kernel, n, m, width, chunk),
                in_specs=[VMEM] * 5 + [HBM] * len(update),
                out_specs=HBM,
                out_shape=jax.ShapeDtypeStruct((projection.shape[0], n * width), jnp.bfloat16),
                input_output_aliases={5: 0} if update else {},
                scratch_shapes=[
                    pltpu.VMEM((copies, projection.shape[0], n * (stop - start) // copies), jnp.bfloat16),
                    pltpu.SemaphoreType.DMA((copies,)),
                ],
                compiler_params=pltpu.CompilerParams(vmem_limit_bytes=16 << 20),
                name="expand",
            )(*placed(pltpu.VMEM, relative, *parts[chunk]), *update)
        ]
    return (*update, new_moment, new_second)


def solution(mesh):
    in_specs = (
        P(AXES, None),
        P(AXES, None),
        P("fsdp", None),
        P("fsdp", None),
        P("fsdp", None),
    )
    out_specs = (P("fsdp", None), P("fsdp", None), P("fsdp", None))

    def body(*args):
        return local(mesh.shape["fsdp"], mesh.shape["dp"], *args)

    return jax.shard_map(body, mesh=mesh, in_specs=in_specs, out_specs=out_specs, check_vma=False)
```

time: 105 us -> 104 us (level)
  starting transfers between devices: 43.4 us -> 39.4 us
  Pallas kernels: 9.66 us -> 12.9 us
    ppermute x6, starting transfers between devices: 11.3 us -> 4.8 us  [local(): got = lax.ppermute(held, AXES, pairs(n, m, both))]
    ppermute x2, starting transfers between devices: 0.47 us -> 4.02 us  [local(): got = lax.ppermute(full, 'dp', [(w, w ^ 1 << k) for w in range(m)])]
    pallas_call x2 -> x4, Pallas kernels: 8.54 us -> 11.8 us  [the longest x1 4.53 us: local(): pl.pallas_call(functools.partial(first_kernel, n, m, width), in_specs=[HB...]
    ppermute x2, waiting for transfers between devices: 4.8 us -> 6.92 us  [local(): rest = lax.ppermute(held, AXES, pairs(n, m, steps[0]))]
    ppermute x6, waiting for transfers between devices: 12 us -> 10.2 us  [local(): got = lax.ppermute(held, AXES, pairs(n, m, both))]
    ppermute x2, waiting for transfers between devices: 3.05 us -> 1.98 us  [local(): got = lax.ppermute(full, 'dp', [(w, w ^ 1 << k) for w in range(m)])]
  transfers between devices with their start and end apart: 39 -> 39, of which waited for: 23 -> 19; matrix products, arithmetic and copies ran while one was open for 2% -> 2% of each run, Pallas kernels for 1% -> 6%
where the time goes in v2:
time: 104 us
  waiting for transfers between devices  48 us (46%)
  starting transfers between devices  39.4 us (38%)
  Pallas kernels  12.9 us (12%)
  other arithmetic  1.36 us (1%)
  between operations  1.11 us (1%)
    ppermute x8, waiting for transfers between devices, local(): got = lax.ppermute(send, AXES, pairs(n, m, both)).astype(jnp.float32)  17.8 us
    ppermute x7, starting transfers between devices, local(): lax.ppermute(held[source], 'fsdp', [(w, w ^ 1 << k) for w in range(n)])  15.3 us
    ppermute x8, starting transfers between devices, local(): got = lax.ppermute(send, AXES, pairs(n, m, both)).astype(jnp.float32)  11.8 us
    ppermute x6, waiting for transfers between devices, local(): got = lax.ppermute(held, AXES, pairs(n, m, both))  10.2 us
    ppermute x2, waiting for transfers between devices, local(): rest = lax.ppermute(held, AXES, pairs(n, m, steps[0]))  6.92 us
    ppermute x7, waiting for transfers between devices, local(): lax.ppermute(held[source], 'fsdp', [(w, w ^ 1 << k) for w in range(n)])  5.98 us
    ppermute x6, starting transfers between devices, local(): got = lax.ppermute(held, AXES, pairs(n, m, both))  4.8 us
    pallas_call x1, Pallas kernels, local(): pl.pallas_call(functools.partial(first_kernel, n, m, width), in_specs=[HB...  4.53 us
  transfers between devices with their start and end apart: 39, of which 19 were waited for; matrix products, arithmetic and copies ran while one was open for 2% of the time, Pallas kernels for 6%

profile of v2, /device:TPU:0, one launch (start us, length us, event | category | flops | bytes accessed | tf_op | source)
XLA Modules:
  0.0 103.6 jit_solution(6076119927156144439)
XLA Ops:
  0.6 0.6 collective-permute-start.16
  1.3 2.9 %collective-permute-start.2 = (bf16[256,128]{1,0:T(8,128)(2,1)}, bf16[256,128]{1,0:T(8,128)(2,1)S(1)}, u32[]{:S(2)}, u32[]{:S(2)}) collective-permute-start(bf16[256,128]{1,0:T(8,128)(2,1)} %own_hbm.1), channel_id=1, source_target_pairs={{0,4},{2,6},{4,0},{6,2},{8,12},{10,14},{12,8},{14,10},{16,20},{18,... | collective-permute-start | bytes 196616 | tf_op jit(solution)/shard_map/ppermute | solution.py:206
  4.2 1.6 %collective-permute-start.4 = (bf16[256,128]{1,0:T(8,128)(2,1)}, bf16[256,128]{1,0:T(8,128)(2,1)S(1)}, u32[]{:S(2)}, u32[]{:S(2)}) collective-permute-start(bf16[256,128]{1,0:T(8,128)(2,1)} %own_hbm.1), channel_id=1, source_target_pairs={{0,8},{2,10},{4,12},{6,14},{8,0},{10,2},{12,4},{14,6},{16,24},{18,... | collective-permute-start | bytes 196616 | tf_op jit(solution)/shard_map/ppermute | solution.py:206
  5.8 1.0 collective-permute-done.2.refs_1_
  6.7 3.0 %collective-permute-start.8 = (bf16[256,128]{1,0:T(8,128)(2,1)}, bf16[256,128]{1,0:T(8,128)(2,1)S(1)}, u32[]{:S(2)}, u32[]{:S(2)}) collective-permute-start(bf16[256,128]{1,0:T(8,128)(2,1)} %own_hbm.1), channel_id=1, source_target_pairs={{0,16},{2,18},{4,20},{6,22},{8,24},{10,26},{12,28},{14,30},{16,0},... | collective-permute-start | bytes 196616 | tf_op jit(solution)/shard_map/ppermute | solution.py:206
  9.7 2.7 %collective-permute-done.1.refs_0_ = bf16[256,128]{1,0:T(8,128)(2,1)S(1)} collective-permute-done((bf16[256,128]{1,0:T(8,128)(2,1)}, bf16[256,128]{1,0:T(8,128)(2,1)S(1)}, u32[]{:S(2)}, u32[]{:S(2)}) %collective-permute-start.1) | collective-permute-done | bytes 65568 | tf_op jit(solution)/shard_map/ppermute | solution.py:204
  12.4 0.4 collective-permute-start.3
  12.8 2.6 %collective-permute-start.6 = (bf16[256,128]{1,0:T(8,128)(2,1)S(1)}, bf16[256,128]{1,0:T(8,128)(2,1)S(1)}, u32[]{:S(2)}, u32[]{:S(2)}) collective-permute-start(bf16[256,128]{1,0:T(8,128)(2,1)S(1)} %collective-permute-done.4.refs_3_), channel_id=1, source_target_pairs={{0,4},{2,6},{4,0},{6,2},{8,12},{10,14},{12,8},{14,10},{16,20},{18,... | collective-permute-start | bytes 196616 | tf_op jit(solution)/shard_map/ppermute | solution.py:206
  15.5 1.6 %collective-permute-start.12 = (bf16[256,128]{1,0:T(8,128)(2,1)S(1)}, bf16[256,128]{1,0:T(8,128)(2,1)S(1)}, u32[]{:S(2)}, u32[]{:S(2)}) collective-permute-start(bf16[256,128]{1,0:T(8,128)(2,1)S(1)} %collective-permute-done.8.refs_7_), channel_id=1, source_target_pairs={{0,8},{2,10},{4,12},{6,14},{8,0},{10,2},{12,4},{14,6},{16,24},{18,... | collective-permute-start | bytes 196616 | tf_op jit(solution)/shard_map/ppermute | solution.py:206
  17.1 0.9 collective-permute-done.6.refs_5_
  18.0 1.7 %collective-permute-start.10 = (bf16[256,128]{1,0:T(8,128)(2,1)S(1)}, bf16[256,128]{1,0:T(8,128)(2,1)S(1)}, u32[]{:S(2)}, u32[]{:S(2)}) collective-permute-start(bf16[256,128]{1,0:T(8,128)(2,1)S(1)} %collective-permute-done.8.refs_7_), channel_id=1, source_target_pairs={{0,4},{2,6},{4,0},{6,2},{8,12},{10,14},{12,8},{14,10},{16,20},{18,... | collective-permute-start | bytes 196616 | tf_op jit(solution)/shard_map/ppermute | solution.py:206
  19.9 0.4 collective-permute-start.7
  20.3 2.0 %collective-permute-done.10.refs_9_ = bf16[256,128]{1,0:T(8,128)(2,1)S(1)} collective-permute-done((bf16[256,128]{1,0:T(8,128)(2,1)S(1)}, bf16[256,128]{1,0:T(8,128)(2,1)S(1)}, u32[]{:S(2)}, u32[]{:S(2)}) %collective-permute-start.10) | collective-permute-done | bytes 65568 | tf_op jit(solution)/shard_map/ppermute | solution.py:206
  22.3 1.8 %collective-permute-start.14 = (bf16[256,128]{1,0:T(8,128)(2,1)S(1)}, bf16[256,128]{1,0:T(8,128)(2,1)S(1)}, u32[]{:S(2)}, u32[]{:S(2)}) collective-permute-start(bf16[256,128]{1,0:T(8,128)(2,1)S(1)} %collective-permute-done.10.refs_9_), channel_id=1, source_target_pairs={{0,8},{2,10},{4,12},{6,14},{8,0},{10,2},{12,4},{14,6},{16,24},{18,... | collective-permute-start | bytes 196616 | tf_op jit(solution)/shard_map/ppermute | solution.py:206
  24.1 0.5 collective-permute-start.13
  24.6 1.9 %collective-permute-done.14.refs_13_ = bf16[256,128]{1,0:T(8,128)(2,1)S(1)} collective-permute-done((bf16[256,128]{1,0:T(8,128)(2,1)S(1)}, bf16[256,128]{1,0:T(8,128)(2,1)S(1)}, u32[]{:S(2)}, u32[]{:S(2)}) %collective-permute-start.14) | collective-permute-done | bytes 65568 | tf_op jit(solution)/shard_map/ppermute | solution.py:206
  26.6 1.2 %collective-permute-done.15.refs_14_ = bf16[256,128]{1,0:T(8,128)(2,1)S(1)} collective-permute-done((bf16[256,128]{1,0:T(8,128)(2,1)S(1)}, bf16[256,128]{1,0:T(8,128)(2,1)S(1)}, u32[]{:S(2)}, u32[]{:S(2)}) %collective-permute-start.15) | collective-permute-done | bytes 65568 | tf_op jit(solution)/shard_map/ppermute | solution.py:207
  27.8 4.5 %project.1 = (f32[8,64,384]{2,1,0:T(8,128)S(1)}, bf16[8,64,384]{2,1,0:T(8,128)(2,1)S(1)}, bf16[2,128,192]{2,1,0:T(8,128)(2,1)S(1)}) custom-call(bf16[192,4096]{1,0:T(8,128)(2,1)} %a_hbm.1, bf16[256,128]{1,0:T(8,128)(2,1)} %own_hbm.1, bf16[192,14336]{1,0:T(8,128)(2,1)} %g_hbm.3, bf16[192,4096]{1,0:T(8,128)(2,1)S(1)} %collective-permute-done.b_ref, ...), custom_call_target="tpu_custom_call" | custom-call | tf_op jit(solution)/shard_map/project/pallas_call | solution.py:221
  32.4 1.9 %collective-permute-start.17 = (bf16[8,64,384]{2,1,0:T(8,128)(2,1)S(1)}, bf16[8,64,384]{2,1,0:T(8,128)(2,1)S(1)}, u32[]{:S(2)}, u32[]{:S(2)}) collective-permute-start(bf16[8,64,384]{2,1,0:T(8,128)(2,1)S(1)} %get-tuple-element.14), channel_id=1, source_target_pairs={{0,8},{1,9},{2,10},{3,11},{4,12},{5,13},{6,14},{7,15},{8,0},{9,1},... | collective-permute-start | bytes 1179656 | tf_op jit(solution)/shard_map/ppermute | solution.py:259
  34.2 2.9 %multiply.5 = (f32[8,64,512]{2,1,0:T(8,128)S(1)}, bf16[8,64,512]{2,1,0:T(8,128)(2,1)S(1)}) custom-call(bf16[192,14336]{1,0:T(8,128)(2,1)} %g_hbm.3, bf16[192,14336]{1,0:T(8,128)(2,1)S(1)} %collective-permute-done.16.refs_15_.h_ref, bf16[2,128,192]{2,1,0:T(8,128)(2,1)S(1)} %get-tuple-element.15.left_ref), custom_call_target="tpu_custom_call" | custom-call | tf_op jit(solution)/shard_map/multiply/pallas_call | solution.py:239
  37.1 1.6 %collective-permute-start.27 = (bf16[8,64,512]{2,1,0:T(8,128)(2,1)S(1)}, bf16[8,64,512]{2,1,0:T(8,128)(2,1)S(1)}, u32[]{:S(2)}, u32[]{:S(2)}) collective-permute-start(bf16[8,64,512]{2,1,0:T(8,128)(2,1)S(1)} %get-tuple-element.17), channel_id=1, source_target_pairs={{0,4},{1,5},{2,3},{3,2},{4,0},{5,1},{6,7},{7,6},{8,12},{9,13},{10,... | collective-permute-start | bytes 1572872 | tf_op jit(solution)/shard_map/ppermute | solution.py:259
  38.7 5.0 %collective-permute-done.17 = bf16[8,64,384]{2,1,0:T(8,128)(2,1)S(1)} collective-permute-done((bf16[8,64,384]{2,1,0:T(8,128)(2,1)S(1)}, bf16[8,64,384]{2,1,0:T(8,128)(2,1)S(1)}, u32[]{:S(2)}, u32[]{:S(2)}) %collective-permute-start.17) | collective-permute-done | bytes 393248 | tf_op jit(solution)/shard_map/ppermute | solution.py:259
  43.8 1.8 %collective-permute-start.18 = (bf16[4,64,384]{2,1,0:T(8,128)(2,1)S(1)}, bf16[4,64,384]{2,1,0:T(8,128)(2,1)S(1)}, u32[]{:S(2)}, u32[]{:S(2)}) collective-permute-start(bf16[4,64,384]{2,1,0:T(8,128)(2,1)S(1)} %get-tuple-element.30), channel_id=1, source_target_pairs={{0,1},{1,0},{2,6},{3,7},{4,5},{5,4},{6,2},{7,3},{8,9},{9,8},{10,14... | collective-permute-start | bytes 589832 | tf_op jit(solution)/shard_map/ppermute | solution.py:259
  45.6 1.3 %collective-permute-done.27 = bf16[8,64,512]{2,1,0:T(8,128)(2,1)S(1)} collective-permute-done((bf16[8,64,512]{2,1,0:T(8,128)(2,1)S(1)}, bf16[8,64,512]{2,1,0:T(8,128)(2,1)S(1)}, u32[]{:S(2)}, u32[]{:S(2)}) %collective-permute-start.27) | collective-permute-done | bytes 524320 | tf_op jit(solution)/shard_map/ppermute | solution.py:259
  47.6 2.0 %collective-permute-done.18 = bf16[4,64,384]{2,1,0:T(8,128)(2,1)S(1)} collective-permute-done((bf16[4,64,384]{2,1,0:T(8,128)(2,1)S(1)}, bf16[4,64,384]{2,1,0:T(8,128)(2,1)S(1)}, u32[]{:S(2)}, u32[]{:S(2)}) %collective-permute-start.18) | collective-permute-done | bytes 196640 | tf_op jit(solution)/shard_map/ppermute | solution.py:259
  49.7 1.7 %collective-permute-start.19 = (bf16[2,64,384]{2,1,0:T(8,128)(2,1)S(1)}, bf16[2,64,384]{2,1,0:T(8,128)(2,1)S(1)}, u32[]{:S(2)}, u32[]{:S(2)}) collective-permute-start(bf16[2,64,384]{2,1,0:T(8,128)(2,1)S(1)} %get-tuple-element.34), channel_id=1, source_target_pairs={{0,4},{1,5},{2,3},{3,2},{4,0},{5,1},{6,7},{7,6},{8,12},{9,13},{10,... | collective-permute-start | bytes 294920 | tf_op jit(solution)/shard_map/ppermute | solution.py:259
  51.4 2.3 %collective-permute-done.28 = bf16[4,64,512]{2,1,0:T(8,128)(2,1)S(1)} collective-permute-done((bf16[4,64,512]{2,1,0:T(8,128)(2,1)S(1)}, bf16[4,64,512]{2,1,0:T(8,128)(2,1)S(1)}, u32[]{:S(2)}, u32[]{:S(2)}) %collective-permute-start.28) | collective-permute-done | bytes 262176 | tf_op jit(solution)/shard_map/ppermute | solution.py:259
  53.9 1.5 %collective-permute-start.29 = (bf16[2,64,512]{2,1,0:T(8,128)(2,1)S(1)}, bf16[2,64,512]{2,1,0:T(8,128)(2,1)S(1)}, u32[]{:S(2)}, u32[]{:S(2)}) collective-permute-start(bf16[2,64,512]{2,1,0:T(8,128)(2,1)S(1)} %get-tuple-element.32), channel_id=1, source_target_pairs={{0,1},{1,0},{2,10},{3,11},{4,5},{5,4},{6,14},{7,15},{8,9},{9,8},{1... | collective-permute-start | bytes 393224 | tf_op jit(solution)/shard_map/ppermute | solution.py:259
  56.1 2.8 %collective-permute-done.29 = bf16[2,64,512]{2,1,0:T(8,128)(2,1)S(1)} collective-permute-done((bf16[2,64,512]{2,1,0:T(8,128)(2,1)S(1)}, bf16[2,64,512]{2,1,0:T(8,128)(2,1)S(1)}, u32[]{:S(2)}, u32[]{:S(2)}) %collective-permute-start.29) | collective-permute-done | bytes 131104 | tf_op jit(solution)/shard_map/ppermute | solution.py:259
  59.0 2.6 %collective-permute-start.30 = (bf16[1,64,512]{2,1,0:T(8,128)(2,1)S(1)}, bf16[1,64,512]{2,1,0:T(8,128)(2,1)S(1)}, u32[]{:S(2)}, u32[]{:S(2)}) collective-permute-start(bf16[1,64,512]{2,1,0:T(8,128)(2,1)S(1)} %fusion.9), channel_id=1, source_target_pairs={{0,16},{1,17},{2,18},{3,19},{4,20},{5,21},{6,22},{7,23},{8,24},{9,... | collective-permute-start | bytes 196616 | tf_op jit(solution)/shard_map/ppermute | solution.py:259
  61.6 0.5 collective-permute-start.20
  62.0 4.4 %collective-permute-done.30 = bf16[1,64,512]{2,1,0:T(8,128)(2,1)S(1)} collective-permute-done((bf16[1,64,512]{2,1,0:T(8,128)(2,1)S(1)}, bf16[1,64,512]{2,1,0:T(8,128)(2,1)S(1)}, u32[]{:S(2)}, u32[]{:S(2)}) %collective-permute-start.30) | collective-permute-done | bytes 65568 | tf_op jit(solution)/shard_map/ppermute | solution.py:259
  66.6 1.1 %collective-permute-start.31 = (bf16[1,64,512]{2,1,0:T(8,128)(2,1)S(1)}, bf16[1,64,512]{2,1,0:T(8,128)(2,1)S(1)}, u32[]{:S(2)}, u32[]{:S(2)}) collective-permute-start(bf16[1,64,512]{2,1,0:T(8,128)(2,1)S(1)} %get-tuple-element.23), channel_id=1, source_target_pairs={{0,16},{1,17},{2,18},{3,19},{4,20},{5,21},{6,22},{7,23},{8,24},{9,... | collective-permute-start | bytes 196616 | tf_op jit(solution)/shard_map/ppermute | solution.py:279
  67.8 1.9 %collective-permute-start.21 = (bf16[1,64,384]{2,1,0:T(8,128)(2,1)S(1)}, bf16[1,64,384]{2,1,0:T(8,128)(2,1)S(1)}, u32[]{:S(2)}, u32[]{:S(2)}) collective-permute-start(bf16[1,64,384]{2,1,0:T(8,128)(2,1)S(1)} %get-tuple-element.25), channel_id=1, source_target_pairs={{0,16},{1,17},{2,18},{3,19},{4,20},{5,21},{6,22},{7,23},{8,24},{9,... | collective-permute-start | bytes 147464 | tf_op jit(solution)/shard_map/ppermute | solution.py:279
  69.7 2.6 %collective-permute-done.31 = bf16[1,64,512]{2,1,0:T(8,128)(2,1)S(1)} collective-permute-done((bf16[1,64,512]{2,1,0:T(8,128)(2,1)S(1)}, bf16[1,64,512]{2,1,0:T(8,128)(2,1)S(1)}, u32[]{:S(2)}, u32[]{:S(2)}) %collective-permute-start.31) | collective-permute-done | bytes 65568 | tf_op jit(solution)/shard_map/ppermute | solution.py:279
  72.4 2.0 %collective-permute-start.35 = (f32[64,384]{1,0:T(8,128)S(1)}, f32[64,384]{1,0:T(8,128)S(1)}, u32[]{:S(2)}, u32[]{:S(2)}) collective-permute-start(f32[64,384]{1,0:T(8,128)S(1)} %get-tuple-element.26), channel_id=1, source_target_pairs={{0,1},{1,0},{2,3},{3,2},{4,5},{5,4},{6,7},{7,6},{8,9},{9,8},{10,11... | collective-permute-start | bytes 294920 | tf_op jit(solution)/shard_map/ppermute | solution.py:273
  74.4 1.5 %collective-permute-start.22 = (bf16[2,64,384]{2,1,0:T(8,128)(2,1)S(1)}, bf16[2,64,384]{2,1,0:T(8,128)(2,1)S(1)}, u32[]{:S(2)}, u32[]{:S(2)}) collective-permute-start(bf16[2,64,384]{2,1,0:T(8,128)(2,1)S(1)} %pad_maximum_fusion.7), channel_id=1, source_target_pairs={{0,4},{1,5},{2,3},{3,2},{4,0},{5,1},{6,7},{7,6},{8,12},{9,13},{10,... | collective-permute-start | bytes 294920 | tf_op jit(solution)/shard_map/ppermute | solution.py:279
  76.0 2.6 %collective-permute-done.32 = bf16[2,64,512]{2,1,0:T(8,128)(2,1)S(1)} collective-permute-done((bf16[2,64,512]{2,1,0:T(8,128)(2,1)S(1)}, bf16[2,64,512]{2,1,0:T(8,128)(2,1)S(1)}, u32[]{:S(2)}, u32[]{:S(2)}) %collective-permute-start.32) | collective-permute-done | bytes 131104 | tf_op jit(solution)/shard_map/ppermute | solution.py:279
  78.7 2.0 %collective-permute-done.35 = f32[64,384]{1,0:T(8,128)S(1)} collective-permute-done((f32[64,384]{1,0:T(8,128)S(1)}, f32[64,384]{1,0:T(8,128)S(1)}, u32[]{:S(2)}, u32[]{:S(2)}) %collective-permute-start.35) | collective-permute-done | bytes 98336 | tf_op jit(solution)/shard_map/ppermute | solution.py:273
  80.8 2.0 %collective-permute-start.36 = (f32[64,512]{1,0:T(8,128)S(1)}, f32[64,512]{1,0:T(8,128)S(1)}, u32[]{:S(2)}, u32[]{:S(2)}) collective-permute-start(f32[64,512]{1,0:T(8,128)S(1)} %get-tuple-element.24), channel_id=1, source_target_pairs={{0,1},{1,0},{2,3},{3,2},{4,5},{5,4},{6,7},{7,6},{8,9},{9,8},{10,11... | collective-permute-start | bytes 393224 | tf_op jit(solution)/shard_map/ppermute | solution.py:273
  82.8 5.0 %collective-permute-done.33 = bf16[4,64,512]{2,1,0:T(8,128)(2,1)S(1)} collective-permute-done((bf16[4,64,512]{2,1,0:T(8,128)(2,1)S(1)}, bf16[4,64,512]{2,1,0:T(8,128)(2,1)S(1)}, u32[]{:S(2)}, u32[]{:S(2)}) %collective-permute-start.33) | collective-permute-done | bytes 262176 | tf_op jit(solution)/shard_map/ppermute | solution.py:279
  87.9 1.0 collective-permute-start.34
  89.1 1.1 %state.1 = (f32[896,128]{1,0:T(8,128)}, f32[896,128]{1,0:T(8,128)}) custom-call(f32[896,128]{1,0:T(8,128)S(1)} %copy-done.1, f32[896,128]{1,0:T(8,128)S(1)} %copy-done, f32[128,384]{1,0:T(8,128)S(1)} %pad_maximum_fusion.5.refs_0_, f32[128,512]{1,0:T(8,128)S(1)} %pad_maximum_fusion.3.refs_1_), custom_call_target="tpu_custom_call" | custom-call | tf_op jit(solution)/shard_map/state/pallas_call | solution.py:283
  90.2 6.9 %collective-permute-done.34.refs_1_ = bf16[8,64,512]{2,1,0:T(8,128)(2,1)S(1)} collective-permute-done((bf16[8,64,512]{2,1,0:T(8,128)(2,1)S(1)}, bf16[8,64,512]{2,1,0:T(8,128)(2,1)S(1)}, u32[]{:S(2)}, u32[]{:S(2)}) %collective-permute-start.34) | collective-permute-done | bytes 524320 | tf_op jit(solution)/shard_map/ppermute | solution.py:289
  97.1 0.5 collective-permute-start.25
  97.9 1.2 %collective-permute-done.38.refs_3_ = bf16[8,64,512]{2,1,0:T(8,128)(2,1)S(1)} collective-permute-done((bf16[8,64,512]{2,1,0:T(8,128)(2,1)S(1)}, bf16[8,64,512]{2,1,0:T(8,128)(2,1)S(1)}, u32[]{:S(2)}, u32[]{:S(2)}) %collective-permute-start.38) | collective-permute-done | bytes 524320 | tf_op jit(solution)/shard_map/ppermute | solution.py:292
  99.0 2.4 %expand.2.refs_4_ = bf16[256,14336]{1,0:T(8,128)(2,1)} custom-call(bf16[256,128]{1,0:T(8,128)(2,1)S(1)} %maximum_select_fusion.p_ref, bf16[8,64,512]{2,1,0:T(8,128)(2,1)S(1)} %pad_maximum_fusion.refs_0_, bf16[8,64,512]{2,1,0:T(8,128)(2,1)S(1)} %collective-permute-done.34.refs_1_, bf16[8,64,512]{2,1,0:T(8,128)(2,1)S(1)} %collective-permute-done.37.refs_2_, ...), custom_call_target="tpu_custom_call" | custom-call | tf_op jit(solution)/shard_map/expand/pallas_call | solution.py:300
  101.4 2.0 %expand.3 = bf16[256,14336]{1,0:T(8,128)(2,1)} custom-call(bf16[256,128]{1,0:T(8,128)(2,1)S(1)} %maximum_select_fusion.p_ref, bf16[8,64,384]{2,1,0:T(8,128)(2,1)S(1)} %pad_maximum_fusion.1.refs_0_, bf16[8,64,384]{2,1,0:T(8,128)(2,1)S(1)} %collective-permute-done.24.refs_1_, ...), custom_call_target="tpu_custom_call", output_to_operand_aliasing={{}: (5, {})} | custom-call | tf_op jit(solution)/shard_map/expand/pallas_call | solution.py:300
  (70 shorter events, 3.1 us)
Async XLA Ops:
  0.6 27.2 %collective-permute-start.16 = (bf16[192,14336]{1,0:T(8,128)(2,1)}, bf16[192,14336]{1,0:T(8,128)(2,1)S(1)}, u32[]{:S(2)}, u32[]{:S(2)}) collective-permute-start(bf16[192,14336]{1,0:T(8,128)(2,1)} %g_hbm.3), channel_id=1, source_target_pairs={{0,2},{2,0},{4,6},{6,4},{8,10},{10,8},{12,14},{14,12},{16,18},{18,... | collective-permute-start | bytes 16515080 | tf_op jit(solution)/shard_map/ppermute | solution.py:201
  1.2 26.6 %collective-permute-start = (bf16[192,4096]{1,0:T(8,128)(2,1)}, bf16[192,4096]{1,0:T(8,128)(2,1)S(1)}, u32[]{:S(2)}, u32[]{:S(2)}) collective-permute-start(bf16[192,4096]{1,0:T(8,128)(2,1)} %a_hbm.1), channel_id=1, source_target_pairs={{0,2},{2,0},{4,6},{6,4},{8,10},{10,8},{12,14},{14,12},{16,18},{18,... | collective-permute-start | bytes 4718600 | tf_op jit(solution)/shard_map/ppermute | solution.py:200
  1.3 5.4 %collective-permute-start.2 = (bf16[256,128]{1,0:T(8,128)(2,1)}, bf16[256,128]{1,0:T(8,128)(2,1)S(1)}, u32[]{:S(2)}, u32[]{:S(2)}) collective-permute-start(bf16[256,128]{1,0:T(8,128)(2,1)} %own_hbm.1), channel_id=1, source_target_pairs={{0,4},{2,6},{4,0},{6,2},{8,12},{10,14},{12,8},{14,10},{16,20},{18,... | collective-permute-start | bytes 196616 | tf_op jit(solution)/shard_map/ppermute | solution.py:206
  4.2 8.2 %collective-permute-start.1 = (bf16[256,128]{1,0:T(8,128)(2,1)}, bf16[256,128]{1,0:T(8,128)(2,1)S(1)}, u32[]{:S(2)}, u32[]{:S(2)}) collective-permute-start(bf16[256,128]{1,0:T(8,128)(2,1)} %own_hbm.1), channel_id=1, source_target_pairs={{0,2},{2,0},{4,6},{6,4},{8,10},{10,8},{12,14},{14,12},{16,18},{18,... | collective-permute-start | bytes 196616 | tf_op jit(solution)/shard_map/ppermute | solution.py:204
  4.2 8.6 %collective-permute-start.4 = (bf16[256,128]{1,0:T(8,128)(2,1)}, bf16[256,128]{1,0:T(8,128)(2,1)S(1)}, u32[]{:S(2)}, u32[]{:S(2)}) collective-permute-start(bf16[256,128]{1,0:T(8,128)(2,1)} %own_hbm.1), channel_id=1, source_target_pairs={{0,8},{2,10},{4,12},{6,14},{8,0},{10,2},{12,4},{14,6},{16,24},{18,... | collective-permute-start | bytes 196616 | tf_op jit(solution)/shard_map/ppermute | solution.py:206
  6.7 8.7 %collective-permute-start.8 = (bf16[256,128]{1,0:T(8,128)(2,1)}, bf16[256,128]{1,0:T(8,128)(2,1)S(1)}, u32[]{:S(2)}, u32[]{:S(2)}) collective-permute-start(bf16[256,128]{1,0:T(8,128)(2,1)} %own_hbm.1), channel_id=1, source_target_pairs={{0,16},{2,18},{4,20},{6,22},{8,24},{10,26},{12,28},{14,30},{16,0},... | collective-permute-start | bytes 196616 | tf_op jit(solution)/shard_map/ppermute | solution.py:206
  12.4 3.1 %collective-permute-start.3 = (bf16[256,128]{1,0:T(8,128)(2,1)S(1)}, bf16[256,128]{1,0:T(8,128)(2,1)S(1)}, u32[]{:S(2)}, u32[]{:S(2)}) collective-permute-start(bf16[256,128]{1,0:T(8,128)(2,1)S(1)} %collective-permute-done.2.refs_1_), channel_id=1, source_target_pairs={{0,2},{2,0},{4,6},{6,4},{8,10},{10,8},{12,14},{14,12},{16,18},{18,... | collective-permute-start | bytes 196616 | tf_op jit(solution)/shard_map/ppermute | solution.py:207
  12.8 5.2 %collective-permute-start.6 = (bf16[256,128]{1,0:T(8,128)(2,1)S(1)}, bf16[256,128]{1,0:T(8,128)(2,1)S(1)}, u32[]{:S(2)}, u32[]{:S(2)}) collective-permute-start(bf16[256,128]{1,0:T(8,128)(2,1)S(1)} %collective-permute-done.4.refs_3_), channel_id=1, source_target_pairs={{0,4},{2,6},{4,0},{6,2},{8,12},{10,14},{12,8},{14,10},{16,20},{18,... | collective-permute-start | bytes 196616 | tf_op jit(solution)/shard_map/ppermute | solution.py:206
  15.4 4.4 %collective-permute-start.5 = (bf16[256,128]{1,0:T(8,128)(2,1)S(1)}, bf16[256,128]{1,0:T(8,128)(2,1)S(1)}, u32[]{:S(2)}, u32[]{:S(2)}) collective-permute-start(bf16[256,128]{1,0:T(8,128)(2,1)S(1)} %collective-permute-done.4.refs_3_), channel_id=1, source_target_pairs={{0,2},{2,0},{4,6},{6,4},{8,10},{10,8},{12,14},{14,12},{16,18},{18,... | collective-permute-start | bytes 196616 | tf_op jit(solution)/shard_map/ppermute | solution.py:207
  15.5 4.4 %collective-permute-start.12 = (bf16[256,128]{1,0:T(8,128)(2,1)S(1)}, bf16[256,128]{1,0:T(8,128)(2,1)S(1)}, u32[]{:S(2)}, u32[]{:S(2)}) collective-permute-start(bf16[256,128]{1,0:T(8,128)(2,1)S(1)} %collective-permute-done.8.refs_7_), channel_id=1, source_target_pairs={{0,8},{2,10},{4,12},{6,14},{8,0},{10,2},{12,4},{14,6},{16,24},{18,... | collective-permute-start | bytes 196616 | tf_op jit(solution)/shard_map/ppermute | solution.py:206
  18.0 4.3 %collective-permute-start.10 = (bf16[256,128]{1,0:T(8,128)(2,1)S(1)}, bf16[256,128]{1,0:T(8,128)(2,1)S(1)}, u32[]{:S(2)}, u32[]{:S(2)}) collective-permute-start(bf16[256,128]{1,0:T(8,128)(2,1)S(1)} %collective-permute-done.8.refs_7_), channel_id=1, source_target_pairs={{0,4},{2,6},{4,0},{6,2},{8,12},{10,14},{12,8},{14,10},{16,20},{18,... | collective-permute-start | bytes 196616 | tf_op jit(solution)/shard_map/ppermute | solution.py:206
  19.8 4.4 %collective-permute-start.9 = (bf16[256,128]{1,0:T(8,128)(2,1)S(1)}, bf16[256,128]{1,0:T(8,128)(2,1)S(1)}, u32[]{:S(2)}, u32[]{:S(2)}) collective-permute-start(bf16[256,128]{1,0:T(8,128)(2,1)S(1)} %collective-permute-done.8.refs_7_), channel_id=1, source_target_pairs={{0,2},{2,0},{4,6},{6,4},{8,10},{10,8},{12,14},{14,12},{16,18},{18,... | collective-permute-start | bytes 196616 | tf_op jit(solution)/shard_map/ppermute | solution.py:207
  19.9 4.2 %collective-permute-start.7 = (bf16[256,128]{1,0:T(8,128)(2,1)S(1)}, bf16[256,128]{1,0:T(8,128)(2,1)S(1)}, u32[]{:S(2)}, u32[]{:S(2)}) collective-permute-start(bf16[256,128]{1,0:T(8,128)(2,1)S(1)} %collective-permute-done.6.refs_5_), channel_id=1, source_target_pairs={{0,2},{2,0},{4,6},{6,4},{8,10},{10,8},{12,14},{14,12},{16,18},{18,... | collective-permute-start | bytes 196616 | tf_op jit(solution)/shard_map/ppermute | solution.py:207
  22.3 4.3 %collective-permute-start.14 = (bf16[256,128]{1,0:T(8,128)(2,1)S(1)}, bf16[256,128]{1,0:T(8,128)(2,1)S(1)}, u32[]{:S(2)}, u32[]{:S(2)}) collective-permute-start(bf16[256,128]{1,0:T(8,128)(2,1)S(1)} %collective-permute-done.10.refs_9_), channel_id=1, source_target_pairs={{0,8},{2,10},{4,12},{6,14},{8,0},{10,2},{12,4},{14,6},{16,24},{18,... | collective-permute-start | bytes 196616 | tf_op jit(solution)/shard_map/ppermute | solution.py:206
  24.1 2.4 %collective-permute-start.11 = (bf16[256,128]{1,0:T(8,128)(2,1)S(1)}, bf16[256,128]{1,0:T(8,128)(2,1)S(1)}, u32[]{:S(2)}, u32[]{:S(2)}) collective-permute-start(bf16[256,128]{1,0:T(8,128)(2,1)S(1)} %collective-permute-done.10.refs_9_), channel_id=1, source_target_pairs={{0,2},{2,0},{4,6},{6,4},{8,10},{10,8},{12,14},{14,12},{16,18},{18,... | collective-permute-start | bytes 196616 | tf_op jit(solution)/shard_map/ppermute | solution.py:207
  24.1 2.4 %collective-permute-start.13 = (bf16[256,128]{1,0:T(8,128)(2,1)S(1)}, bf16[256,128]{1,0:T(8,128)(2,1)S(1)}, u32[]{:S(2)}, u32[]{:S(2)}) collective-permute-start(bf16[256,128]{1,0:T(8,128)(2,1)S(1)} %collective-permute-done.12.refs_11_), channel_id=1, source_target_pairs={{0,2},{2,0},{4,6},{6,4},{8,10},{10,8},{12,14},{14,12},{16,18},{18,... | collective-permute-start | bytes 196616 | tf_op jit(solution)/shard_map/ppermute | solution.py:207
  26.6 1.3 %collective-permute-start.15 = (bf16[256,128]{1,0:T(8,128)(2,1)S(1)}, bf16[256,128]{1,0:T(8,128)(2,1)S(1)}, u32[]{:S(2)}, u32[]{:S(2)}) collective-permute-start(bf16[256,128]{1,0:T(8,128)(2,1)S(1)} %collective-permute-done.14.refs_13_), channel_id=1, source_target_pairs={{0,2},{2,0},{4,6},{6,4},{8,10},{10,8},{12,14},{14,12},{16,18},{18,... | collective-permute-start | bytes 196616 | tf_op jit(solution)/shard_map/ppermute | solution.py:207
  32.4 11.3 %collective-permute-start.17 = (bf16[8,64,384]{2,1,0:T(8,128)(2,1)S(1)}, bf16[8,64,384]{2,1,0:T(8,128)(2,1)S(1)}, u32[]{:S(2)}, u32[]{:S(2)}) collective-permute-start(bf16[8,64,384]{2,1,0:T(8,128)(2,1)S(1)} %get-tuple-element.14), channel_id=1, source_target_pairs={{0,8},{1,9},{2,10},{3,11},{4,12},{5,13},{6,14},{7,15},{8,0},{9,1},... | collective-permute-start | bytes 1179656 | tf_op jit(solution)/shard_map/ppermute | solution.py:259
  37.1 9.8 %collective-permute-start.27 = (bf16[8,64,512]{2,1,0:T(8,128)(2,1)S(1)}, bf16[8,64,512]{2,1,0:T(8,128)(2,1)S(1)}, u32[]{:S(2)}, u32[]{:S(2)}) collective-permute-start(bf16[8,64,512]{2,1,0:T(8,128)(2,1)S(1)} %get-tuple-element.17), channel_id=1, source_target_pairs={{0,4},{1,5},{2,3},{3,2},{4,0},{5,1},{6,7},{7,6},{8,12},{9,13},{10,... | collective-permute-start | bytes 1572872 | tf_op jit(solution)/shard_map/ppermute | solution.py:259
  43.7 11.6 %copy-start = (f32[896,128]{1,0:T(8,128)S(1)}, f32[896,128]{1,0:T(8,128)}, u32[]{:S(2)}) copy-start(f32[896,128]{1,0:T(8,128)} %second_ref.1) | copy-start | bytes 1376260
  43.7 11.6 %copy-start.1 = (f32[896,128]{1,0:T(8,128)S(1)}, f32[896,128]{1,0:T(8,128)}, u32[]{:S(2)}) copy-start(f32[896,128]{1,0:T(8,128)} %moment_ref.1) | copy-start | bytes 1376260
  43.8 5.7 %collective-permute-start.18 = (bf16[4,64,384]{2,1,0:T(8,128)(2,1)S(1)}, bf16[4,64,384]{2,1,0:T(8,128)(2,1)S(1)}, u32[]{:S(2)}, u32[]{:S(2)}) collective-permute-start(bf16[4,64,384]{2,1,0:T(8,128)(2,1)S(1)} %get-tuple-element.30), channel_id=1, source_target_pairs={{0,1},{1,0},{2,6},{3,7},{4,5},{5,4},{6,2},{7,3},{8,9},{9,8},{10,14... | collective-permute-start | bytes 589832 | tf_op jit(solution)/shard_map/ppermute | solution.py:259
  47.3 6.4 %collective-permute-start.28 = (bf16[4,64,512]{2,1,0:T(8,128)(2,1)S(1)}, bf16[4,64,512]{2,1,0:T(8,128)(2,1)S(1)}, u32[]{:S(2)}, u32[]{:S(2)}) collective-permute-start(bf16[4,64,512]{2,1,0:T(8,128)(2,1)S(1)} %get-tuple-element.28), channel_id=1, source_target_pairs={{0,8},{1,9},{2,6},{3,7},{4,12},{5,13},{6,2},{7,3},{8,0},{9,1},{10,... | collective-permute-start | bytes 786440 | tf_op jit(solution)/shard_map/ppermute | solution.py:259
  49.7 6.4 %collective-permute-start.19 = (bf16[2,64,384]{2,1,0:T(8,128)(2,1)S(1)}, bf16[2,64,384]{2,1,0:T(8,128)(2,1)S(1)}, u32[]{:S(2)}, u32[]{:S(2)}) collective-permute-start(bf16[2,64,384]{2,1,0:T(8,128)(2,1)S(1)} %get-tuple-element.34), channel_id=1, source_target_pairs={{0,4},{1,5},{2,3},{3,2},{4,0},{5,1},{6,7},{7,6},{8,12},{9,13},{10,... | collective-permute-start | bytes 294920 | tf_op jit(solution)/shard_map/ppermute | solution.py:259
  53.9 5.0 %collective-permute-start.29 = (bf16[2,64,512]{2,1,0:T(8,128)(2,1)S(1)}, bf16[2,64,512]{2,1,0:T(8,128)(2,1)S(1)}, u32[]{:S(2)}, u32[]{:S(2)}) collective-permute-start(bf16[2,64,512]{2,1,0:T(8,128)(2,1)S(1)} %get-tuple-element.32), channel_id=1, source_target_pairs={{0,1},{1,0},{2,10},{3,11},{4,5},{5,4},{6,14},{7,15},{8,9},{9,8},{1... | collective-permute-start | bytes 393224 | tf_op jit(solution)/shard_map/ppermute | solution.py:259
  55.7 42.0 %copy-start.2 = (bf16[256,128]{1,0:T(8,128)(2,1)S(1)}, bf16[256,128]{1,0:T(8,128)(2,1)}, u32[]{:S(2)}) copy-start(bf16[256,128]{1,0:T(8,128)(2,1)} %own_hbm.1) | copy-start | bytes 196612
  59.0 7.5 %collective-permute-start.30 = (bf16[1,64,512]{2,1,0:T(8,128)(2,1)S(1)}, bf16[1,64,512]{2,1,0:T(8,128)(2,1)S(1)}, u32[]{:S(2)}, u32[]{:S(2)}) collective-permute-start(bf16[1,64,512]{2,1,0:T(8,128)(2,1)S(1)} %fusion.9), channel_id=1, source_target_pairs={{0,16},{1,17},{2,18},{3,19},{4,20},{5,21},{6,22},{7,23},{8,24},{9,... | collective-permute-start | bytes 196616 | tf_op jit(solution)/shard_map/ppermute | solution.py:259
  61.6 6.1 %collective-permute-start.20 = (bf16[1,64,384]{2,1,0:T(8,128)(2,1)S(1)}, bf16[1,64,384]{2,1,0:T(8,128)(2,1)S(1)}, u32[]{:S(2)}, u32[]{:S(2)}) collective-permute-start(bf16[1,64,384]{2,1,0:T(8,128)(2,1)S(1)} %fusion.20), channel_id=1, source_target_pairs={{0,16},{1,17},{2,18},{3,19},{4,20},{5,21},{6,22},{7,23},{8,24},{9,... | collective-permute-start | bytes 147464 | tf_op jit(solution)/shard_map/ppermute | solution.py:259
  66.6 5.7 %collective-permute-start.31 = (bf16[1,64,512]{2,1,0:T(8,128)(2,1)S(1)}, bf16[1,64,512]{2,1,0:T(8,128)(2,1)S(1)}, u32[]{:S(2)}, u32[]{:S(2)}) collective-permute-start(bf16[1,64,512]{2,1,0:T(8,128)(2,1)S(1)} %get-tuple-element.23), channel_id=1, source_target_pairs={{0,16},{1,17},{2,18},{3,19},{4,20},{5,21},{6,22},{7,23},{8,24},{9,... | collective-permute-start | bytes 196616 | tf_op jit(solution)/shard_map/ppermute | solution.py:279
  67.8 6.6 %collective-permute-start.21 = (bf16[1,64,384]{2,1,0:T(8,128)(2,1)S(1)}, bf16[1,64,384]{2,1,0:T(8,128)(2,1)S(1)}, u32[]{:S(2)}, u32[]{:S(2)}) collective-permute-start(bf16[1,64,384]{2,1,0:T(8,128)(2,1)S(1)} %get-tuple-element.25), channel_id=1, source_target_pairs={{0,16},{1,17},{2,18},{3,19},{4,20},{5,21},{6,22},{7,23},{8,24},{9,... | collective-permute-start | bytes 147464 | tf_op jit(solution)/shard_map/ppermute | solution.py:279
  72.3 6.3 %collective-permute-start.32 = (bf16[2,64,512]{2,1,0:T(8,128)(2,1)S(1)}, bf16[2,64,512]{2,1,0:T(8,128)(2,1)S(1)}, u32[]{:S(2)}, u32[]{:S(2)}) collective-permute-start(bf16[2,64,512]{2,1,0:T(8,128)(2,1)S(1)} %pad_maximum_fusion.6), channel_id=1, source_target_pairs={{0,1},{1,0},{2,10},{3,11},{4,5},{5,4},{6,14},{7,15},{8,9},{9,8},{1... | collective-permute-start | bytes 393224 | tf_op jit(solution)/shard_map/ppermute | solution.py:279
  72.4 8.3 %collective-permute-start.35 = (f32[64,384]{1,0:T(8,128)S(1)}, f32[64,384]{1,0:T(8,128)S(1)}, u32[]{:S(2)}, u32[]{:S(2)}) collective-permute-start(f32[64,384]{1,0:T(8,128)S(1)} %get-tuple-element.26), channel_id=1, source_target_pairs={{0,1},{1,0},{2,3},{3,2},{4,5},{5,4},{6,7},{7,6},{8,9},{9,8},{10,11... | collective-permute-start | bytes 294920 | tf_op jit(solution)/shard_map/ppermute | solution.py:273
  74.4 6.2 %collective-permute-start.22 = (bf16[2,64,384]{2,1,0:T(8,128)(2,1)S(1)}, bf16[2,64,384]{2,1,0:T(8,128)(2,1)S(1)}, u32[]{:S(2)}, u32[]{:S(2)}) collective-permute-start(bf16[2,64,384]{2,1,0:T(8,128)(2,1)S(1)} %pad_maximum_fusion.7), channel_id=1, source_target_pairs={{0,4},{1,5},{2,3},{3,2},{4,0},{5,1},{6,7},{7,6},{8,12},{9,13},{10,... | collective-permute-start | bytes 294920 | tf_op jit(solution)/shard_map/ppermute | solution.py:279
  78.6 9.2 %collective-permute-start.33 = (bf16[4,64,512]{2,1,0:T(8,128)(2,1)S(1)}, bf16[4,64,512]{2,1,0:T(8,128)(2,1)S(1)}, u32[]{:S(2)}, u32[]{:S(2)}) collective-permute-start(bf16[4,64,512]{2,1,0:T(8,128)(2,1)S(1)} %pad_maximum_fusion.2), channel_id=1, source_target_pairs={{0,8},{1,9},{2,6},{3,7},{4,12},{5,13},{6,2},{7,3},{8,0},{9,1},{10,... | collective-permute-start | bytes 786440 | tf_op jit(solution)/shard_map/ppermute | solution.py:279
  80.7 8.2 %collective-permute-start.23 = (bf16[4,64,384]{2,1,0:T(8,128)(2,1)S(1)}, bf16[4,64,384]{2,1,0:T(8,128)(2,1)S(1)}, u32[]{:S(2)}, u32[]{:S(2)}) collective-permute-start(bf16[4,64,384]{2,1,0:T(8,128)(2,1)S(1)} %pad_maximum_fusion.4), channel_id=1, source_target_pairs={{0,1},{1,0},{2,6},{3,7},{4,5},{5,4},{6,2},{7,3},{8,9},{9,8},{10,14... | collective-permute-start | bytes 589832 | tf_op jit(solution)/shard_map/ppermute | solution.py:279
  80.8 8.2 %collective-permute-start.36 = (f32[64,512]{1,0:T(8,128)S(1)}, f32[64,512]{1,0:T(8,128)S(1)}, u32[]{:S(2)}, u32[]{:S(2)}) collective-permute-start(f32[64,512]{1,0:T(8,128)S(1)} %get-tuple-element.24), channel_id=1, source_target_pairs={{0,1},{1,0},{2,3},{3,2},{4,5},{5,4},{6,7},{7,6},{8,9},{9,8},{10,11... | collective-permute-start | bytes 393224 | tf_op jit(solution)/shard_map/ppermute | solution.py:273
  87.9 9.2 %collective-permute-start.34 = (bf16[8,64,512]{2,1,0:T(8,128)(2,1)S(1)}, bf16[8,64,512]{2,1,0:T(8,128)(2,1)S(1)}, u32[]{:S(2)}, u32[]{:S(2)}) collective-permute-start(bf16[8,64,512]{2,1,0:T(8,128)(2,1)S(1)} %pad_maximum_fusion.refs_0_), channel_id=1, source_target_pairs={{0,4},{1,5},{2,3},{3,2},{4,0},{5,1},{6,7},{7,6},{8,12},{9,13},{10,... | collective-permute-start | bytes 1572872 | tf_op jit(solution)/shard_map/ppermute | solution.py:289
  88.9 8.7 %collective-permute-start.24 = (bf16[8,64,384]{2,1,0:T(8,128)(2,1)S(1)}, bf16[8,64,384]{2,1,0:T(8,128)(2,1)S(1)}, u32[]{:S(2)}, u32[]{:S(2)}) collective-permute-start(bf16[8,64,384]{2,1,0:T(8,128)(2,1)S(1)} %pad_maximum_fusion.1.refs_0_), channel_id=1, source_target_pairs={{0,8},{1,9},{2,10},{3,11},{4,12},{5,13},{6,14},{7,15},{8,0},{9,1},... | collective-permute-start | bytes 1179656 | tf_op jit(solution)/shard_map/ppermute | solution.py:289
  90.2 7.6 %collective-permute-start.37 = (bf16[8,64,512]{2,1,0:T(8,128)(2,1)S(1)}, bf16[8,64,512]{2,1,0:T(8,128)(2,1)S(1)}, u32[]{:S(2)}, u32[]{:S(2)}) collective-permute-start(bf16[8,64,512]{2,1,0:T(8,128)(2,1)S(1)} %pad_maximum_fusion.refs_0_), channel_id=1, source_target_pairs={{0,2},{2,0},{4,6},{6,4},{8,10},{10,8},{12,14},{14,12},{16,18},{18,... | collective-permute-start | bytes 1572872 | tf_op jit(solution)/shard_map/ppermute | solution.py:292
  97.1 1.9 %collective-permute-start.38 = (bf16[8,64,512]{2,1,0:T(8,128)(2,1)S(1)}, bf16[8,64,512]{2,1,0:T(8,128)(2,1)S(1)}, u32[]{:S(2)}, u32[]{:S(2)}) collective-permute-start(bf16[8,64,512]{2,1,0:T(8,128)(2,1)S(1)} %collective-permute-done.34.refs_1_), channel_id=1, source_target_pairs={{0,2},{2,0},{4,6},{6,4},{8,10},{10,8},{12,14},{14,12},{16,18},{18,... | collective-permute-start | bytes 1572872 | tf_op jit(solution)/shard_map/ppermute | solution.py:292
  97.1 4.3 %collective-permute-start.25 = (bf16[8,64,384]{2,1,0:T(8,128)(2,1)S(1)}, bf16[8,64,384]{2,1,0:T(8,128)(2,1)S(1)}, u32[]{:S(2)}, u32[]{:S(2)}) collective-permute-start(bf16[8,64,384]{2,1,0:T(8,128)(2,1)S(1)} %pad_maximum_fusion.1.refs_0_), channel_id=1, source_target_pairs={{0,2},{2,0},{4,6},{6,4},{8,10},{10,8},{12,14},{14,12},{16,18},{18,... | collective-permute-start | bytes 1179656 | tf_op jit(solution)/shard_map/ppermute | solution.py:292
  97.7 3.8 %collective-permute-start.26 = (bf16[8,64,384]{2,1,0:T(8,128)(2,1)S(1)}, bf16[8,64,384]{2,1,0:T(8,128)(2,1)S(1)}, u32[]{:S(2)}, u32[]{:S(2)}) collective-permute-start(bf16[8,64,384]{2,1,0:T(8,128)(2,1)S(1)} %collective-permute-done.24.refs_1_), channel_id=1, source_target_pairs={{0,2},{2,0},{4,6},{6,4},{8,10},{10,8},{12,14},{14,12},{16,18},{18,... | collective-permute-start | bytes 1179656 | tf_op jit(solution)/shard_map/ppermute | solution.py:292

commit v3 on v2

--- a/solution.py
+++ b/solution.py
@@ -8,8 +8,7 @@
 from jax.sharding import PartitionSpec as P
 
 STEP = 10
-ORDERS = (("zyxw", "zxyw"), ("xzyw", "yxzw"))
-EXPAND = (1, 0)
+ORDERS = (("zxyw", "zxyw"), ("xzyw", "yxzw"))
 AXES = ("fsdp", "dp")
 
 
@@ -144,8 +143,9 @@
     multiply(n, m, width, chunk, left_ref, loads, g_ref, h_ref, keep_ref, send_ref)
 
 
-def expand_kernel(n, m, width, chunk, p_ref, *refs):
-    parts, (o_ref, stage_ref, sems) = refs[:4], refs[-3:]
+def expand_kernel(n, m, width, whose, p_ref, *refs):
+    count = len(chunks_of(width))
+    parts, (o_ref, stage_ref, sems) = refs[: 2 * count * len(whose)], refs[-3:]
     i = lax.axis_index("fsdp")
     core, own = i & 1, i >> 1
     half = parts[0].shape[0]
@@ -153,20 +153,28 @@
     def rows(c):
         copies = []
         for block in range(n // 2):
-            pair = []
-            for owner in range(2):
-                mine = parts[:2] if owner == c else parts[2:]
-                slots = [slot_of(orders(n, m, chunk)[owner], block, part) for part in range(m)]
-                right = jnp.concatenate([mine[t // half][t % half] for t in slots], axis=0)
-                out = jnp.dot(p_ref[...], right, preferred_element_type=jnp.float32)
-                pair.append(out.astype(o_ref.dtype))
-            whole = [jnp.concatenate(pair, axis=1)] if width % 128 else pair
-            for owner, out in enumerate(whole):
-                k = block * len(whole) + owner
-                stage_ref[k] = out
-                at = columns_of(width, chunk, block ^ own, owner)
-                copies.append(pltpu.make_async_copy(stage_ref.at[k], o_ref.at[:, at], sems.at[k]))
-                copies[-1].start()
+            outs = {}
+            for k, other in enumerate(whose):
+                owner = c ^ other
+                columns = []
+                for chunk in range(count):
+                    first = 2 * (k * count + chunk)
+                    order = orders(n, m, chunk)[owner]
+                    slots = [slot_of(order, block, part) for part in range(m)]
+                    right = jnp.concatenate([parts[first + t // half][t % half] for t in slots], axis=0)
+                    out = jnp.dot(p_ref[...], right, preferred_element_type=jnp.float32)
+                    columns.append(out.astype(o_ref.dtype))
+                outs[owner] = columns
+            if width % 128:
+                stage_ref[block] = jnp.concatenate(outs[0] + outs[1], axis=1)
+                at = pl.ds(pl.multiple_of((block ^ own) * 2 * width, 128), 2 * width)
+            else:
+                ((owner, columns),) = outs.items()
+                for (first, last), out in zip(chunks_of(width), columns):
+                    stage_ref[block, :, first:last] = out
+                at = pl.ds(pl.multiple_of((2 * (block ^ own) + owner) * width, 128), width)
+            copies.append(pltpu.make_async_copy(stage_ref.at[block], o_ref.at[:, at], sems.at[block]))
+            copies[-1].start()
         for copy in copies:
             copy.wait()
 
@@ -251,7 +259,7 @@
     second_t = lax.dynamic_slice_in_dim(second.T, y * size, size)
     first_fix = 1.0 - 0.9**STEP
     second_fix = 1.0 - 0.999**STEP
-    parts, fulls = [], []
+    parts, fulls = [[], []], []
     for chunk, (start, stop) in enumerate(chunks_of(width)):
         steps = list(zip(*orders(n, m, chunk)))
         keep, send = sums[2 * chunk : 2 * chunk + 2]
@@ -289,27 +297,28 @@
         rest = lax.ppermute(held, AXES, pairs(n, m, steps[0]))
         if stop == width:
             rest, new_moment, new_second = lax.optimization_barrier((rest, new_moment, new_second))
-        parts.append([held, rest, lax.ppermute(held, "fsdp", partner), lax.ppermute(rest, "fsdp", partner)])
-
-    copies = n if width % 128 == 0 else n // 2
+        parts[0] += [held, rest]
+        parts[1] += [lax.ppermute(held, "fsdp", partner), lax.ppermute(rest, "fsdp", partner)]
+
     relative = relative_ranks(projection, y, m)
     update = []
-    for chunk in EXPAND[-len(parts) :]:
-        start, stop = chunks_of(width)[chunk]
+    for whose in ((0,), (1,)) if width % 128 == 0 else ((0, 1),):
+        span = len(whose) * width
+        sources = [part for other in whose for part in parts[other]]
         update = [
             pl.pallas_call(
-                functools.partial(expand_kernel, n, m, width, chunk),
-                in_specs=[VMEM] * 5 + [HBM] * len(update),
+                functools.partial(expand_kernel, n, m, width, whose),
+                in_specs=[VMEM] * (1 + len(sources)) + [HBM] * len(update),
                 out_specs=HBM,
                 out_shape=jax.ShapeDtypeStruct((projection.shape[0], n * width), jnp.bfloat16),
-                input_output_aliases={5: 0} if update else {},
+                input_output_aliases={1 + len(sources): 0} if update else {},
                 scratch_shapes=[
-                    pltpu.VMEM((copies, projection.shape[0], n * (stop - start) // copies), jnp.bfloat16),
-                    pltpu.SemaphoreType.DMA((copies,)),
+                    pltpu.VMEM((n // 2, projection.shape[0], span), jnp.bfloat16),
+                    pltpu.SemaphoreType.DMA((n // 2,)),
                 ],
                 compiler_params=pltpu.CompilerParams(vmem_limit_bytes=16 << 20),
                 name="expand",
-            )(*placed(pltpu.VMEM, relative, *parts[chunk]), *update)
+            )(*placed(pltpu.VMEM, relative, *sources), *update)
         ]
     return (*update, new_moment, new_second)
 

time: 104 us -> 101 us (0.971)
  waiting for transfers between devices: 48 us -> 36.9 us
  starting transfers between devices: 39.4 us -> 47.8 us
    ppermute x6, waiting for transfers between devices: 10.2 us -> 4.62 us  [local(): got = lax.ppermute(held, AXES, pairs(n, m, both))]
    ppermute x6, starting transfers between devices: 4.8 us -> 10.1 us  [local(): got = lax.ppermute(held, AXES, pairs(n, m, both))]
    ppermute x2, starting transfers between devices: 1.03 us -> 6.17 us  [local(): rest = lax.ppermute(held, AXES, pairs(n, m, steps[0]))]
    ppermute x2, waiting for transfers between devices: 6.92 us -> 4.06 us  [local(): rest = lax.ppermute(held, AXES, pairs(n, m, steps[0]))]
    ppermute x2, starting transfers between devices: 4.02 us -> 2.03 us  [local(): got = lax.ppermute(full, 'dp', [(w, w ^ 1 << k) for w in range(m)])]
    ppermute x2, waiting for transfers between devices: 1.98 us -> 0.01 us  [local(): got = lax.ppermute(full, 'dp', [(w, w ^ 1 << k) for w in range(m)])]
    ppermute x2, waiting for transfers between devices: 1.19 us -> 0.01 us  [local(): lax.ppermute(rest, 'fsdp', partner)]
  transfers between devices with their start and end apart: 39 -> 39, of which waited for: 19 -> 21; matrix products, arithmetic and copies ran while one was open for 2% -> 2% of each run, Pallas kernels for 6% -> 6%
where the time goes in v3:
time: 101 us
  starting transfers between devices  47.8 us (47%)
  waiting for transfers between devices  36.9 us (37%)
  Pallas kernels  12.9 us (13%)
  other arithmetic  1.35 us (1%)
  between operations  1.05 us (1%)
    ppermute x8, waiting for transfers between devices, local(): got = lax.ppermute(send, AXES, pairs(n, m, both)).astype(jnp.float32)  18.3 us
    ppermute x7, starting transfers between devices, local(): lax.ppermute(held[source], 'fsdp', [(w, w ^ 1 << k) for w in range(n)])  15.3 us
    ppermute x8, starting transfers between devices, local(): got = lax.ppermute(send, AXES, pairs(n, m, both)).astype(jnp.float32)  11.8 us
    ppermute x6, starting transfers between devices, local(): got = lax.ppermute(held, AXES, pairs(n, m, both))  10.1 us
    ppermute x2, starting transfers between devices, local(): rest = lax.ppermute(held, AXES, pairs(n, m, steps[0]))  6.17 us
    ppermute x7, waiting for transfers between devices, local(): lax.ppermute(held[source], 'fsdp', [(w, w ^ 1 << k) for w in range(n)])  5.98 us
    ppermute x6, waiting for transfers between devices, local(): got = lax.ppermute(held, AXES, pairs(n, m, both))  4.62 us
    pallas_call x1, Pallas kernels, local(): pl.pallas_call(functools.partial(first_kernel, n, m, width), in_specs=[HB...  4.53 us
  transfers between devices with their start and end apart: 39, of which 21 were waited for; matrix products, arithmetic and copies ran while one was open for 2% of the time, Pallas kernels for 6%

profile of v3, /device:TPU:0, one launch (start us, length us, event | category | flops | bytes accessed | tf_op | source)
XLA Modules:
  0.0 100.8 jit_solution(14806764008545965002)
XLA Ops:
  0.6 0.6 collective-permute-start.16
  1.3 2.9 %collective-permute-start.2 = (bf16[256,128]{1,0:T(8,128)(2,1)}, bf16[256,128]{1,0:T(8,128)(2,1)S(1)}, u32[]{:S(2)}, u32[]{:S(2)}) collective-permute-start(bf16[256,128]{1,0:T(8,128)(2,1)} %own_hbm.1), channel_id=1, source_target_pairs={{0,4},{2,6},{4,0},{6,2},{8,12},{10,14},{12,8},{14,10},{16,20},{18,... | collective-permute-start | bytes 196616 | tf_op jit(solution)/shard_map/ppermute | solution.py:214
  4.2 1.6 %collective-permute-start.4 = (bf16[256,128]{1,0:T(8,128)(2,1)}, bf16[256,128]{1,0:T(8,128)(2,1)S(1)}, u32[]{:S(2)}, u32[]{:S(2)}) collective-permute-start(bf16[256,128]{1,0:T(8,128)(2,1)} %own_hbm.1), channel_id=1, source_target_pairs={{0,8},{2,10},{4,12},{6,14},{8,0},{10,2},{12,4},{14,6},{16,24},{18,... | collective-permute-start | bytes 196616 | tf_op jit(solution)/shard_map/ppermute | solution.py:214
  5.8 1.0 collective-permute-done.2.refs_1_
  6.7 3.0 %collective-permute-start.8 = (bf16[256,128]{1,0:T(8,128)(2,1)}, bf16[256,128]{1,0:T(8,128)(2,1)S(1)}, u32[]{:S(2)}, u32[]{:S(2)}) collective-permute-start(bf16[256,128]{1,0:T(8,128)(2,1)} %own_hbm.1), channel_id=1, source_target_pairs={{0,16},{2,18},{4,20},{6,22},{8,24},{10,26},{12,28},{14,30},{16,0},... | collective-permute-start | bytes 196616 | tf_op jit(solution)/shard_map/ppermute | solution.py:214
  9.7 2.7 %collective-permute-done.1.refs_0_ = bf16[256,128]{1,0:T(8,128)(2,1)S(1)} collective-permute-done((bf16[256,128]{1,0:T(8,128)(2,1)}, bf16[256,128]{1,0:T(8,128)(2,1)S(1)}, u32[]{:S(2)}, u32[]{:S(2)}) %collective-permute-start.1) | collective-permute-done | bytes 65568 | tf_op jit(solution)/shard_map/ppermute | solution.py:212
  12.8 2.6 %collective-permute-start.6 = (bf16[256,128]{1,0:T(8,128)(2,1)S(1)}, bf16[256,128]{1,0:T(8,128)(2,1)S(1)}, u32[]{:S(2)}, u32[]{:S(2)}) collective-permute-start(bf16[256,128]{1,0:T(8,128)(2,1)S(1)} %collective-permute-done.4.refs_3_), channel_id=1, source_target_pairs={{0,4},{2,6},{4,0},{6,2},{8,12},{10,14},{12,8},{14,10},{16,20},{18,... | collective-permute-start | bytes 196616 | tf_op jit(solution)/shard_map/ppermute | solution.py:214
  15.5 1.6 %collective-permute-start.12 = (bf16[256,128]{1,0:T(8,128)(2,1)S(1)}, bf16[256,128]{1,0:T(8,128)(2,1)S(1)}, u32[]{:S(2)}, u32[]{:S(2)}) collective-permute-start(bf16[256,128]{1,0:T(8,128)(2,1)S(1)} %collective-permute-done.8.refs_7_), channel_id=1, source_target_pairs={{0,8},{2,10},{4,12},{6,14},{8,0},{10,2},{12,4},{14,6},{16,24},{18,... | collective-permute-start | bytes 196616 | tf_op jit(solution)/shard_map/ppermute | solution.py:214
  17.1 0.9 collective-permute-done.6.refs_5_
  18.0 1.7 %collective-permute-start.10 = (bf16[256,128]{1,0:T(8,128)(2,1)S(1)}, bf16[256,128]{1,0:T(8,128)(2,1)S(1)}, u32[]{:S(2)}, u32[]{:S(2)}) collective-permute-start(bf16[256,128]{1,0:T(8,128)(2,1)S(1)} %collective-permute-done.8.refs_7_), channel_id=1, source_target_pairs={{0,4},{2,6},{4,0},{6,2},{8,12},{10,14},{12,8},{14,10},{16,20},{18,... | collective-permute-start | bytes 196616 | tf_op jit(solution)/shard_map/ppermute | solution.py:214
  20.3 2.0 %collective-permute-done.10.refs_9_ = bf16[256,128]{1,0:T(8,128)(2,1)S(1)} collective-permute-done((bf16[256,128]{1,0:T(8,128)(2,1)S(1)}, bf16[256,128]{1,0:T(8,128)(2,1)S(1)}, u32[]{:S(2)}, u32[]{:S(2)}) %collective-permute-start.10) | collective-permute-done | bytes 65568 | tf_op jit(solution)/shard_map/ppermute | solution.py:214
  22.3 1.8 %collective-permute-start.14 = (bf16[256,128]{1,0:T(8,128)(2,1)S(1)}, bf16[256,128]{1,0:T(8,128)(2,1)S(1)}, u32[]{:S(2)}, u32[]{:S(2)}) collective-permute-start(bf16[256,128]{1,0:T(8,128)(2,1)S(1)} %collective-permute-done.10.refs_9_), channel_id=1, source_target_pairs={{0,8},{2,10},{4,12},{6,14},{8,0},{10,2},{12,4},{14,6},{16,24},{18,... | collective-permute-start | bytes 196616 | tf_op jit(solution)/shard_map/ppermute | solution.py:214
  24.1 0.5 collective-permute-start.13
  24.6 1.9 %collective-permute-done.14.refs_13_ = bf16[256,128]{1,0:T(8,128)(2,1)S(1)} collective-permute-done((bf16[256,128]{1,0:T(8,128)(2,1)S(1)}, bf16[256,128]{1,0:T(8,128)(2,1)S(1)}, u32[]{:S(2)}, u32[]{:S(2)}) %collective-permute-start.14) | collective-permute-done | bytes 65568 | tf_op jit(solution)/shard_map/ppermute | solution.py:214
  26.6 1.2 %collective-permute-done.15.refs_14_ = bf16[256,128]{1,0:T(8,128)(2,1)S(1)} collective-permute-done((bf16[256,128]{1,0:T(8,128)(2,1)S(1)}, bf16[256,128]{1,0:T(8,128)(2,1)S(1)}, u32[]{:S(2)}, u32[]{:S(2)}) %collective-permute-start.15) | collective-permute-done | bytes 65568 | tf_op jit(solution)/shard_map/ppermute | solution.py:215
  27.8 4.5 %project.1 = (f32[8,64,384]{2,1,0:T(8,128)S(1)}, bf16[8,64,384]{2,1,0:T(8,128)(2,1)S(1)}, bf16[2,128,192]{2,1,0:T(8,128)(2,1)S(1)}) custom-call(bf16[192,4096]{1,0:T(8,128)(2,1)} %a_hbm.1, bf16[256,128]{1,0:T(8,128)(2,1)} %own_hbm.1, bf16[192,14336]{1,0:T(8,128)(2,1)} %g_hbm.3, bf16[192,4096]{1,0:T(8,128)(2,1)S(1)} %collective-permute-done.b_ref, ...), custom_call_target="tpu_custom_call" | custom-call | tf_op jit(solution)/shard_map/project/pallas_call | solution.py:229
  32.4 1.9 %collective-permute-start.17 = (bf16[8,64,384]{2,1,0:T(8,128)(2,1)S(1)}, bf16[8,64,384]{2,1,0:T(8,128)(2,1)S(1)}, u32[]{:S(2)}, u32[]{:S(2)}) collective-permute-start(bf16[8,64,384]{2,1,0:T(8,128)(2,1)S(1)} %get-tuple-element.14), channel_id=1, source_target_pairs={{0,8},{1,9},{2,10},{3,11},{4,12},{5,13},{6,14},{7,15},{8,0},{9,1},... | collective-permute-start | bytes 1179656 | tf_op jit(solution)/shard_map/ppermute | solution.py:267
  34.2 2.9 %multiply.5 = (f32[8,64,512]{2,1,0:T(8,128)S(1)}, bf16[8,64,512]{2,1,0:T(8,128)(2,1)S(1)}) custom-call(bf16[192,14336]{1,0:T(8,128)(2,1)} %g_hbm.3, bf16[192,14336]{1,0:T(8,128)(2,1)S(1)} %collective-permute-done.16.refs_15_.h_ref, bf16[2,128,192]{2,1,0:T(8,128)(2,1)S(1)} %get-tuple-element.15.left_ref), custom_call_target="tpu_custom_call" | custom-call | tf_op jit(solution)/shard_map/multiply/pallas_call | solution.py:247
  37.1 1.6 %collective-permute-start.27 = (bf16[8,64,512]{2,1,0:T(8,128)(2,1)S(1)}, bf16[8,64,512]{2,1,0:T(8,128)(2,1)S(1)}, u32[]{:S(2)}, u32[]{:S(2)}) collective-permute-start(bf16[8,64,512]{2,1,0:T(8,128)(2,1)S(1)} %get-tuple-element.17), channel_id=1, source_target_pairs={{0,4},{1,5},{2,3},{3,2},{4,0},{5,1},{6,7},{7,6},{8,12},{9,13},{10,... | collective-permute-start | bytes 1572872 | tf_op jit(solution)/shard_map/ppermute | solution.py:267
  38.7 5.0 %collective-permute-done.17 = bf16[8,64,384]{2,1,0:T(8,128)(2,1)S(1)} collective-permute-done((bf16[8,64,384]{2,1,0:T(8,128)(2,1)S(1)}, bf16[8,64,384]{2,1,0:T(8,128)(2,1)S(1)}, u32[]{:S(2)}, u32[]{:S(2)}) %collective-permute-start.17) | collective-permute-done | bytes 393248 | tf_op jit(solution)/shard_map/ppermute | solution.py:267
  43.8 1.7 %collective-permute-start.18 = (bf16[4,64,384]{2,1,0:T(8,128)(2,1)S(1)}, bf16[4,64,384]{2,1,0:T(8,128)(2,1)S(1)}, u32[]{:S(2)}, u32[]{:S(2)}) collective-permute-start(bf16[4,64,384]{2,1,0:T(8,128)(2,1)S(1)} %get-tuple-element.30), channel_id=1, source_target_pairs={{0,4},{1,5},{2,6},{3,7},{4,0},{5,1},{6,2},{7,3},{8,12},{9,13},{10,... | collective-permute-start | bytes 589832 | tf_op jit(solution)/shard_map/ppermute | solution.py:267
  45.6 1.3 %collective-permute-done.27 = bf16[8,64,512]{2,1,0:T(8,128)(2,1)S(1)} collective-permute-done((bf16[8,64,512]{2,1,0:T(8,128)(2,1)S(1)}, bf16[8,64,512]{2,1,0:T(8,128)(2,1)S(1)}, u32[]{:S(2)}, u32[]{:S(2)}) %collective-permute-start.27) | collective-permute-done | bytes 524320 | tf_op jit(solution)/shard_map/ppermute | solution.py:267
  47.6 4.1 %collective-permute-done.18 = bf16[4,64,384]{2,1,0:T(8,128)(2,1)S(1)} collective-permute-done((bf16[4,64,384]{2,1,0:T(8,128)(2,1)S(1)}, bf16[4,64,384]{2,1,0:T(8,128)(2,1)S(1)}, u32[]{:S(2)}, u32[]{:S(2)}) %collective-permute-start.18) | collective-permute-done | bytes 196640 | tf_op jit(solution)/shard_map/ppermute | solution.py:267
  51.8 1.8 %collective-permute-start.19 = (bf16[2,64,384]{2,1,0:T(8,128)(2,1)S(1)}, bf16[2,64,384]{2,1,0:T(8,128)(2,1)S(1)}, u32[]{:S(2)}, u32[]{:S(2)}) collective-permute-start(bf16[2,64,384]{2,1,0:T(8,128)(2,1)S(1)} %get-tuple-element.34), channel_id=1, source_target_pairs={{0,1},{1,0},{2,3},{3,2},{4,5},{5,4},{6,7},{7,6},{8,9},{9,8},{10,11... | collective-permute-start | bytes 294920 | tf_op jit(solution)/shard_map/ppermute | solution.py:267
  53.9 1.5 %collective-permute-start.29 = (bf16[2,64,512]{2,1,0:T(8,128)(2,1)S(1)}, bf16[2,64,512]{2,1,0:T(8,128)(2,1)S(1)}, u32[]{:S(2)}, u32[]{:S(2)}) collective-permute-start(bf16[2,64,512]{2,1,0:T(8,128)(2,1)S(1)} %get-tuple-element.32), channel_id=1, source_target_pairs={{0,1},{1,0},{2,10},{3,11},{4,5},{5,4},{6,14},{7,15},{8,9},{9,8},{1... | collective-permute-start | bytes 393224 | tf_op jit(solution)/shard_map/ppermute | solution.py:267
  56.5 2.4 %collective-permute-done.29 = bf16[2,64,512]{2,1,0:T(8,128)(2,1)S(1)} collective-permute-done((bf16[2,64,512]{2,1,0:T(8,128)(2,1)S(1)}, bf16[2,64,512]{2,1,0:T(8,128)(2,1)S(1)}, u32[]{:S(2)}, u32[]{:S(2)}) %collective-permute-start.29) | collective-permute-done | bytes 131104 | tf_op jit(solution)/shard_map/ppermute | solution.py:267
  59.0 2.6 %collective-permute-start.30 = (bf16[1,64,512]{2,1,0:T(8,128)(2,1)S(1)}, bf16[1,64,512]{2,1,0:T(8,128)(2,1)S(1)}, u32[]{:S(2)}, u32[]{:S(2)}) collective-permute-start(bf16[1,64,512]{2,1,0:T(8,128)(2,1)S(1)} %fusion.9), channel_id=1, source_target_pairs={{0,16},{1,17},{2,18},{3,19},{4,20},{5,21},{6,22},{7,23},{8,24},{9,... | collective-permute-start | bytes 196616 | tf_op jit(solution)/shard_map/ppermute | solution.py:267
  61.6 0.5 collective-permute-start.20
  62.0 3.7 %collective-permute-done.30 = bf16[1,64,512]{2,1,0:T(8,128)(2,1)S(1)} collective-permute-done((bf16[1,64,512]{2,1,0:T(8,128)(2,1)S(1)}, bf16[1,64,512]{2,1,0:T(8,128)(2,1)S(1)}, u32[]{:S(2)}, u32[]{:S(2)}) %collective-permute-start.30) | collective-permute-done | bytes 65568 | tf_op jit(solution)/shard_map/ppermute | solution.py:267
  65.9 1.1 %collective-permute-start.31 = (bf16[1,64,512]{2,1,0:T(8,128)(2,1)S(1)}, bf16[1,64,512]{2,1,0:T(8,128)(2,1)S(1)}, u32[]{:S(2)}, u32[]{:S(2)}) collective-permute-start(bf16[1,64,512]{2,1,0:T(8,128)(2,1)S(1)} %get-tuple-element.23), channel_id=1, source_target_pairs={{0,16},{1,17},{2,18},{3,19},{4,20},{5,21},{6,22},{7,23},{8,24},{9,... | collective-permute-start | bytes 196616 | tf_op jit(solution)/shard_map/ppermute | solution.py:287
  67.0 1.1 %collective-permute-done.20 = bf16[1,64,384]{2,1,0:T(8,128)(2,1)S(1)} collective-permute-done((bf16[1,64,384]{2,1,0:T(8,128)(2,1)S(1)}, bf16[1,64,384]{2,1,0:T(8,128)(2,1)S(1)}, u32[]{:S(2)}, u32[]{:S(2)}) %collective-permute-start.20) | collective-permute-done | bytes 49184 | tf_op jit(solution)/shard_map/ppermute | solution.py:267
  68.2 0.8 collective-permute-start.21
  69.0 2.6 %collective-permute-done.31 = bf16[1,64,512]{2,1,0:T(8,128)(2,1)S(1)} collective-permute-done((bf16[1,64,512]{2,1,0:T(8,128)(2,1)S(1)}, bf16[1,64,512]{2,1,0:T(8,128)(2,1)S(1)}, u32[]{:S(2)}, u32[]{:S(2)}) %collective-permute-start.31) | collective-permute-done | bytes 65568 | tf_op jit(solution)/shard_map/ppermute | solution.py:287
  71.7 2.0 %collective-permute-start.32 = (bf16[2,64,512]{2,1,0:T(8,128)(2,1)S(1)}, bf16[2,64,512]{2,1,0:T(8,128)(2,1)S(1)}, u32[]{:S(2)}, u32[]{:S(2)}) collective-permute-start(bf16[2,64,512]{2,1,0:T(8,128)(2,1)S(1)} %pad_maximum_fusion.6), channel_id=1, source_target_pairs={{0,1},{1,0},{2,10},{3,11},{4,5},{5,4},{6,14},{7,15},{8,9},{9,8},{1... | collective-permute-start | bytes 393224 | tf_op jit(solution)/shard_map/ppermute | solution.py:287
  73.8 2.0 %collective-permute-start.22 = (bf16[2,64,384]{2,1,0:T(8,128)(2,1)S(1)}, bf16[2,64,384]{2,1,0:T(8,128)(2,1)S(1)}, u32[]{:S(2)}, u32[]{:S(2)}) collective-permute-start(bf16[2,64,384]{2,1,0:T(8,128)(2,1)S(1)} %pad_maximum_fusion.7), channel_id=1, source_target_pairs={{0,1},{1,0},{2,3},{3,2},{4,5},{5,4},{6,7},{7,6},{8,9},{9,8},{10,11... | collective-permute-start | bytes 294920 | tf_op jit(solution)/shard_map/ppermute | solution.py:287
  75.7 1.1 %collective-permute-done.32 = bf16[2,64,512]{2,1,0:T(8,128)(2,1)S(1)} collective-permute-done((bf16[2,64,512]{2,1,0:T(8,128)(2,1)S(1)}, bf16[2,64,512]{2,1,0:T(8,128)(2,1)S(1)}, u32[]{:S(2)}, u32[]{:S(2)}) %collective-permute-start.32) | collective-permute-done | bytes 131104 | tf_op jit(solution)/shard_map/ppermute | solution.py:287
  76.9 2.1 %collective-permute-start.33 = (bf16[4,64,512]{2,1,0:T(8,128)(2,1)S(1)}, bf16[4,64,512]{2,1,0:T(8,128)(2,1)S(1)}, u32[]{:S(2)}, u32[]{:S(2)}) collective-permute-start(bf16[4,64,512]{2,1,0:T(8,128)(2,1)S(1)} %pad_maximum_fusion.2), channel_id=1, source_target_pairs={{0,8},{1,9},{2,6},{3,7},{4,12},{5,13},{6,2},{7,3},{8,0},{9,1},{10,... | collective-permute-start | bytes 786440 | tf_op jit(solution)/shard_map/ppermute | solution.py:287
  79.3 2.2 %collective-permute-start.23 = (bf16[4,64,384]{2,1,0:T(8,128)(2,1)S(1)}, bf16[4,64,384]{2,1,0:T(8,128)(2,1)S(1)}, u32[]{:S(2)}, u32[]{:S(2)}) collective-permute-start(bf16[4,64,384]{2,1,0:T(8,128)(2,1)S(1)} %pad_maximum_fusion.4), channel_id=1, source_target_pairs={{0,4},{1,5},{2,6},{3,7},{4,0},{5,1},{6,2},{7,3},{8,12},{9,13},{10,... | collective-permute-start | bytes 589832 | tf_op jit(solution)/shard_map/ppermute | solution.py:287
  81.5 1.9 %collective-permute-start.37 = (f32[64,512]{1,0:T(8,128)S(1)}, f32[64,512]{1,0:T(8,128)S(1)}, u32[]{:S(2)}, u32[]{:S(2)}) collective-permute-start(f32[64,512]{1,0:T(8,128)S(1)} %get-tuple-element.24), channel_id=1, source_target_pairs={{0,1},{1,0},{2,3},{3,2},{4,5},{5,4},{6,7},{7,6},{8,9},{9,8},{10,11... | collective-permute-start | bytes 393224 | tf_op jit(solution)/shard_map/ppermute | solution.py:281
  83.4 0.6 collective-permute-done.33
  84.0 3.6 %collective-permute-start.35 = (bf16[8,64,512]{2,1,0:T(8,128)(2,1)S(1)}, bf16[8,64,512]{2,1,0:T(8,128)(2,1)S(1)}, u32[]{:S(2)}, u32[]{:S(2)}) collective-permute-start(bf16[8,64,512]{2,1,0:T(8,128)(2,1)S(1)} %pad_maximum_fusion.refs_2_), channel_id=1, source_target_pairs={{0,4},{1,5},{2,3},{3,2},{4,0},{5,1},{6,7},{7,6},{8,12},{9,13},{10,... | collective-permute-start | bytes 1572872 | tf_op jit(solution)/shard_map/ppermute | solution.py:297
  87.7 2.5 %collective-permute-start.25 = (bf16[8,64,384]{2,1,0:T(8,128)(2,1)S(1)}, bf16[8,64,384]{2,1,0:T(8,128)(2,1)S(1)}, u32[]{:S(2)}, u32[]{:S(2)}) collective-permute-start(bf16[8,64,384]{2,1,0:T(8,128)(2,1)S(1)} %pad_maximum_fusion.1.refs_0_), channel_id=1, source_target_pairs={{0,8},{1,9},{2,10},{3,11},{4,12},{5,13},{6,14},{7,15},{8,0},{9,1},... | collective-permute-start | bytes 1179656 | tf_op jit(solution)/shard_map/ppermute | solution.py:297
  90.3 1.1 %state.1 = (f32[896,128]{1,0:T(8,128)}, f32[896,128]{1,0:T(8,128)}) custom-call(f32[896,128]{1,0:T(8,128)S(1)} %copy-done.1, f32[896,128]{1,0:T(8,128)S(1)} %copy-done, f32[128,384]{1,0:T(8,128)S(1)} %pad_maximum_fusion.5.refs_0_, f32[128,512]{1,0:T(8,128)S(1)} %pad_maximum_fusion.3.refs_1_), custom_call_target="tpu_custom_call" | custom-call | tf_op jit(solution)/shard_map/state/pallas_call | solution.py:291
  91.5 3.3 %collective-permute-done.35.refs_3_ = bf16[8,64,512]{2,1,0:T(8,128)(2,1)S(1)} collective-permute-done((bf16[8,64,512]{2,1,0:T(8,128)(2,1)S(1)}, bf16[8,64,512]{2,1,0:T(8,128)(2,1)S(1)}, u32[]{:S(2)}, u32[]{:S(2)}) %collective-permute-start.35) | collective-permute-done | bytes 524320 | tf_op jit(solution)/shard_map/ppermute | solution.py:297
  94.8 0.5 collective-permute-start.24
  95.3 0.7 collective-permute-done.25.refs_1_
  96.2 2.2 %expand.2.refs_4_ = bf16[256,14336]{1,0:T(8,128)(2,1)} custom-call(bf16[256,128]{1,0:T(8,128)(2,1)S(1)} %maximum_select_fusion.p_ref, bf16[8,64,384]{2,1,0:T(8,128)(2,1)S(1)} %pad_maximum_fusion.1.refs_0_, bf16[8,64,384]{2,1,0:T(8,128)(2,1)S(1)} %collective-permute-done.25.refs_1_, bf16[8,64,512]{2,1,0:T(8,128)(2,1)S(1)} %pad_maximum_fusion.refs_2_, ...), custom_call_target="tpu_custom_call" | custom-call | tf_op jit(solution)/shard_map/expand/pallas_call | solution.py:309
  98.5 2.2 %expand.3 = bf16[256,14336]{1,0:T(8,128)(2,1)} custom-call(bf16[256,128]{1,0:T(8,128)(2,1)S(1)} %maximum_select_fusion.p_ref, bf16[8,64,384]{2,1,0:T(8,128)(2,1)S(1)} %collective-permute-done.24.refs_0_, bf16[8,64,384]{2,1,0:T(8,128)(2,1)S(1)} %collective-permute-done.26.refs_1_, ...), custom_call_target="tpu_custom_call", output_to_operand_aliasing={{}: (5, {})} | custom-call | tf_op jit(solution)/shard_map/expand/pallas_call | solution.py:309
  (70 shorter events, 4.6 us)
Async XLA Ops:
  0.6 27.2 %collective-permute-start.16 = (bf16[192,14336]{1,0:T(8,128)(2,1)}, bf16[192,14336]{1,0:T(8,128)(2,1)S(1)}, u32[]{:S(2)}, u32[]{:S(2)}) collective-permute-start(bf16[192,14336]{1,0:T(8,128)(2,1)} %g_hbm.3), channel_id=1, source_target_pairs={{0,2},{2,0},{4,6},{6,4},{8,10},{10,8},{12,14},{14,12},{16,18},{18,... | collective-permute-start | bytes 16515080 | tf_op jit(solution)/shard_map/ppermute | solution.py:209
  1.2 26.6 %collective-permute-start = (bf16[192,4096]{1,0:T(8,128)(2,1)}, bf16[192,4096]{1,0:T(8,128)(2,1)S(1)}, u32[]{:S(2)}, u32[]{:S(2)}) collective-permute-start(bf16[192,4096]{1,0:T(8,128)(2,1)} %a_hbm.1), channel_id=1, source_target_pairs={{0,2},{2,0},{4,6},{6,4},{8,10},{10,8},{12,14},{14,12},{16,18},{18,... | collective-permute-start | bytes 4718600 | tf_op jit(solution)/shard_map/ppermute | solution.py:208
  1.3 5.4 %collective-permute-start.2 = (bf16[256,128]{1,0:T(8,128)(2,1)}, bf16[256,128]{1,0:T(8,128)(2,1)S(1)}, u32[]{:S(2)}, u32[]{:S(2)}) collective-permute-start(bf16[256,128]{1,0:T(8,128)(2,1)} %own_hbm.1), channel_id=1, source_target_pairs={{0,4},{2,6},{4,0},{6,2},{8,12},{10,14},{12,8},{14,10},{16,20},{18,... | collective-permute-start | bytes 196616 | tf_op jit(solution)/shard_map/ppermute | solution.py:214
  4.2 8.2 %collective-permute-start.1 = (bf16[256,128]{1,0:T(8,128)(2,1)}, bf16[256,128]{1,0:T(8,128)(2,1)S(1)}, u32[]{:S(2)}, u32[]{:S(2)}) collective-permute-start(bf16[256,128]{1,0:T(8,128)(2,1)} %own_hbm.1), channel_id=1, source_target_pairs={{0,2},{2,0},{4,6},{6,4},{8,10},{10,8},{12,14},{14,12},{16,18},{18,... | collective-permute-start | bytes 196616 | tf_op jit(solution)/shard_map/ppermute | solution.py:212
  4.2 8.6 %collective-permute-start.4 = (bf16[256,128]{1,0:T(8,128)(2,1)}, bf16[256,128]{1,0:T(8,128)(2,1)S(1)}, u32[]{:S(2)}, u32[]{:S(2)}) collective-permute-start(bf16[256,128]{1,0:T(8,128)(2,1)} %own_hbm.1), channel_id=1, source_target_pairs={{0,8},{2,10},{4,12},{6,14},{8,0},{10,2},{12,4},{14,6},{16,24},{18,... | collective-permute-start | bytes 196616 | tf_op jit(solution)/shard_map/ppermute | solution.py:214
  6.7 8.7 %collective-permute-start.8 = (bf16[256,128]{1,0:T(8,128)(2,1)}, bf16[256,128]{1,0:T(8,128)(2,1)S(1)}, u32[]{:S(2)}, u32[]{:S(2)}) collective-permute-start(bf16[256,128]{1,0:T(8,128)(2,1)} %own_hbm.1), channel_id=1, source_target_pairs={{0,16},{2,18},{4,20},{6,22},{8,24},{10,26},{12,28},{14,30},{16,0},... | collective-permute-start | bytes 196616 | tf_op jit(solution)/shard_map/ppermute | solution.py:214
  12.4 3.1 %collective-permute-start.3 = (bf16[256,128]{1,0:T(8,128)(2,1)S(1)}, bf16[256,128]{1,0:T(8,128)(2,1)S(1)}, u32[]{:S(2)}, u32[]{:S(2)}) collective-permute-start(bf16[256,128]{1,0:T(8,128)(2,1)S(1)} %collective-permute-done.2.refs_1_), channel_id=1, source_target_pairs={{0,2},{2,0},{4,6},{6,4},{8,10},{10,8},{12,14},{14,12},{16,18},{18,... | collective-permute-start | bytes 196616 | tf_op jit(solution)/shard_map/ppermute | solution.py:215
  12.8 5.2 %collective-permute-start.6 = (bf16[256,128]{1,0:T(8,128)(2,1)S(1)}, bf16[256,128]{1,0:T(8,128)(2,1)S(1)}, u32[]{:S(2)}, u32[]{:S(2)}) collective-permute-start(bf16[256,128]{1,0:T(8,128)(2,1)S(1)} %collective-permute-done.4.refs_3_), channel_id=1, source_target_pairs={{0,4},{2,6},{4,0},{6,2},{8,12},{10,14},{12,8},{14,10},{16,20},{18,... | collective-permute-start | bytes 196616 | tf_op jit(solution)/shard_map/ppermute | solution.py:214
  15.4 4.4 %collective-permute-start.5 = (bf16[256,128]{1,0:T(8,128)(2,1)S(1)}, bf16[256,128]{1,0:T(8,128)(2,1)S(1)}, u32[]{:S(2)}, u32[]{:S(2)}) collective-permute-start(bf16[256,128]{1,0:T(8,128)(2,1)S(1)} %collective-permute-done.4.refs_3_), channel_id=1, source_target_pairs={{0,2},{2,0},{4,6},{6,4},{8,10},{10,8},{12,14},{14,12},{16,18},{18,... | collective-permute-start | bytes 196616 | tf_op jit(solution)/shard_map/ppermute | solution.py:215
  15.5 4.4 %collective-permute-start.12 = (bf16[256,128]{1,0:T(8,128)(2,1)S(1)}, bf16[256,128]{1,0:T(8,128)(2,1)S(1)}, u32[]{:S(2)}, u32[]{:S(2)}) collective-permute-start(bf16[256,128]{1,0:T(8,128)(2,1)S(1)} %collective-permute-done.8.refs_7_), channel_id=1, source_target_pairs={{0,8},{2,10},{4,12},{6,14},{8,0},{10,2},{12,4},{14,6},{16,24},{18,... | collective-permute-start | bytes 196616 | tf_op jit(solution)/shard_map/ppermute | solution.py:214
  18.0 4.3 %collective-permute-start.10 = (bf16[256,128]{1,0:T(8,128)(2,1)S(1)}, bf16[256,128]{1,0:T(8,128)(2,1)S(1)}, u32[]{:S(2)}, u32[]{:S(2)}) collective-permute-start(bf16[256,128]{1,0:T(8,128)(2,1)S(1)} %collective-permute-done.8.refs_7_), channel_id=1, source_target_pairs={{0,4},{2,6},{4,0},{6,2},{8,12},{10,14},{12,8},{14,10},{16,20},{18,... | collective-permute-start | bytes 196616 | tf_op jit(solution)/shard_map/ppermute | solution.py:214
  19.8 4.4 %collective-permute-start.9 = (bf16[256,128]{1,0:T(8,128)(2,1)S(1)}, bf16[256,128]{1,0:T(8,128)(2,1)S(1)}, u32[]{:S(2)}, u32[]{:S(2)}) collective-permute-start(bf16[256,128]{1,0:T(8,128)(2,1)S(1)} %collective-permute-done.8.refs_7_), channel_id=1, source_target_pairs={{0,2},{2,0},{4,6},{6,4},{8,10},{10,8},{12,14},{14,12},{16,18},{18,... | collective-permute-start | bytes 196616 | tf_op jit(solution)/shard_map/ppermute | solution.py:215
  19.9 4.2 %collective-permute-start.7 = (bf16[256,128]{1,0:T(8,128)(2,1)S(1)}, bf16[256,128]{1,0:T(8,128)(2,1)S(1)}, u32[]{:S(2)}, u32[]{:S(2)}) collective-permute-start(bf16[256,128]{1,0:T(8,128)(2,1)S(1)} %collective-permute-done.6.refs_5_), channel_id=1, source_target_pairs={{0,2},{2,0},{4,6},{6,4},{8,10},{10,8},{12,14},{14,12},{16,18},{18,... | collective-permute-start | bytes 196616 | tf_op jit(solution)/shard_map/ppermute | solution.py:215
  22.3 4.3 %collective-permute-start.14 = (bf16[256,128]{1,0:T(8,128)(2,1)S(1)}, bf16[256,128]{1,0:T(8,128)(2,1)S(1)}, u32[]{:S(2)}, u32[]{:S(2)}) collective-permute-start(bf16[256,128]{1,0:T(8,128)(2,1)S(1)} %collective-permute-done.10.refs_9_), channel_id=1, source_target_pairs={{0,8},{2,10},{4,12},{6,14},{8,0},{10,2},{12,4},{14,6},{16,24},{18,... | collective-permute-start | bytes 196616 | tf_op jit(solution)/shard_map/ppermute | solution.py:214
  24.1 2.4 %collective-permute-start.11 = (bf16[256,128]{1,0:T(8,128)(2,1)S(1)}, bf16[256,128]{1,0:T(8,128)(2,1)S(1)}, u32[]{:S(2)}, u32[]{:S(2)}) collective-permute-start(bf16[256,128]{1,0:T(8,128)(2,1)S(1)} %collective-permute-done.10.refs_9_), channel_id=1, source_target_pairs={{0,2},{2,0},{4,6},{6,4},{8,10},{10,8},{12,14},{14,12},{16,18},{18,... | collective-permute-start | bytes 196616 | tf_op jit(solution)/shard_map/ppermute | solution.py:215
  24.1 2.4 %collective-permute-start.13 = (bf16[256,128]{1,0:T(8,128)(2,1)S(1)}, bf16[256,128]{1,0:T(8,128)(2,1)S(1)}, u32[]{:S(2)}, u32[]{:S(2)}) collective-permute-start(bf16[256,128]{1,0:T(8,128)(2,1)S(1)} %collective-permute-done.12.refs_11_), channel_id=1, source_target_pairs={{0,2},{2,0},{4,6},{6,4},{8,10},{10,8},{12,14},{14,12},{16,18},{18,... | collective-permute-start | bytes 196616 | tf_op jit(solution)/shard_map/ppermute | solution.py:215
  26.6 1.3 %collective-permute-start.15 = (bf16[256,128]{1,0:T(8,128)(2,1)S(1)}, bf16[256,128]{1,0:T(8,128)(2,1)S(1)}, u32[]{:S(2)}, u32[]{:S(2)}) collective-permute-start(bf16[256,128]{1,0:T(8,128)(2,1)S(1)} %collective-permute-done.14.refs_13_), channel_id=1, source_target_pairs={{0,2},{2,0},{4,6},{6,4},{8,10},{10,8},{12,14},{14,12},{16,18},{18,... | collective-permute-start | bytes 196616 | tf_op jit(solution)/shard_map/ppermute | solution.py:215
  32.4 11.3 %collective-permute-start.17 = (bf16[8,64,384]{2,1,0:T(8,128)(2,1)S(1)}, bf16[8,64,384]{2,1,0:T(8,128)(2,1)S(1)}, u32[]{:S(2)}, u32[]{:S(2)}) collective-permute-start(bf16[8,64,384]{2,1,0:T(8,128)(2,1)S(1)} %get-tuple-element.14), channel_id=1, source_target_pairs={{0,8},{1,9},{2,10},{3,11},{4,12},{5,13},{6,14},{7,15},{8,0},{9,1},... | collective-permute-start | bytes 1179656 | tf_op jit(solution)/shard_map/ppermute | solution.py:267
  37.1 9.8 %collective-permute-start.27 = (bf16[8,64,512]{2,1,0:T(8,128)(2,1)S(1)}, bf16[8,64,512]{2,1,0:T(8,128)(2,1)S(1)}, u32[]{:S(2)}, u32[]{:S(2)}) collective-permute-start(bf16[8,64,512]{2,1,0:T(8,128)(2,1)S(1)} %get-tuple-element.17), channel_id=1, source_target_pairs={{0,4},{1,5},{2,3},{3,2},{4,0},{5,1},{6,7},{7,6},{8,12},{9,13},{10,... | collective-permute-start | bytes 1572872 | tf_op jit(solution)/shard_map/ppermute | solution.py:267
  43.7 11.6 %copy-start = (f32[896,128]{1,0:T(8,128)S(1)}, f32[896,128]{1,0:T(8,128)}, u32[]{:S(2)}) copy-start(f32[896,128]{1,0:T(8,128)} %second_ref.1) | copy-start | bytes 1376260
  43.7 11.6 %copy-start.1 = (f32[896,128]{1,0:T(8,128)S(1)}, f32[896,128]{1,0:T(8,128)}, u32[]{:S(2)}) copy-start(f32[896,128]{1,0:T(8,128)} %moment_ref.1) | copy-start | bytes 1376260
  43.8 7.8 %collective-permute-start.18 = (bf16[4,64,384]{2,1,0:T(8,128)(2,1)S(1)}, bf16[4,64,384]{2,1,0:T(8,128)(2,1)S(1)}, u32[]{:S(2)}, u32[]{:S(2)}) collective-permute-start(bf16[4,64,384]{2,1,0:T(8,128)(2,1)S(1)} %get-tuple-element.30), channel_id=1, source_target_pairs={{0,4},{1,5},{2,6},{3,7},{4,0},{5,1},{6,2},{7,3},{8,12},{9,13},{10,... | collective-permute-start | bytes 589832 | tf_op jit(solution)/shard_map/ppermute | solution.py:267
  47.3 6.4 %collective-permute-start.28 = (bf16[4,64,512]{2,1,0:T(8,128)(2,1)S(1)}, bf16[4,64,512]{2,1,0:T(8,128)(2,1)S(1)}, u32[]{:S(2)}, u32[]{:S(2)}) collective-permute-start(bf16[4,64,512]{2,1,0:T(8,128)(2,1)S(1)} %get-tuple-element.28), channel_id=1, source_target_pairs={{0,8},{1,9},{2,6},{3,7},{4,12},{5,13},{6,2},{7,3},{8,0},{9,1},{10,... | collective-permute-start | bytes 786440 | tf_op jit(solution)/shard_map/ppermute | solution.py:267
  51.8 4.7 %collective-permute-start.19 = (bf16[2,64,384]{2,1,0:T(8,128)(2,1)S(1)}, bf16[2,64,384]{2,1,0:T(8,128)(2,1)S(1)}, u32[]{:S(2)}, u32[]{:S(2)}) collective-permute-start(bf16[2,64,384]{2,1,0:T(8,128)(2,1)S(1)} %get-tuple-element.34), channel_id=1, source_target_pairs={{0,1},{1,0},{2,3},{3,2},{4,5},{5,4},{6,7},{7,6},{8,9},{9,8},{10,11... | collective-permute-start | bytes 294920 | tf_op jit(solution)/shard_map/ppermute | solution.py:267
  53.9 5.0 %collective-permute-start.29 = (bf16[2,64,512]{2,1,0:T(8,128)(2,1)S(1)}, bf16[2,64,512]{2,1,0:T(8,128)(2,1)S(1)}, u32[]{:S(2)}, u32[]{:S(2)}) collective-permute-start(bf16[2,64,512]{2,1,0:T(8,128)(2,1)S(1)} %get-tuple-element.32), channel_id=1, source_target_pairs={{0,1},{1,0},{2,10},{3,11},{4,5},{5,4},{6,14},{7,15},{8,9},{9,8},{1... | collective-permute-start | bytes 393224 | tf_op jit(solution)/shard_map/ppermute | solution.py:267
  55.7 40.4 %copy-start.2 = (bf16[256,128]{1,0:T(8,128)(2,1)S(1)}, bf16[256,128]{1,0:T(8,128)(2,1)}, u32[]{:S(2)}) copy-start(bf16[256,128]{1,0:T(8,128)(2,1)} %own_hbm.1) | copy-start | bytes 196612
  59.0 6.8 %collective-permute-start.30 = (bf16[1,64,512]{2,1,0:T(8,128)(2,1)S(1)}, bf16[1,64,512]{2,1,0:T(8,128)(2,1)S(1)}, u32[]{:S(2)}, u32[]{:S(2)}) collective-permute-start(bf16[1,64,512]{2,1,0:T(8,128)(2,1)S(1)} %fusion.9), channel_id=1, source_target_pairs={{0,16},{1,17},{2,18},{3,19},{4,20},{5,21},{6,22},{7,23},{8,24},{9,... | collective-permute-start | bytes 196616 | tf_op jit(solution)/shard_map/ppermute | solution.py:267
  61.6 6.5 %collective-permute-start.20 = (bf16[1,64,384]{2,1,0:T(8,128)(2,1)S(1)}, bf16[1,64,384]{2,1,0:T(8,128)(2,1)S(1)}, u32[]{:S(2)}, u32[]{:S(2)}) collective-permute-start(bf16[1,64,384]{2,1,0:T(8,128)(2,1)S(1)} %fusion.20), channel_id=1, source_target_pairs={{0,16},{1,17},{2,18},{3,19},{4,20},{5,21},{6,22},{7,23},{8,24},{9,... | collective-permute-start | bytes 147464 | tf_op jit(solution)/shard_map/ppermute | solution.py:267
  65.9 5.8 %collective-permute-start.31 = (bf16[1,64,512]{2,1,0:T(8,128)(2,1)S(1)}, bf16[1,64,512]{2,1,0:T(8,128)(2,1)S(1)}, u32[]{:S(2)}, u32[]{:S(2)}) collective-permute-start(bf16[1,64,512]{2,1,0:T(8,128)(2,1)S(1)} %get-tuple-element.23), channel_id=1, source_target_pairs={{0,16},{1,17},{2,18},{3,19},{4,20},{5,21},{6,22},{7,23},{8,24},{9,... | collective-permute-start | bytes 196616 | tf_op jit(solution)/shard_map/ppermute | solution.py:287
  68.2 5.6 %collective-permute-start.21 = (bf16[1,64,384]{2,1,0:T(8,128)(2,1)S(1)}, bf16[1,64,384]{2,1,0:T(8,128)(2,1)S(1)}, u32[]{:S(2)}, u32[]{:S(2)}) collective-permute-start(bf16[1,64,384]{2,1,0:T(8,128)(2,1)S(1)} %get-tuple-element.25), channel_id=1, source_target_pairs={{0,16},{1,17},{2,18},{3,19},{4,20},{5,21},{6,22},{7,23},{8,24},{9,... | collective-permute-start | bytes 147464 | tf_op jit(solution)/shard_map/ppermute | solution.py:287
  71.7 5.2 %collective-permute-start.32 = (bf16[2,64,512]{2,1,0:T(8,128)(2,1)S(1)}, bf16[2,64,512]{2,1,0:T(8,128)(2,1)S(1)}, u32[]{:S(2)}, u32[]{:S(2)}) collective-permute-start(bf16[2,64,512]{2,1,0:T(8,128)(2,1)S(1)} %pad_maximum_fusion.6), channel_id=1, source_target_pairs={{0,1},{1,0},{2,10},{3,11},{4,5},{5,4},{6,14},{7,15},{8,9},{9,8},{1... | collective-permute-start | bytes 393224 | tf_op jit(solution)/shard_map/ppermute | solution.py:287
  73.6 5.3 %collective-permute-start.36 = (f32[64,384]{1,0:T(8,128)S(1)}, f32[64,384]{1,0:T(8,128)S(1)}, u32[]{:S(2)}, u32[]{:S(2)}) collective-permute-start(f32[64,384]{1,0:T(8,128)S(1)} %get-tuple-element.26), channel_id=1, source_target_pairs={{0,1},{1,0},{2,3},{3,2},{4,5},{5,4},{6,7},{7,6},{8,9},{9,8},{10,11... | collective-permute-start | bytes 294920 | tf_op jit(solution)/shard_map/ppermute | solution.py:281
  73.8 5.5 %collective-permute-start.22 = (bf16[2,64,384]{2,1,0:T(8,128)(2,1)S(1)}, bf16[2,64,384]{2,1,0:T(8,128)(2,1)S(1)}, u32[]{:S(2)}, u32[]{:S(2)}) collective-permute-start(bf16[2,64,384]{2,1,0:T(8,128)(2,1)S(1)} %pad_maximum_fusion.7), channel_id=1, source_target_pairs={{0,1},{1,0},{2,3},{3,2},{4,5},{5,4},{6,7},{7,6},{8,9},{9,8},{10,11... | collective-permute-start | bytes 294920 | tf_op jit(solution)/shard_map/ppermute | solution.py:287
  76.9 7.1 %collective-permute-start.33 = (bf16[4,64,512]{2,1,0:T(8,128)(2,1)S(1)}, bf16[4,64,512]{2,1,0:T(8,128)(2,1)S(1)}, u32[]{:S(2)}, u32[]{:S(2)}) collective-permute-start(bf16[4,64,512]{2,1,0:T(8,128)(2,1)S(1)} %pad_maximum_fusion.2), channel_id=1, source_target_pairs={{0,8},{1,9},{2,6},{3,7},{4,12},{5,13},{6,2},{7,3},{8,0},{9,1},{10,... | collective-permute-start | bytes 786440 | tf_op jit(solution)/shard_map/ppermute | solution.py:287
  79.3 8.3 %collective-permute-start.23 = (bf16[4,64,384]{2,1,0:T(8,128)(2,1)S(1)}, bf16[4,64,384]{2,1,0:T(8,128)(2,1)S(1)}, u32[]{:S(2)}, u32[]{:S(2)}) collective-permute-start(bf16[4,64,384]{2,1,0:T(8,128)(2,1)S(1)} %pad_maximum_fusion.4), channel_id=1, source_target_pairs={{0,4},{1,5},{2,6},{3,7},{4,0},{5,1},{6,2},{7,3},{8,12},{9,13},{10,... | collective-permute-start | bytes 589832 | tf_op jit(solution)/shard_map/ppermute | solution.py:287
  81.5 8.8 %collective-permute-start.37 = (f32[64,512]{1,0:T(8,128)S(1)}, f32[64,512]{1,0:T(8,128)S(1)}, u32[]{:S(2)}, u32[]{:S(2)}) collective-permute-start(f32[64,512]{1,0:T(8,128)S(1)} %get-tuple-element.24), channel_id=1, source_target_pairs={{0,1},{1,0},{2,3},{3,2},{4,5},{5,4},{6,7},{7,6},{8,9},{9,8},{10,11... | collective-permute-start | bytes 393224 | tf_op jit(solution)/shard_map/ppermute | solution.py:281
  84.0 10.8 %collective-permute-start.35 = (bf16[8,64,512]{2,1,0:T(8,128)(2,1)S(1)}, bf16[8,64,512]{2,1,0:T(8,128)(2,1)S(1)}, u32[]{:S(2)}, u32[]{:S(2)}) collective-permute-start(bf16[8,64,512]{2,1,0:T(8,128)(2,1)S(1)} %pad_maximum_fusion.refs_2_), channel_id=1, source_target_pairs={{0,4},{1,5},{2,3},{3,2},{4,0},{5,1},{6,7},{7,6},{8,12},{9,13},{10,... | collective-permute-start | bytes 1572872 | tf_op jit(solution)/shard_map/ppermute | solution.py:297
  87.7 8.3 %collective-permute-start.25 = (bf16[8,64,384]{2,1,0:T(8,128)(2,1)S(1)}, bf16[8,64,384]{2,1,0:T(8,128)(2,1)S(1)}, u32[]{:S(2)}, u32[]{:S(2)}) collective-permute-start(bf16[8,64,384]{2,1,0:T(8,128)(2,1)S(1)} %pad_maximum_fusion.1.refs_0_), channel_id=1, source_target_pairs={{0,8},{1,9},{2,10},{3,11},{4,12},{5,13},{6,14},{7,15},{8,0},{9,1},... | collective-permute-start | bytes 1179656 | tf_op jit(solution)/shard_map/ppermute | solution.py:297
  91.5 7.0 %collective-permute-start.34 = (bf16[8,64,512]{2,1,0:T(8,128)(2,1)S(1)}, bf16[8,64,512]{2,1,0:T(8,128)(2,1)S(1)}, u32[]{:S(2)}, u32[]{:S(2)}) collective-permute-start(bf16[8,64,512]{2,1,0:T(8,128)(2,1)S(1)} %pad_maximum_fusion.refs_2_), channel_id=1, source_target_pairs={{0,2},{2,0},{4,6},{6,4},{8,10},{10,8},{12,14},{14,12},{16,18},{18,... | collective-permute-start | bytes 1572872 | tf_op jit(solution)/shard_map/ppermute | solution.py:301
  94.8 3.7 %collective-permute-start.38 = (bf16[8,64,512]{2,1,0:T(8,128)(2,1)S(1)}, bf16[8,64,512]{2,1,0:T(8,128)(2,1)S(1)}, u32[]{:S(2)}, u32[]{:S(2)}) collective-permute-start(bf16[8,64,512]{2,1,0:T(8,128)(2,1)S(1)} %collective-permute-done.35.refs_3_), channel_id=1, source_target_pairs={{0,2},{2,0},{4,6},{6,4},{8,10},{10,8},{12,14},{14,12},{16,18},{18,... | collective-permute-start | bytes 1572872 | tf_op jit(solution)/shard_map/ppermute | solution.py:301
  94.8 3.6 %collective-permute-start.24 = (bf16[8,64,384]{2,1,0:T(8,128)(2,1)S(1)}, bf16[8,64,384]{2,1,0:T(8,128)(2,1)S(1)}, u32[]{:S(2)}, u32[]{:S(2)}) collective-permute-start(bf16[8,64,384]{2,1,0:T(8,128)(2,1)S(1)} %pad_maximum_fusion.1.refs_0_), channel_id=1, source_target_pairs={{0,2},{2,0},{4,6},{6,4},{8,10},{10,8},{12,14},{14,12},{16,18},{18,... | collective-permute-start | bytes 1179656 | tf_op jit(solution)/shard_map/ppermute | solution.py:301
  96.1 2.4 %collective-permute-start.26 = (bf16[8,64,384]{2,1,0:T(8,128)(2,1)S(1)}, bf16[8,64,384]{2,1,0:T(8,128)(2,1)S(1)}, u32[]{:S(2)}, u32[]{:S(2)}) collective-permute-start(bf16[8,64,384]{2,1,0:T(8,128)(2,1)S(1)} %collective-permute-done.25.refs_1_), channel_id=1, source_target_pairs={{0,2},{2,0},{4,6},{6,4},{8,10},{10,8},{12,14},{14,12},{16,18},{18,... | collective-permute-start | bytes 1179656 | tf_op jit(solution)/shard_map/ppermute | solution.py:301
